TPU v7x, 128 devices: a whole 4x4x4 slice. The times are simulated.
128 devices in a mesh: row: 16 (over x, y_lo, core), col: 8 (over z, y_hi).
Axes of the slice: x: 4, y: 4 (y_hi: 2, y_lo: 2; y = y_hi * 2 + y_lo), z: 4, core: 2. Of those that a mesh axis runs over, the one named last changes fastest.
Arguments:
- basis_values: bfloat16 [16, 8, 16, 128, 1024], P('row', 'col'), may hold values from -2 to 2
- potential: float32 [16, 8, 1024], P('row', 'col'), may hold values from -4 to 4
- task_pairs: int32 [16, 8, 128, 2], P('row', 'col'), may hold values from 0 to 15
- task_owner: int32 [16, 8, 128, 1], P('row', 'col'), may hold values from 0 to 127; in each aligned block of 128 rows (0 to 127, 128 to 255, ..., all dimensions but the last counted through in order) at most 2 rows name the same one
- task_slot: int32 [16, 8, 128], P('row', 'col'), may hold values from 0 to 31
- matrix_blocks: bfloat16 [16, 16, 16, 128, 128], P('row', 'col'), may hold values from -4 to 4
- matrix_columns: int32 [16, 16, 16], P('row', 'col'), may hold values from 0 to 15
Outputs:
- fock_blocks: bfloat16 [16, 16, 16, 128, 128], P('row', 'col')
- square_blocks: bfloat16 [16, 16, 16, 128, 128], P('row', 'col')
Inputs may be any that keep to these rules, and one draw needn't show every extreme that they name: `task_owner`: among the 128 tasks of one device no owner is named more than 2 times, a bound that some block reaches.
All inputs are finite; a program needn't handle non-finite values.
Results may differ from a plain program's by a relative error of at most 0.0057.
Values may be sent and summed in bfloat16 or wider, within the bound.
No kernel may reach another device: no remote copies, remote signals or barrier semaphores. Data moves between devices by JAX's collectives and lax.ppermute only.
A program may use at most 192 MiB of HBM per device.

v0:
```python
import jax
import jax.numpy as jnp
from jax import lax
from jax.sharding import Mesh
from jax.sharding import PartitionSpec as P

COL = ("col_0", "col_1")
ROW_COL = ("row", "col_0", "col_1")


def gathered_by_axis(shard, axes, dim):
    if not axes:
        return shard
    nearer = lax.all_gather(shard, axes[-1], axis=dim, tiled=True)
    return gathered_by_axis(nearer, axes[:-1], dim)


def task_products(basis_local, potential_local, pairs_local):
    weighted = (basis_local.astype(jnp.float32) * potential_local[None, None, :]).astype(
        jnp.bfloat16
    )
    local_count = basis_local.shape[0]
    block_width = basis_local.shape[1]
    point_count = basis_local.shape[2]
    weighted_flat = weighted.reshape((local_count, block_width * point_count))
    basis_flat = basis_local.reshape((local_count, block_width * point_count))
    task_count = pairs_local.shape[0]
    group_size = min(task_count, 16)
    grouped = pairs_local.reshape((task_count // group_size, group_size, 2))
    local_range = jnp.arange(local_count, dtype=jnp.int32)

    def one_group(pair_group):
        left_hits = (pair_group[:, 0:1] == local_range[None, :]).astype(jnp.bfloat16)
        right_hits = (pair_group[:, 1:2] == local_range[None, :]).astype(jnp.bfloat16)
        left_rows = jnp.dot(left_hits, weighted_flat, preferred_element_type=jnp.float32).astype(
            jnp.bfloat16
        )
        right_rows = jnp.dot(right_hits, basis_flat, preferred_element_type=jnp.float32).astype(
            jnp.bfloat16
        )
        left_rows = left_rows.reshape((group_size, block_width, point_count))
        right_rows = right_rows.reshape((group_size, block_width, point_count))
        products = jnp.einsum(
            "tap,tbp->tab", left_rows, right_rows, preferred_element_type=jnp.float32
        )
        return products.astype(jnp.bfloat16)

    blocks = lax.map(one_group, grouped)
    return blocks.reshape((task_count,) + blocks.shape[2:])


def filtered_product(left_values, left_columns, right_values, right_columns, target_columns):
    cell_rows = left_columns.shape[-1]
    block_width = right_values.shape[-1]
    ordered_columns = jnp.swapaxes(right_columns, 0, 1)
    pick_form = "hnqp,nhpx->hnqx"
    slot_range = jnp.arange(cell_rows, dtype=jnp.int32)
    chosen = (left_columns[..., None] == slot_range) & (
        ordered_columns[:, :, None, :] == target_columns[:, None, :, None]
    )
    hits = chosen.astype(right_values.dtype)
    right_flat = right_values.reshape(right_values.shape[:3] + (block_width * block_width,))
    picked = jnp.einsum(pick_form, hits, right_flat, preferred_element_type=jnp.float32).astype(
        right_values.dtype
    )
    picked = picked.reshape(picked.shape[:3] + (block_width, block_width))
    return jnp.einsum("hnqab,hnqbc->hqac", left_values, picked, preferred_element_type=jnp.float32)


def body(basis_values, potential, task_pairs, task_owner, task_slot, matrix_blocks, matrix_columns):
    blocks = task_products(basis_values[0, 0], potential[0, 0], task_pairs[0, 0])
    owners = task_owner[0, 0, :, 0]
    slot_index = task_slot[0, 0]
    row_count = lax.axis_size("row")
    column_count = lax.axis_size(COL)
    device_count = row_count * column_count
    task_count = owners.shape[0]
    capacity = max(2, 2 * task_count // device_count)
    cell_rows = matrix_blocks.shape[2]
    block_width = matrix_blocks.shape[3]
    owner_hits = (owners[:, None] == jnp.arange(device_count, dtype=jnp.int32)[None, :]).astype(
        jnp.int32
    )
    bucket_rank = jnp.sum(jnp.cumsum(owner_hits, axis=0) * owner_hits, axis=1) - 1
    bucket_place = owners * capacity + bucket_rank
    place_hits = (
        jnp.arange(device_count * capacity, dtype=jnp.int32)[:, None] == bucket_place[None, :]
    ).astype(jnp.bfloat16)
    send_flat = jnp.dot(
        place_hits,
        blocks.reshape((task_count, block_width * block_width)),
        preferred_element_type=jnp.float32,
    )
    send_values = send_flat.astype(jnp.bfloat16).reshape(
        (device_count * capacity, block_width, block_width)
    )
    send_slots = (
        jnp.full((device_count * capacity,), -1, jnp.int32).at[bucket_place].set(slot_index)
    )
    arrived_values, arrived_slots = (
        lax.all_to_all(send_values, ROW_COL, split_axis=0, concat_axis=0, tiled=True),
        lax.all_to_all(send_slots, ROW_COL, split_axis=0, concat_axis=0, tiled=True),
    )
    slot_hits = (
        arrived_slots[None, :] == jnp.arange(2 * cell_rows, dtype=jnp.int32)[:, None]
    ).astype(jnp.bfloat16)
    fock_sum = jnp.dot(
        slot_hits,
        arrived_values.reshape((device_count * capacity, block_width * block_width)),
        preferred_element_type=jnp.float32,
    )
    fock_blocks = fock_sum.astype(jnp.bfloat16).reshape((1, 2, cell_rows, block_width, block_width))
    own_values = matrix_blocks[0]
    own_columns = matrix_columns[0]
    panel_values, panel_columns = (
        gathered_by_axis(own_values, COL, 0),
        gathered_by_axis(own_columns, COL, 0),
    )
    piece_values = lax.all_gather(own_values[None], "row", axis=0, tiled=True)
    piece_columns = lax.all_gather(own_columns[None], "row", axis=0, tiled=True)
    left_values = panel_values
    left_columns = panel_columns
    left_values = jnp.broadcast_to(left_values[None], (2,) + left_values.shape)
    left_columns = jnp.broadcast_to(left_columns[None], (2,) + left_columns.shape)
    product_sum = filtered_product(
        left_values, left_columns, piece_values, piece_columns, own_columns
    )
    square_blocks = product_sum.astype(jnp.bfloat16).reshape(
        (1, 2, cell_rows, block_width, block_width)
    )
    return (fock_blocks, square_blocks)


def solution(mesh):
    finer = Mesh(mesh.devices.reshape(mesh.shape["row"], 4, 2), ("row", "col_0", "col_1"))
    return jax.shard_map(
        body,
        mesh=finer,
        in_specs=(
            P("row", COL, None, None, None),
            P("row", COL, None),
            P("row", COL, None, None),
            P("row", COL, None, None),
            P("row", COL, None),
            P("row", COL, None, None, None),
            P("row", COL, None),
        ),
        out_specs=(P("row", COL, None, None, None), P("row", COL, None, None, None)),
        check_vma=False,
    )
```

profile of v0, /device:TPU:1, one launch (start us, length us, event | category | flops | bytes accessed | tf_op | source)
XLA Modules:
  0.0 382.2 jit_solution(3847121922971806656)
XLA Ops:
  8.0 0.7 all-gather.8.cloned.1.call-update
  8.7 0.7 fusion.34
  9.6 0.8 select_reduce_fusion
  11.1 1.1 scatter_custom_fusion
  12.2 0.8 all_to_all.9
  13.0 11.5 %all-to-all-start = ((s32[128,2,1]{1,2,0:T(1,128)}), s32[128,2,1]{1,2,0:T(1,128)S(1)}, u32[]{:S(2)}, u32[]{:S(2)}) async-start(s32[128,2,1]{1,2,0:T(1,128)} %bitcast.5), calls=%async_computation | async-start | bytes 131072 | tf_op jit(solution)/shard_map/all_to_all | solution.py:102
  24.5 6.7 %copy.36 = bf16[2,8,128,1024]{3,1,2,0:T(8,128)(2,1)} copy(bf16[2,8,128,1024]{3,2,1,0:T(8,128)(2,1)} %bitcast.117) | data formatting | bytes 8388608
  31.5 4.9 %multiply_convert_fusion = bf16[16,131072]{1,0:T(8,128)(2,1)} fusion(bf16[16,131072]{1,0:T(8,128)(2,1)} %bitcast.110, f32[131072]{0:T(1024)S(1)} %bitcast.119), kind=kLoop, calls=%fused_computation.23 | loop fusion | flops 6291456 | bytes 8912896 | tf_op jit(solution)/shard_map/convert_element_type | solution.py:19
  36.4 14.5 %all-gather.10.cloned.1.call-done = bf16[1,4,16,128,128]{4,3,2,0,1:T(8,128)(2,1)} async-done(((bf16[1,2,16,128,128]{4,3,2,0,1:T(8,128)(2,1)}), bf16[1,4,16,128,128]{4,3,2,0,1:T(8,128)(2,1)}) %all-gather.10.cloned.1.call-update) | async-done | bytes 2097168 | tf_op jit(solution)/shard_map/all_gather | solution.py:14
  50.9 94.1 %while.12 = (s32[]{:T(128)}, bf16[8,16,128,128]{3,2,1,0:T(8,128)(2,1)}, s32[8,16,2]{1,0,2:T(8,128)S(1)}, bf16[16,131072]{1,0:T(8,128)(2,1)}, bf16[16,131072]{1,0:T(8,128)(2,1)}, /*index=5*/s32[]{:T(128)}) while((s32[]{:T(128)}, bf16[8,16,128,128]{3,2,1,0:T(8,128)(2,1)}, s32[8,16,2]{1,0,2:T(8,128)S(1)}, ...), condition=%wide.region_4.5_spmd.clone.clone, body=%wide.region_3.4_spmd.clone.clone.sunk | while | flops 675545600 | bytes 59245796 | solution.py:48
  50.9 3.6 convolution_convert_fusion.8
  54.5 2.3 copy.66
  56.9 1.3 convolution_convert_fusion.9
  58.2 2.3 copy.67
  60.5 2.1 fusion.54
  62.6 3.6 convolution_convert_fusion.8
  66.3 2.3 copy.66
  68.6 1.3 convolution_convert_fusion.9
  69.9 2.3 copy.67
  72.2 2.1 fusion.54
  74.4 3.8 convolution_convert_fusion.8
  78.2 2.3 copy.66
  80.5 1.3 convolution_convert_fusion.9
  81.8 2.3 copy.67
  84.1 2.1 fusion.54
  86.2 3.7 convolution_convert_fusion.8
  89.9 2.3 copy.66
  92.2 1.3 convolution_convert_fusion.9
  93.5 2.3 copy.67
  95.9 2.1 fusion.54
  98.0 3.7 convolution_convert_fusion.8
  101.6 2.3 copy.66
  104.0 1.3 convolution_convert_fusion.9
  105.3 2.3 copy.67
  107.6 2.1 fusion.54
  109.7 3.6 convolution_convert_fusion.8
  113.3 2.3 copy.66
  115.7 1.3 convolution_convert_fusion.9
  117.0 2.3 copy.67
  119.3 2.1 fusion.54
  121.4 3.7 convolution_convert_fusion.8
  125.1 2.3 copy.66
  127.5 1.3 convolution_convert_fusion.9
  128.8 2.3 copy.67
  131.1 2.0 fusion.54
  133.2 3.7 convolution_convert_fusion.8
  136.9 2.3 copy.66
  139.2 1.3 convolution_convert_fusion.9
  140.5 2.3 copy.67
  142.8 2.1 fusion.54
  144.9 8.9 %fusion.12 = bf16[32,8,128,128]{3,1,2,0:T(8,128)(2,1)} fusion(bf16[16,8,128,128]{3,2,1,0:T(8,128)(2,1)} %bitcast.35, s32[128]{0:T(128)S(1)} %multiply_add_fusion), kind=kOutput, calls=%fused_computation.24 | convolution fusion | flops 1077968896 | bytes 12583424 | tf_op jit(solution)/shard_map/dot_general | solution.py:89
  153.8 10.3 %copy.39 = bf16[32,8,128,128]{3,2,1,0:T(8,128)(2,1)} copy(bf16[32,8,128,128]{3,1,2,0:T(8,128)(2,1)} %fusion.12) | data formatting | bytes 16777216
  164.1 7.9 %all-to-all-start.1 = ((bf16[256,128,128]{2,1,0:T(8,128)(2,1)}), bf16[256,128,128]{2,1,0:T(8,128)(2,1)}, u32[]{:S(2)}, u32[]{:S(2)}) async-start(bf16[256,128,128]{2,1,0:T(8,128)(2,1)} %bitcast.115), calls=%async_computation.1 | async-start | bytes 16777216 | tf_op jit(solution)/shard_map/all_to_all | solution.py:101
  172.0 112.8 %all_gather.20 = s32[16,2,16]{2,1,0:T(2,128)S(1)} all-gather(s32[1,2,16]{2,1,0:T(2,128)S(1)} %copy-done.3), channel_id=1, replica_groups=mesh['row'=16,'col_0'=4,'col_1'=2] {'row'}, dimensions={0}, use_global_device_ids=true | all-gather | bytes 2176 | tf_op jit(solution)/shard_map/all_gather | solution.py:120
  284.8 4.6 %all-gather = s32[1,4,16]{2,0,1:T(1,128)S(1)} all-gather(s32[1,2,16]{2,0,1:T(1,128)S(1)} %bitcast.124), channel_id=2, replica_groups=mesh['row'=16,'col_0'=4,'col_1'=2] {'col_1'}, dimensions={1}, use_global_device_ids=true | all-gather | bytes 384 | tf_op jit(solution)/shard_map/all_gather | solution.py:14
  289.4 11.1 %all-gather.1 = s32[1,16,16]{2,0,1:T(1,128)S(1)} all-gather(s32[1,4,16]{2,0,1:T(1,128)S(1)} %all-gather), channel_id=3, replica_groups=mesh['row'=16,'col_0'=4,'col_1'=2] {'col_0'}, dimensions={1}, use_global_device_ids=true | all-gather | bytes 1280 | tf_op jit(solution)/shard_map/all_gather | solution.py:14
  301.0 0.8 reduce.3
  302.0 8.2 %fusion.24 = bf16[4,8,128,128]{3,1,2,0:T(8,128)(2,1)S(1)} fusion(bf16[32,8,128,128]{3,2,1,0:T(8,128)(2,1)} %bitcast.39, s32[256]{0:T(256)S(1)} %eq.98), kind=kOutput, calls=%fused_computation.29 | convolution fusion | flops 268967936 | bytes 9438208 | tf_op jit(solution)/shard_map/dot_general | solution.py:107
  310.2 1.2 copy.41
  311.4 25.3 %reshape.105 = bf16[16,2,16,16384]{3,2,1,0:T(8,128)(2,1)} reshape(bf16[16,2,16,128,128]{4,3,2,1,0:T(8,128)(2,1)} %all-gather.8.cloned.1.call-done) | data formatting | bytes 33554432 | tf_op jit(solution)/shard_map/reshape | solution.py:62
  336.7 11.4 %convolution_convert_fusion.3 = bf16[2,16,16,16384]{3,2,1,0:T(8,128)(2,1)} fusion(bf16[16,2,16,16384]{3,2,1,0:T(8,128)(2,1)} %reshape.105, s32[2,16]{1,0:T(2,128)S(1)} %bitcast.125, s32[2,16,16]{2,1,0:T(8,128)S(1)} %copy.23, s32[16,16]{1,0:T(8,128)S(1)} %bitcast.121), kind=kOutput, calls=%fused_computation.14 | convolution fusion | flops 276848640 | bytes 33557632 | tf_op jit(solution)/shard_map/hnqp,nhpx->hnqx/dot_general | solution.py:63
  348.2 15.2 %copy.42 = bf16[64,8,128,128]{3,2,1,0:T(8,128)(2,1)} copy(bf16[64,8,128,128]{3,1,2,0:T(8,128)(2,1)} %bitcast.114) | data formatting | bytes 33554432
  363.4 11.0 %fusion.19 = bf16[1,2,16,128,128]{3,4,2,1,0:T(8,128)(2,1)S(1)} fusion(bf16[2,16,16,128,128]{4,3,2,1,0:T(8,128)(2,1)} %bitcast.116, bf16[1,16,16,128,128]{4,3,2,0,1:T(8,128)(2,1)} %all-gather.12.cloned.1.call-done), kind=kOutput, calls=%fused_computation.28 | convolution fusion | flops 2148007936 | bytes 26214400 | tf_op jit(solution)/shard_map/hnqab,hnqbc->hqac/dot_general | solution.py:67
  374.3 1.3 copy.28
  (61 shorter events, 2.7 us)
Async XLA Ops:
  7.2 24.1 %copy-start = (f32[1,1,1024]{2,1,0:T(1,128)S(1)}, f32[1,1,1024]{2,1,0:T(1,128)}, u32[]{:S(2)}) copy-start(f32[1,1,1024]{2,1,0:T(1,128)} %param.10) | copy-start | bytes 12292
  7.2 24.2 %copy-start.5 = (s32[1,1,128,2]{2,3,1,0:T(2,128)S(1)}, s32[1,1,128,2]{2,3,1,0:T(2,128)}, u32[]{:S(2)}) copy-start(s32[1,1,128,2]{2,3,1,0:T(2,128)} %param.11) | copy-start | bytes 3076
  7.2 43.6 %all-gather.10.cloned.1.call-start = ((), (), s32[]{:S(2)}) async-start(), calls=%async_computation.3 | async-start | bytes 3145728 | tf_op jit(solution)/shard_map/all_gather | solution.py:14
  7.9 303.5 %all-gather.8.cloned.1.call-start = ((), (), s32[]{:S(2)}) async-start(), calls=%async_computation.2 | async-start | bytes 17825792 | tf_op jit(solution)/shard_map/all_gather | solution.py:119
  13.0 151.1 %all-to-all-start = ((s32[128,2,1]{1,2,0:T(1,128)}), s32[128,2,1]{1,2,0:T(1,128)S(1)}, u32[]{:S(2)}, u32[]{:S(2)}) async-start(s32[128,2,1]{1,2,0:T(1,128)} %bitcast.5), calls=%async_computation | async-start | bytes 131072 | tf_op jit(solution)/shard_map/all_to_all | solution.py:102
  24.5 338.9 %all-gather.12.cloned.1.call-start = ((), (), s32[]{:S(2)}) async-start(), calls=%async_computation.4 | async-start | bytes 10485760 | tf_op jit(solution)/shard_map/all_gather | solution.py:14
  50.8 94.1 %copy-start.4 = (s32[1,1,128,1]{2,3,1,0:T(1,128)S(1)}, s32[1,1,128,1]{2,3,1,0:T(1,128)}, u32[]{:S(2)}) copy-start(s32[1,1,128,1]{2,3,1,0:T(1,128)} %param.12) | copy-start | bytes 1540
  50.9 6.0 %copy-start.2 = (bf16[16,131072]{1,0:T(8,128)(2,1)S(1)}, bf16[16,131072]{1,0:T(8,128)(2,1)}, u32[]{:S(2)}) copy-start(bf16[16,131072]{1,0:T(8,128)(2,1)} %get-tuple-element.145) | copy-start | bytes 12582916 | tf_op jit(solution)/shard_map/while
  62.6 6.0 %copy-start.2 = (bf16[16,131072]{1,0:T(8,128)(2,1)S(1)}, bf16[16,131072]{1,0:T(8,128)(2,1)}, u32[]{:S(2)}) copy-start(bf16[16,131072]{1,0:T(8,128)(2,1)} %get-tuple-element.145) | copy-start | bytes 12582916 | tf_op jit(solution)/shard_map/while
  74.4 6.1 %copy-start.2 = (bf16[16,131072]{1,0:T(8,128)(2,1)S(1)}, bf16[16,131072]{1,0:T(8,128)(2,1)}, u32[]{:S(2)}) copy-start(bf16[16,131072]{1,0:T(8,128)(2,1)} %get-tuple-element.145) | copy-start | bytes 12582916 | tf_op jit(solution)/shard_map/while
  86.2 6.0 %copy-start.2 = (bf16[16,131072]{1,0:T(8,128)(2,1)S(1)}, bf16[16,131072]{1,0:T(8,128)(2,1)}, u32[]{:S(2)}) copy-start(bf16[16,131072]{1,0:T(8,128)(2,1)} %get-tuple-element.145) | copy-start | bytes 12582916 | tf_op jit(solution)/shard_map/while
  97.9 6.0 %copy-start.2 = (bf16[16,131072]{1,0:T(8,128)(2,1)S(1)}, bf16[16,131072]{1,0:T(8,128)(2,1)}, u32[]{:S(2)}) copy-start(bf16[16,131072]{1,0:T(8,128)(2,1)} %get-tuple-element.145) | copy-start | bytes 12582916 | tf_op jit(solution)/shard_map/while
  109.7 6.0 %copy-start.2 = (bf16[16,131072]{1,0:T(8,128)(2,1)S(1)}, bf16[16,131072]{1,0:T(8,128)(2,1)}, u32[]{:S(2)}) copy-start(bf16[16,131072]{1,0:T(8,128)(2,1)} %get-tuple-element.145) | copy-start | bytes 12582916 | tf_op jit(solution)/shard_map/while
  121.4 6.1 %copy-start.2 = (bf16[16,131072]{1,0:T(8,128)(2,1)S(1)}, bf16[16,131072]{1,0:T(8,128)(2,1)}, u32[]{:S(2)}) copy-start(bf16[16,131072]{1,0:T(8,128)(2,1)} %get-tuple-element.145) | copy-start | bytes 12582916 | tf_op jit(solution)/shard_map/while
  133.1 6.1 %copy-start.2 = (bf16[16,131072]{1,0:T(8,128)(2,1)S(1)}, bf16[16,131072]{1,0:T(8,128)(2,1)}, u32[]{:S(2)}) copy-start(bf16[16,131072]{1,0:T(8,128)(2,1)} %get-tuple-element.145) | copy-start | bytes 12582916 | tf_op jit(solution)/shard_map/while
  164.1 7.9 %copy-start.3 = (s32[1,2,16]{2,1,0:T(2,128)S(1)}, s32[1,2,16]{2,1,0:T(2,128)}, u32[]{:S(2)}) copy-start(s32[1,2,16]{2,1,0:T(2,128)} %param.15) | copy-start | bytes 388
  164.1 137.9 %all-to-all-start.1 = ((bf16[256,128,128]{2,1,0:T(8,128)(2,1)}), bf16[256,128,128]{2,1,0:T(8,128)(2,1)}, u32[]{:S(2)}, u32[]{:S(2)}) async-start(bf16[256,128,128]{2,1,0:T(8,128)(2,1)} %bitcast.115), calls=%async_computation.1 | async-start | bytes 16777216 | tf_op jit(solution)/shard_map/all_to_all | solution.py:101
  363.4 12.3 %copy-start.1 = (f32[1,1,1024]{2,1,0:T(1,128)S(1)}, f32[1,1,1024]{2,1,0:T(1,128)}, u32[]{:S(2)}) copy-start(f32[1,1,1024]{2,1,0:T(1,128)} %param.10) | copy-start | bytes 12292
Sparse Core Ops, SparseCore 0:
  9.7 41.0 all-gather.9
  52.5 91.3 all-gather.7
  145.6 177.8 all-gather.11
where the time goes:
time: 385 us; the launch traced here: 382 us
  blocking collectives  129 us (34%)
  local copies, waits for them, and re-layouts  100 us (26%)
  matrix products  95.9 us (25%)
  starting transfers between devices  19.5 us (5%)
  waiting for transfers between devices  15.9 us (4%)
  between operations  13.9 us (4%)
  other arithmetic  8.12 us (2%)
    all_gather x1, blocking collectives, body(): piece_columns = lax.all_gather(own_columns[None], 'row', axis=0, tiled=True)  113 us
    while x32, local copies, waits for them, and re-layouts  37.3 us
    unnamed x17, local copies, waits for them, and re-layouts  34.8 us
    dot_general x8, matrix products, one_group(): jnp.dot(left_hits, weighted_flat, preferred_element_type=jnp.float32)  29.5 us
    reshape x1, local copies, waits for them, and re-layouts, filtered_product(): right_values.reshape(right_values.shape[:3] + (block_width * block_width,))  25.3 us
    dot_general x8, matrix products, one_group(): jnp.einsum('tap,tbp->tab', left_rows, right_rows, preferred_element_type=...  16.6 us
    all_gather x2, blocking collectives, gathered_by_axis(): nearer = lax.all_gather(shard, axes[-1], axis=dim, tiled=True)  15.7 us
    all_gather x2, waiting for transfers between devices, gathered_by_axis(): nearer = lax.all_gather(shard, axes[-1], axis=dim, tiled=True)  14.5 us
  transfers between devices with their start and end apart: 5, of which 1 were waited for; matrix products, arithmetic and copies ran while one was open for 50% of the time, Pallas kernels for 0%

commit v1 on v0

v1 whole, which is shorter than its diff:
```python
import functools

import jax
import jax.numpy as jnp
from jax import lax
from jax.experimental import pallas as pl
from jax.experimental.pallas import tpu as pltpu
from jax.sharding import Mesh
from jax.sharding import PartitionSpec as P

ROW = ("x", "yl", "c")
COL = ("z", "yh")
ALL = ROW + COL
F32 = jnp.float32
BF16 = jnp.bfloat16


def shift(value, axis, step):
    size = lax.axis_size(axis)
    return lax.ppermute(value, axis, [(i, (i + step) % size) for i in range(size)])


def pair_kernel(pairs, places, basis, potential, send, weighted, table, sem):
    local_count, width, points = basis.shape
    task_count = places.shape[0]
    for a in range(local_count):
        weighted[a] = (basis[a].astype(F32) * potential[...]).astype(BF16)

    def columns(step, carry):
        left = weighted[...].reshape(local_count * width, points)
        right = basis[pl.ds(2 * step, 2)].reshape(2 * width, points)
        product = lax.dot_general(left, right, (((1,), (1,)), ((), ())), preferred_element_type=F32)
        product = product.astype(BF16).reshape(local_count, width, 2 * width)
        table[2 * step] = product[:, :, :width]
        table[2 * step + 1] = product[:, :, width:]
        return carry

    lax.fori_loop(0, local_count // 2, columns, 0)

    def start(t, carry):
        block = table.at[pairs[2 * t + 1], pairs[2 * t]]
        pltpu.make_async_copy(block, send.at[places[t]], sem).start()
        return carry

    lax.fori_loop(0, task_count, start, 0)
    whole = send.at[pl.ds(0, task_count)]
    pltpu.make_async_copy(whole, whole, sem).wait()


def pair_blocks(basis, potential, pairs, places, slot_count):
    local_count, width, points = basis.shape
    task_count = places.shape[0]
    smem = pl.BlockSpec(memory_space=pltpu.SMEM)
    vmem = pl.BlockSpec(memory_space=pltpu.VMEM)
    return pl.pallas_call(
        pair_kernel,
        out_shape=jax.ShapeDtypeStruct((slot_count, width, width), BF16),
        in_specs=[smem, smem, vmem, vmem],
        out_specs=pl.BlockSpec(memory_space=pl.ANY),
        scratch_shapes=[
            pltpu.VMEM((local_count, width, points), BF16),
            pltpu.VMEM((local_count, local_count, width, width), BF16),
            pltpu.SemaphoreType.DMA,
        ],
        cost_estimate=pl.CostEstimate(
            flops=2 * (local_count * width) ** 2 * points,
            transcendentals=0,
            bytes_accessed=2 * basis.size + 2 * task_count * width * width,
        ),
        name="pair_blocks",
    )(pairs.reshape(-1), places, basis, potential)


def fock_kernel(slots, arrived, out, total):
    step = pl.program_id(0)
    chunk = arrived.shape[0]

    @pl.when(step == 0)
    def _():
        total[...] = jnp.zeros_like(total)

    def add(t, carry):
        slot = slots[step * chunk + t]

        @pl.when(slot >= 0)
        def _():
            total[slot] += arrived[t].astype(F32)

        return carry

    lax.fori_loop(0, chunk, add, 0)

    @pl.when(step == pl.num_programs(0) - 1)
    def _():
        out[...] = total[...].astype(BF16)


def fock_sum(slots, arrived, slot_count):
    count, width, _ = arrived.shape
    chunk = 32
    return pl.pallas_call(
        fock_kernel,
        grid=(count // chunk,),
        out_shape=jax.ShapeDtypeStruct((slot_count, width, width), BF16),
        in_specs=[
            pl.BlockSpec(memory_space=pltpu.SMEM),
            pl.BlockSpec((chunk, width, width), lambda s: (s, 0, 0)),
        ],
        out_specs=pl.BlockSpec((slot_count, width, width), lambda s: (0, 0, 0)),
        scratch_shapes=[pltpu.VMEM((slot_count, width, width), F32)],
        cost_estimate=pl.CostEstimate(
            flops=arrived.size, transcendentals=0, bytes_accessed=2 * arrived.size
        ),
        name="fock_sum",
    )(slots, arrived)


def square_kernel(places, cell_rows, where, picks, *refs):
    pieces = refs[: len(places)]
    out, left, right, sems = refs[len(places) :]
    cells = left.shape[0] // cell_rows
    width = left.shape[-1]
    zero = right.shape[0] - 1
    copies = []
    for n, (side, cell_count) in enumerate(places):
        size = cell_count * cell_rows
        first = pl.multiple_of(where[n], cell_rows)
        target = (left if side == 0 else right).at[pl.ds(first, size)]
        copies.append(pltpu.make_async_copy(pieces[n], target, sems.at[n]))
    for copy in copies:
        copy.start()
    right[zero] = jnp.zeros((width, width), BF16)
    for copy in copies:
        copy.wait()

    def block_row(q, carry):
        total = jnp.zeros((width, 2 * width), F32)
        for k in range(0, cells, 2):
            a = jnp.concatenate([left[k * cell_rows + q], left[(k + 1) * cell_rows + q]], axis=1)
            b = [[right[picks[(q * cells + k + h) * 2 + j]] for j in range(2)] for h in range(2)]
            b = jnp.concatenate([jnp.concatenate(b[h], axis=1) for h in range(2)], axis=0)
            total += jnp.dot(a, b, preferred_element_type=F32)
        out[q] = total[:, :width].astype(BF16)
        out[cell_rows + q] = total[:, width:].astype(BF16)
        return carry

    lax.fori_loop(0, cell_rows, block_row, 0)


def square_sum(picks, pieces, cells, cell_rows, width):
    places = tuple((side, piece.shape[0] // cell_rows) for side, _, piece in pieces)
    where = jnp.stack([first for _, first, _ in pieces]).astype(jnp.int32) * cell_rows
    smem = pl.BlockSpec(memory_space=pltpu.SMEM)
    return pl.pallas_call(
        functools.partial(square_kernel, places, cell_rows),
        out_shape=jax.ShapeDtypeStruct((2 * cell_rows, width, width), BF16),
        in_specs=[smem, smem] + [pl.BlockSpec(memory_space=pl.ANY)] * len(pieces),
        out_specs=pl.BlockSpec(memory_space=pltpu.VMEM),
        scratch_shapes=[
            pltpu.VMEM((cells * cell_rows, width, width), BF16),
            pltpu.VMEM((cells * 2 * cell_rows + 1, width, width), BF16),
            pltpu.SemaphoreType.DMA((len(pieces),)),
        ],
        cost_estimate=pl.CostEstimate(
            flops=4 * cells * cell_rows * width**3,
            transcendentals=0,
            bytes_accessed=2 * 3 * cells * cell_rows * width * width,
        ),
        name="square_sum",
    )(where, picks, *[piece for _, _, piece in pieces])


def ring_and_pair(own, ring, pair, half):
    got = {(0, 0): [(None, own)]}
    across = shift(own, pair, 1)
    got[(0, 1)] = [(None, across)]
    for other, value in ((0, own), (1, across)):
        behind, ahead = shift(value, ring, 1), shift(value, ring, -1)
        got[(3, other)] = [(None, behind)]
        got[(1, other)] = [(None, ahead)]
        got[(2, other)] = [
            (0, shift(behind[:half], ring, 1)),
            (1, shift(ahead[half:], ring, -1)),
        ]
    return got


def body(basis_values, potential, task_pairs, task_owner, task_slot, matrix_blocks, matrix_columns):
    x, yl, c, z, yh = (lax.axis_index(axis) for axis in ALL)
    cell_rows, width = matrix_blocks.shape[2], matrix_blocks.shape[3]
    row_count = lax.axis_size(ROW)
    device_count = row_count * lax.axis_size(COL)
    cells = 2 * lax.axis_size(COL)
    own = matrix_blocks.reshape(2 * cell_rows, width, width)

    rows = ring_and_pair(own, "z", "yh", cell_rows)
    columns = ring_and_pair(own, "x", "yl", cell_rows)
    pieces = []
    for (ring, pair), values in rows.items():
        first = 2 * (((z + ring) % 4) * 2 + (yh + pair) % 2)
        for half, value in values:
            pieces.append((0, first + (half or 0), value))
    for (ring, pair), values in columns.items():
        first = 2 * ((((x + ring) % 4) * 2 + (yl + pair) % 2) * 2 + c)
        other = 2 * ((((x + ring) % 4) * 2 + (yl + pair) % 2) * 2 + (1 - c))
        for half, value in values:
            pieces.append((1, first + (half or 0), value))
            pieces.append((1, other + (half or 0), shift(value, "c", 1)))

    owners, slots = task_owner.reshape(-1), task_slot.reshape(-1)
    task_count = owners.shape[0]
    order = jnp.arange(task_count, dtype=jnp.int32)
    earlier = (owners[:, None] == owners[None, :]) & (order[None, :] < order[:, None])
    places = owners * 2 + jnp.sum(earlier.astype(jnp.int32), axis=1)
    spots = jnp.arange(2 * device_count, dtype=jnp.int32)
    named = places[None, :] == spots[:, None]
    send_slots = jnp.max(jnp.where(named, slots[None, :], -1), axis=1)
    send = pair_blocks(basis_values[0, 0], potential[0], task_pairs[0, 0], places, 2 * device_count)

    own_columns = matrix_columns.reshape(1, -1)
    numbers = jnp.concatenate(
        [
            send_slots.reshape(device_count, 2),
            jnp.broadcast_to(own_columns, (device_count, own_columns.shape[1])),
        ],
        axis=1,
    )
    numbers = lax.all_to_all(numbers[:, None, :], ALL, 0, 0, tiled=True)[:, 0, :]
    arrived = lax.all_to_all(send, ALL, 0, 0, tiled=True)
    fock = fock_sum(numbers[:, :2].reshape(-1), arrived, 2 * cell_rows)

    every = numbers[:, 2:].reshape(row_count, cells, cell_rows)
    me_row = (x * 2 + yl) * 2 + c
    me_col = z * 2 + yh
    left_columns = lax.dynamic_index_in_dim(every, me_row, 0, keepdims=False)
    right_columns = lax.dynamic_slice_in_dim(every, 2 * me_col, 2, 1)
    target = matrix_columns.reshape(2, cell_rows)
    slot_range = jnp.arange(cell_rows, dtype=jnp.int32)
    cell_range = jnp.arange(cells, dtype=jnp.int32)
    chosen = left_columns.T[:, :, None, None] == slot_range
    found = jnp.sum(jnp.where(chosen, right_columns[None], 0), axis=-1)
    spot = (cell_range[None, :, None] * 2 + jnp.arange(2, dtype=jnp.int32)) * cell_rows
    spot = spot + left_columns.T[:, :, None]
    picks = jnp.where(found == target.T[:, None, :], spot, cells * 2 * cell_rows)
    square = square_sum(picks.reshape(-1), pieces, cells, cell_rows, width)
    shape = (1, 2, cell_rows, width, width)
    return fock.reshape(shape), square.reshape(shape)


def solution(mesh):
    finer = Mesh(mesh.devices.reshape(4, 2, 2, 4, 2), ALL)
    return jax.shard_map(
        body,
        mesh=finer,
        in_specs=(
            P(ROW, COL, None, None, None),
            P(ROW, COL, None),
            P(ROW, COL, None, None),
            P(ROW, COL, None, None),
            P(ROW, COL, None),
            P(ROW, COL, None, None, None),
            P(ROW, COL, None),
        ),
        out_specs=(P(ROW, COL, None, None, None), P(ROW, COL, None, None, None)),
        check_vma=False,
    )
```

time: 385 us -> 286 us (0.74)
  waiting for transfers between devices: 15.9 us -> 165 us
  blocking collectives: 129 us -> 0 us
  matrix products: 95.9 us -> 0 us
  local copies, waits for them, and re-layouts: 100 us -> 11.2 us
  starting transfers between devices: 19.5 us -> 63.9 us
  Pallas kernels: 0 us -> 39.6 us
  between operations: 13.9 us -> 0.96 us
    ppermute x0 -> x28, waiting for transfers between devices: none -> 165 us  [shift(): lax.ppermute(value, axis, [(i, (i + step) % size) for i in range(size)])]
    all_gather x3 -> x0, blocking collectives: 129 us -> none  [the longest x1 113 us: body(): piece_columns = lax.all_gather(own_columns[None], 'row', axis=0, tiled=True)]
    dot_general x28 -> x0, matrix products: 95.9 us -> none  [the longest x8 29.5 us: one_group(): jnp.dot(left_hits, weighted_flat, preferred_element_type=jnp.float32)]
    ppermute x0 -> x28, starting transfers between devices: none -> 42.1 us  [shift(): lax.ppermute(value, axis, [(i, (i + step) % size) for i in range(size)])]
    pallas_call x0 -> x3, Pallas kernels: none -> 39.6 us  [the longest x1 15.2 us: pair_blocks(): pl.pallas_call(pair_kernel, out_shape=jax.ShapeDtypeStruct((slot_count, w...]
    while x32 -> x0, local copies, waits for them, and re-layouts: 37.3 us -> none
    unnamed x17 -> x27, local copies, waits for them, and re-layouts: 34.8 us -> 0.84 us
    reshape x1 -> x3, local copies, waits for them, and re-layouts: 25.3 us -> 0.9 us  [the longest x1 0.69 us: body(): fock = fock_sum(numbers[:, :2].reshape(-1), arrived, 2 * cell_rows)]
  transfers between devices with their start and end apart: 5 -> 30, of which waited for: 1 -> 8; matrix products, arithmetic and copies ran while one was open for 50% -> 4% of each run, Pallas kernels for 0% -> 11%
where the time goes in v1:
time: 286 us; the launch traced here: 285 us
  waiting for transfers between devices  165 us (58%)
  starting transfers between devices  63.9 us (22%)
  Pallas kernels  39.6 us (14%)
  local copies, waits for them, and re-layouts  11.2 us (4%)
  other arithmetic  4.34 us (2%)
    ppermute x28, waiting for transfers between devices, shift(): lax.ppermute(value, axis, [(i, (i + step) % size) for i in range(size)])  165 us
    ppermute x28, starting transfers between devices, shift(): lax.ppermute(value, axis, [(i, (i + step) % size) for i in range(size)])  42.1 us
    pallas_call x1, Pallas kernels, pair_blocks(): pl.pallas_call(pair_kernel, out_shape=jax.ShapeDtypeStruct((slot_count, w...  15.2 us
    pallas_call x1, Pallas kernels, square_sum(): pl.pallas_call(functools.partial(square_kernel, places, cell_rows), out_s...  15.1 us
    all_to_all x1, starting transfers between devices, body(): lax.all_to_all(numbers[:, None, :], ALL, 0, 0, tiled=True)[:, 0, :]  11.5 us
    all_to_all x1, starting transfers between devices, body(): arrived = lax.all_to_all(send, ALL, 0, 0, tiled=True)  10.2 us
    pallas_call x1, Pallas kernels, fock_sum(): pl.pallas_call(fock_kernel, grid=(count // chunk,), out_shape=jax.ShapeDt...  9.21 us
  transfers between devices with their start and end apart: 30, of which 8 were waited for; matrix products, arithmetic and copies ran while one was open for 4% of the time, Pallas kernels for 11%

profile of v1, /device:TPU:1, one launch (start us, length us, event | category | flops | bytes accessed | tf_op | source)
XLA Modules:
  0.0 285.1 jit_solution(17167927761966656361)
XLA Ops:
  0.6 0.9 convert_reduce_fusion
  1.5 0.7 multiply_add_fusion.places
  2.2 0.8 reshape.100
  3.0 0.8 select_reduce_fusion.1
  3.7 0.1 reshape.93
  3.9 0.1 pad.1.clone
  4.0 0.6 pad_add_fusion
  4.6 11.5 %all-to-all-start = ((s32[128,1,34]{2,1,0:T(1,128)}), s32[128,1,34]{2,1,0:T(1,128)S(1)}, u32[]{:S(2)}, u32[]{:S(2)}) async-start(s32[128,1,34]{2,1,0:T(1,128)} %bitcast.2), calls=%async_computation | async-start | bytes 131072 | tf_op jit(solution)/shard_map/all_to_all | solution.py:228
  16.1 0.8 copy.20
  16.9 0.7 reshape_squeeze.3.pairs
  17.6 15.2 %pair_blocks.1 = bf16[256,128,128]{2,1,0:T(8,128)(2,1)} custom-call(s32[256]{0:T(256)} %reshape_squeeze.3.pairs, s32[128]{0:T(128)} %copy-done.12, bf16[16,128,1024]{2,1,0:T(8,128)(2,1)} %bitcast.65, f32[1,1024]{1,0:T(1,128)} %bitcast.66), custom_call_target="tpu_custom_call" | custom-call | flops 8589934592 | bytes 8388608 | tf_op jit(solution)/shard_map/pair_blocks/pallas_call | solution.py:55
  32.8 0.0 copy-start
  32.8 0.0 copy-start.11
  32.9 10.2 %all-to-all-start.1 = ((bf16[256,128,128]{2,1,0:T(8,128)(2,1)}), bf16[256,128,128]{2,1,0:T(8,128)(2,1)}, u32[]{:S(2)}, u32[]{:S(2)}) async-start(bf16[256,128,128]{2,1,0:T(8,128)(2,1)} %pair_blocks.1), calls=%async_computation.1 | async-start | bytes 16777216 | tf_op jit(solution)/shard_map/all_to_all | solution.py:229
  43.1 2.7 collective-permute-start.14
  45.8 3.1 %collective-permute-start.2 = (bf16[32,128,128]{2,1,0:T(8,128)(2,1)S(1)}, bf16[32,128,128]{2,1,0:T(8,128)(2,1)S(1)}, u32[]{:S(2)}, u32[]{:S(2)}) collective-permute-start(bf16[32,128,128]{2,1,0:T(8,128)(2,1)S(1)} %bitcast.54), channel_id=1, source_target_pairs={{0,6},{2,0},{4,2},{6,4},{1,7},{3,1},{5,3},{7,5},{8,14},{10,8},{12,... | collective-permute-start | bytes 3145736 | tf_op jit(solution)/shard_map/ppermute | solution.py:20
  48.9 1.2 collective-permute-start.10
  50.1 1.2 collective-permute-start.9
  51.3 111.3 %collective-permute-done.14.refs_16_ = bf16[32,128,128]{2,1,0:T(8,128)(2,1)S(1)} collective-permute-done((bf16[32,128,128]{2,1,0:T(8,128)(2,1)S(1)}, bf16[32,128,128]{2,1,0:T(8,128)(2,1)S(1)}, u32[]{:S(2)}, u32[]{:S(2)}) %collective-permute-start.14) | collective-permute-done | bytes 1048608 | tf_op jit(solution)/shard_map/ppermute | solution.py:20
  162.6 0.3 collective-permute-start.1
  163.0 5.8 %collective-permute-start = (bf16[32,128,128]{2,1,0:T(8,128)(2,1)S(1)}, bf16[32,128,128]{2,1,0:T(8,128)(2,1)}, u32[]{:S(2)}, u32[]{:S(2)}) collective-permute-start(bf16[32,128,128]{2,1,0:T(8,128)(2,1)S(1)} %bitcast.58), channel_id=1, source_target_pairs={{0,1},{1,0},{2,3},{3,2},{4,5},{5,4},{6,7},{7,6},{8,9},{9,8},{10,11... | collective-permute-start | bytes 3145736 | tf_op jit(solution)/shard_map/ppermute | solution.py:20
  168.9 0.1 collective-permute-start.18
  169.0 1.5 collective-permute-start.16
  170.6 17.3 %collective-permute-done.1.refs_2_ = bf16[32,128,128]{2,1,0:T(8,128)(2,1)S(1)} collective-permute-done((bf16[32,128,128]{2,1,0:T(8,128)(2,1)S(1)}, bf16[32,128,128]{2,1,0:T(8,128)(2,1)S(1)}, u32[]{:S(2)}, u32[]{:S(2)}) %collective-permute-start.1) | collective-permute-done | bytes 1048608 | tf_op jit(solution)/shard_map/ppermute | solution.py:20
  187.9 2.3 collective-permute-start.22
  190.2 1.0 collective-permute-done.refs_1_
  191.3 0.5 collective-permute-start.3
  191.8 2.3 collective-permute-start.6
  194.0 2.3 collective-permute-start.19
  196.4 7.8 %collective-permute-done.3.refs_4_ = bf16[16,128,128]{2,1,0:T(8,128)(2,1)S(1)} collective-permute-done((bf16[16,128,128]{2,1,0:T(8,128)(2,1)S(1)}, bf16[16,128,128]{2,1,0:T(8,128)(2,1)S(1)}, u32[]{:S(2)}, u32[]{:S(2)}) %collective-permute-start.3) | collective-permute-done | bytes 524320 | tf_op jit(solution)/shard_map/ppermute | solution.py:20
  204.2 2.7 collective-permute-start.15
  206.9 0.1 collective-permute-start.13
  207.0 4.3 %collective-permute-done.22.refs_24_ = bf16[32,128,128]{2,1,0:T(8,128)(2,1)} collective-permute-done((bf16[32,128,128]{2,1,0:T(8,128)(2,1)}, bf16[32,128,128]{2,1,0:T(8,128)(2,1)}, u32[]{:S(2)}, u32[]{:S(2)}) %collective-permute-start.22) | collective-permute-done | bytes 1048608 | tf_op jit(solution)/shard_map/ppermute | solution.py:20
  211.3 2.6 collective-permute-start.11
  213.9 1.7 collective-permute-done.20.refs_22_
  215.5 0.7 collective-permute-start.5
  216.3 2.7 collective-permute-start.17
  219.0 0.1 stack.123
  219.1 0.5 broadcast_multiply_fusion.where
  219.6 1.9 slice.49
  221.5 0.8 slice.48
  222.4 1.9 slice.45
  224.3 1.4 collective-permute-start.26
  225.7 0.1 collective-permute-start.24
  225.7 3.6 %collective-permute-start.8 = (bf16[16,128,128]{2,1,0:T(8,128)(2,1)}, bf16[16,128,128]{2,1,0:T(8,128)(2,1)}, u32[]{:S(2)}, u32[]{:S(2)}) collective-permute-start(bf16[16,128,128]{2,1,0:T(8,128)(2,1)} %slice.45), channel_id=1, source_target_pairs={{0,6},{2,0},{4,2},{6,4},{1,7},{3,1},{5,3},{7,5},{8,14},{10,8},{12,... | collective-permute-start | bytes 1572872 | tf_op jit(solution)/shard_map/ppermute | solution.py:20
  229.3 0.7 collective-permute-start.23
  230.1 8.9 %collective-permute-done.5.refs_6_ = bf16[32,128,128]{2,1,0:T(8,128)(2,1)} collective-permute-done((bf16[32,128,128]{2,1,0:T(8,128)(2,1)}, bf16[32,128,128]{2,1,0:T(8,128)(2,1)}, u32[]{:S(2)}, u32[]{:S(2)}) %collective-permute-start.5) | collective-permute-done | bytes 1048608 | tf_op jit(solution)/shard_map/ppermute | solution.py:20
  239.0 3.6 %collective-permute-start.21 = (bf16[32,128,128]{2,1,0:T(8,128)(2,1)S(1)}, bf16[32,128,128]{2,1,0:T(8,128)(2,1)}, u32[]{:S(2)}, u32[]{:S(2)}) collective-permute-start(bf16[32,128,128]{2,1,0:T(8,128)(2,1)S(1)} %collective-permute-done.20.refs_22_), channel_id=1, source_target_pairs={{0,8},{8,0},{1,9},{9,1},{2,10},{10,2},{3,11},{11,3},{4,12},{12,4},... | collective-permute-start | bytes 3145736 | tf_op jit(solution)/shard_map/ppermute | solution.py:20
  242.6 0.1 copy.23
  242.7 0.1 slice.41
  242.8 0.7 reshape.94.slots
  243.5 0.1 reshape.96
  243.6 0.1 copy.21
  243.7 1.9 slice.44
  245.6 0.1 collective-permute-start.27
  245.7 0.5 collective-permute-start.25
  246.2 0.1 iota_compare_fusion
  246.3 0.6 select_reduce_fusion
  246.9 0.1 compare_select_fusion
  247.0 0.2 copy.25
  247.2 0.7 select_n.163.picks
  247.9 12.7 %collective-permute-done.7.refs_8_ = bf16[16,128,128]{2,1,0:T(8,128)(2,1)} collective-permute-done((bf16[16,128,128]{2,1,0:T(8,128)(2,1)}, bf16[16,128,128]{2,1,0:T(8,128)(2,1)}, u32[]{:S(2)}, u32[]{:S(2)}) %collective-permute-start.7) | collective-permute-done | bytes 524320 | tf_op jit(solution)/shard_map/ppermute | solution.py:20
  260.7 15.1 %square_sum.1 = bf16[32,128,128]{2,1,0:T(8,128)(2,1)} custom-call(s32[30]{0:T(128)} %broadcast_multiply_fusion.where, s32[512]{0:T(512)} %select_n.163.picks, bf16[32,128,128]{2,1,0:T(8,128)(2,1)} %bitcast.50, bf16[32,128,128]{2,1,0:T(8,128)(2,1)} %collective-permute-done.refs_1_, bf16[32,128,128]{2,1,0:T(8,128)(2,1)} %copy-done.4, ...), custom_call_target="tpu_custom_call" | custom-call | flops 2147483648 | bytes 25165824 | tf_op jit(solution)/shard_map/square_sum/pallas_call | solution.py:154
  275.9 9.2 %fock_sum.1 = bf16[32,128,128]{2,1,0:T(8,128)(2,1)} custom-call(s32[256]{0:T(256)} %reshape.94.slots, bf16[256,128,128]{2,1,0:T(8,128)(2,1)} %all-to-all-done.1.arrived), custom_call_target="tpu_custom_call" | custom-call | flops 4194304 | bytes 8388608 | tf_op jit(solution)/shard_map/fock_sum/pallas_call | solution.py:101
  (59 shorter events, 0.3 us)
Async XLA Ops:
  2.2 15.4 %copy-start.12 = (s32[128]{0:T(128)}, s32[128]{0:T(128)S(1)}, u32[]{:S(2)}) copy-start(s32[128]{0:T(128)S(1)} %multiply_add_fusion.places) | copy-start | bytes 1540
  4.6 28.3 %all-to-all-start = ((s32[128,1,34]{2,1,0:T(1,128)}), s32[128,1,34]{2,1,0:T(1,128)S(1)}, u32[]{:S(2)}, u32[]{:S(2)}) async-start(s32[128,1,34]{2,1,0:T(1,128)} %bitcast.2), calls=%async_computation | async-start | bytes 131072 | tf_op jit(solution)/shard_map/all_to_all | solution.py:228
  32.8 10.3 %copy-start = (bf16[1,2,16,128,128]{4,3,2,1,0:T(8,128)(2,1)S(1)}, bf16[1,2,16,128,128]{4,3,2,1,0:T(8,128)(2,1)}, u32[]{:S(2)}) copy-start(bf16[1,2,16,128,128]{4,3,2,1,0:T(8,128)(2,1)} %param.12) | copy-start | bytes 3145732
  32.8 209.8 %copy-start.11 = (s32[1,2,16]{2,1,0:T(2,128)S(1)}, s32[1,2,16]{2,1,0:T(2,128)}, u32[]{:S(2)}) copy-start(s32[1,2,16]{2,1,0:T(2,128)} %param.13) | copy-start | bytes 388
  32.9 243.0 %all-to-all-start.1 = ((bf16[256,128,128]{2,1,0:T(8,128)(2,1)}), bf16[256,128,128]{2,1,0:T(8,128)(2,1)}, u32[]{:S(2)}, u32[]{:S(2)}) async-start(bf16[256,128,128]{2,1,0:T(8,128)(2,1)} %pair_blocks.1), calls=%async_computation.1 | async-start | bytes 16777216 | tf_op jit(solution)/shard_map/all_to_all | solution.py:229
  43.1 119.5 %collective-permute-start.14 = (bf16[32,128,128]{2,1,0:T(8,128)(2,1)S(1)}, bf16[32,128,128]{2,1,0:T(8,128)(2,1)S(1)}, u32[]{:S(2)}, u32[]{:S(2)}) collective-permute-start(bf16[32,128,128]{2,1,0:T(8,128)(2,1)S(1)} %bitcast.52), channel_id=1, source_target_pairs={{0,96},{32,0},{64,32},{96,64},{1,97},{33,1},{65,33},{97,65},{2,98}... | collective-permute-start | bytes 3145736 | tf_op jit(solution)/shard_map/ppermute | solution.py:20
  45.8 117.2 %collective-permute-start.12 = (bf16[32,128,128]{2,1,0:T(8,128)(2,1)S(1)}, bf16[32,128,128]{2,1,0:T(8,128)(2,1)S(1)}, u32[]{:S(2)}, u32[]{:S(2)}) collective-permute-start(bf16[32,128,128]{2,1,0:T(8,128)(2,1)S(1)} %bitcast.53), channel_id=1, source_target_pairs={{0,32},{32,64},{64,96},{96,0},{1,33},{33,65},{65,97},{97,1},{2,34}... | collective-permute-start | bytes 3145736 | tf_op jit(solution)/shard_map/ppermute | solution.py:20
  45.8 123.1 %collective-permute-start.2 = (bf16[32,128,128]{2,1,0:T(8,128)(2,1)S(1)}, bf16[32,128,128]{2,1,0:T(8,128)(2,1)S(1)}, u32[]{:S(2)}, u32[]{:S(2)}) collective-permute-start(bf16[32,128,128]{2,1,0:T(8,128)(2,1)S(1)} %bitcast.54), channel_id=1, source_target_pairs={{0,6},{2,0},{4,2},{6,4},{1,7},{3,1},{5,3},{7,5},{8,14},{10,8},{12,... | collective-permute-start | bytes 3145736 | tf_op jit(solution)/shard_map/ppermute | solution.py:20
  48.9 120.2 %collective-permute-start.10 = (bf16[32,128,128]{2,1,0:T(8,128)(2,1)S(1)}, bf16[32,128,128]{2,1,0:T(8,128)(2,1)}, u32[]{:S(2)}, u32[]{:S(2)}) collective-permute-start(bf16[32,128,128]{2,1,0:T(8,128)(2,1)S(1)} %bitcast.55), channel_id=1, source_target_pairs={{0,16},{16,0},{1,17},{17,1},{2,18},{18,2},{3,19},{19,3},{4,20},{20... | collective-permute-start | bytes 3145736 | tf_op jit(solution)/shard_map/ppermute | solution.py:20
  50.1 120.4 %collective-permute-start.9 = (bf16[32,128,128]{2,1,0:T(8,128)(2,1)S(1)}, bf16[32,128,128]{2,1,0:T(8,128)(2,1)S(1)}, u32[]{:S(2)}, u32[]{:S(2)}) collective-permute-start(bf16[32,128,128]{2,1,0:T(8,128)(2,1)S(1)} %bitcast.56), channel_id=1, source_target_pairs={{0,8},{8,0},{1,9},{9,1},{2,10},{10,2},{3,11},{11,3},{4,12},{12,4},... | collective-permute-start | bytes 3145736 | tf_op jit(solution)/shard_map/ppermute | solution.py:20
  162.6 98.0 %copy-start.1 = (bf16[32,128,128]{2,1,0:T(8,128)(2,1)}, bf16[32,128,128]{2,1,0:T(8,128)(2,1)S(1)}, u32[]{:S(2)}) copy-start(bf16[32,128,128]{2,1,0:T(8,128)(2,1)S(1)} %collective-permute-done.14.refs_16_) | copy-start | bytes 3145732
  162.6 25.2 %collective-permute-start.1 = (bf16[32,128,128]{2,1,0:T(8,128)(2,1)S(1)}, bf16[32,128,128]{2,1,0:T(8,128)(2,1)S(1)}, u32[]{:S(2)}, u32[]{:S(2)}) collective-permute-start(bf16[32,128,128]{2,1,0:T(8,128)(2,1)S(1)} %bitcast.57), channel_id=1, source_target_pairs={{0,2},{2,4},{4,6},{6,0},{1,3},{3,5},{5,7},{7,1},{8,10},{10,12},{12... | collective-permute-start | bytes 3145736 | tf_op jit(solution)/shard_map/ppermute | solution.py:20
  163.0 97.7 %copy-start.2 = (bf16[32,128,128]{2,1,0:T(8,128)(2,1)}, bf16[32,128,128]{2,1,0:T(8,128)(2,1)S(1)}, u32[]{:S(2)}) copy-start(bf16[32,128,128]{2,1,0:T(8,128)(2,1)S(1)} %collective-permute-done.12.refs_14_) | copy-start | bytes 3145732
  163.0 28.3 %collective-permute-start = (bf16[32,128,128]{2,1,0:T(8,128)(2,1)S(1)}, bf16[32,128,128]{2,1,0:T(8,128)(2,1)}, u32[]{:S(2)}, u32[]{:S(2)}) collective-permute-start(bf16[32,128,128]{2,1,0:T(8,128)(2,1)S(1)} %bitcast.58), channel_id=1, source_target_pairs={{0,1},{1,0},{2,3},{3,2},{4,5},{5,4},{6,7},{7,6},{8,9},{9,8},{10,11... | collective-permute-start | bytes 3145736 | tf_op jit(solution)/shard_map/ppermute | solution.py:20
  168.9 38.0 %copy-start.3 = (bf16[32,128,128]{2,1,0:T(8,128)(2,1)}, bf16[32,128,128]{2,1,0:T(8,128)(2,1)S(1)}, u32[]{:S(2)}) copy-start(bf16[32,128,128]{2,1,0:T(8,128)(2,1)S(1)} %collective-permute-done.2.refs_3_) | copy-start | bytes 3145732
  168.9 22.4 %collective-permute-start.18 = (bf16[16,128,128]{2,1,0:T(8,128)(2,1)S(1)}, bf16[16,128,128]{2,1,0:T(8,128)(2,1)S(1)}, u32[]{:S(2)}, u32[]{:S(2)}) collective-permute-start(bf16[16,128,128]{2,1,0:T(8,128)(2,1)S(1)} %slice.47), channel_id=1, source_target_pairs={{0,96},{32,0},{64,32},{96,64},{1,97},{33,1},{65,33},{97,65},{2,98}... | collective-permute-start | bytes 1572872 | tf_op jit(solution)/shard_map/ppermute | solution.py:20
  169.0 22.7 %collective-permute-start.16 = (bf16[16,128,128]{2,1,0:T(8,128)(2,1)S(1)}, bf16[16,128,128]{2,1,0:T(8,128)(2,1)}, u32[]{:S(2)}, u32[]{:S(2)}) collective-permute-start(bf16[16,128,128]{2,1,0:T(8,128)(2,1)S(1)} %slice.46), channel_id=1, source_target_pairs={{0,32},{32,64},{64,96},{96,0},{1,33},{33,65},{65,97},{97,1},{2,34}... | collective-permute-start | bytes 1572872 | tf_op jit(solution)/shard_map/ppermute | solution.py:20
  170.6 45.0 %copy-start.6 = (bf16[32,128,128]{2,1,0:T(8,128)(2,1)}, bf16[32,128,128]{2,1,0:T(8,128)(2,1)S(1)}, u32[]{:S(2)}) copy-start(bf16[32,128,128]{2,1,0:T(8,128)(2,1)S(1)} %collective-permute-done.9.refs_11_) | copy-start | bytes 3145732
  170.6 23.5 %collective-permute-start.4 = (bf16[16,128,128]{2,1,0:T(8,128)(2,1)S(1)}, bf16[16,128,128]{2,1,0:T(8,128)(2,1)S(1)}, u32[]{:S(2)}, u32[]{:S(2)}) collective-permute-start(bf16[16,128,128]{2,1,0:T(8,128)(2,1)S(1)} %slice.43), channel_id=1, source_target_pairs={{0,6},{2,0},{4,2},{6,4},{1,7},{3,1},{5,3},{7,5},{8,14},{10,8},{12,... | collective-permute-start | bytes 1572872 | tf_op jit(solution)/shard_map/ppermute | solution.py:20
  187.9 19.0 %copy-start.4 = (bf16[32,128,128]{2,1,0:T(8,128)(2,1)}, bf16[32,128,128]{2,1,0:T(8,128)(2,1)S(1)}, u32[]{:S(2)}) copy-start(bf16[32,128,128]{2,1,0:T(8,128)(2,1)S(1)} %collective-permute-done.1.refs_2_) | copy-start | bytes 3145732
  187.9 23.4 %collective-permute-start.22 = (bf16[32,128,128]{2,1,0:T(8,128)(2,1)}, bf16[32,128,128]{2,1,0:T(8,128)(2,1)}, u32[]{:S(2)}, u32[]{:S(2)}) collective-permute-start(bf16[32,128,128]{2,1,0:T(8,128)(2,1)} %collective-permute-done.10.refs_12_), channel_id=1, source_target_pairs={{0,96},{32,0},{64,32},{96,64},{1,97},{33,1},{65,33},{97,65},{2,98}... | collective-permute-start | bytes 3145736 | tf_op jit(solution)/shard_map/ppermute | solution.py:20
  191.2 24.3 %collective-permute-start.20 = (bf16[32,128,128]{2,1,0:T(8,128)(2,1)}, bf16[32,128,128]{2,1,0:T(8,128)(2,1)S(1)}, u32[]{:S(2)}, u32[]{:S(2)}) collective-permute-start(bf16[32,128,128]{2,1,0:T(8,128)(2,1)} %collective-permute-done.10.refs_12_), channel_id=1, source_target_pairs={{0,32},{32,64},{64,96},{96,0},{1,33},{33,65},{65,97},{97,1},{2,34}... | collective-permute-start | bytes 3145736 | tf_op jit(solution)/shard_map/ppermute | solution.py:20
  191.3 25.0 %copy-start.7 = (bf16[16,128,128]{2,1,0:T(8,128)(2,1)}, bf16[16,128,128]{2,1,0:T(8,128)(2,1)S(1)}, u32[]{:S(2)}) copy-start(bf16[16,128,128]{2,1,0:T(8,128)(2,1)S(1)} %collective-permute-done.18.refs_20_) | copy-start | bytes 1572868
  191.3 12.9 %collective-permute-start.3 = (bf16[16,128,128]{2,1,0:T(8,128)(2,1)S(1)}, bf16[16,128,128]{2,1,0:T(8,128)(2,1)S(1)}, u32[]{:S(2)}, u32[]{:S(2)}) collective-permute-start(bf16[16,128,128]{2,1,0:T(8,128)(2,1)S(1)} %slice.42), channel_id=1, source_target_pairs={{0,2},{2,4},{4,6},{6,0},{1,3},{3,5},{5,7},{7,1},{8,10},{10,12},{12... | collective-permute-start | bytes 1572872 | tf_op jit(solution)/shard_map/ppermute | solution.py:20
  191.8 24.5 %collective-permute-start.6 = (bf16[32,128,128]{2,1,0:T(8,128)(2,1)}, bf16[32,128,128]{2,1,0:T(8,128)(2,1)}, u32[]{:S(2)}, u32[]{:S(2)}) collective-permute-start(bf16[32,128,128]{2,1,0:T(8,128)(2,1)} %collective-permute-done.refs_1_), channel_id=1, source_target_pairs={{0,6},{2,0},{4,2},{6,4},{1,7},{3,1},{5,3},{7,5},{8,14},{10,8},{12,... | collective-permute-start | bytes 3145736 | tf_op jit(solution)/shard_map/ppermute | solution.py:20
  194.0 22.2 %copy-start.8 = (bf16[16,128,128]{2,1,0:T(8,128)(2,1)}, bf16[16,128,128]{2,1,0:T(8,128)(2,1)S(1)}, u32[]{:S(2)}) copy-start(bf16[16,128,128]{2,1,0:T(8,128)(2,1)S(1)} %collective-permute-done.4.refs_5_) | copy-start | bytes 1572868
  194.0 12.9 %collective-permute-start.19 = (bf16[16,128,128]{2,1,0:T(8,128)(2,1)S(1)}, bf16[16,128,128]{2,1,0:T(8,128)(2,1)S(1)}, u32[]{:S(2)}, u32[]{:S(2)}) collective-permute-start(bf16[16,128,128]{2,1,0:T(8,128)(2,1)S(1)} %collective-permute-done.18.refs_20_), channel_id=1, source_target_pairs={{0,8},{8,0},{1,9},{9,1},{2,10},{10,2},{3,11},{11,3},{4,12},{12,4},... | collective-permute-start | bytes 1572872 | tf_op jit(solution)/shard_map/ppermute | solution.py:20
  204.2 14.8 %copy-start.9 = (bf16[16,128,128]{2,1,0:T(8,128)(2,1)}, bf16[16,128,128]{2,1,0:T(8,128)(2,1)S(1)}, u32[]{:S(2)}) copy-start(bf16[16,128,128]{2,1,0:T(8,128)(2,1)S(1)} %collective-permute-done.3.refs_4_) | copy-start | bytes 1572868
  204.2 20.0 %collective-permute-start.15 = (bf16[32,128,128]{2,1,0:T(8,128)(2,1)S(1)}, bf16[32,128,128]{2,1,0:T(8,128)(2,1)}, u32[]{:S(2)}, u32[]{:S(2)}) collective-permute-start(bf16[32,128,128]{2,1,0:T(8,128)(2,1)S(1)} %collective-permute-done.14.refs_16_), channel_id=1, source_target_pairs={{0,8},{8,0},{1,9},{9,1},{2,10},{10,2},{3,11},{11,3},{4,12},{12,4},... | collective-permute-start | bytes 3145736 | tf_op jit(solution)/shard_map/ppermute | solution.py:20
  206.9 12.1 %copy-start.10 = (bf16[16,128,128]{2,1,0:T(8,128)(2,1)}, bf16[16,128,128]{2,1,0:T(8,128)(2,1)S(1)}, u32[]{:S(2)}) copy-start(bf16[16,128,128]{2,1,0:T(8,128)(2,1)S(1)} %collective-permute-done.19.refs_21_) | copy-start | bytes 1572868
  206.9 18.8 %collective-permute-start.13 = (bf16[32,128,128]{2,1,0:T(8,128)(2,1)S(1)}, bf16[32,128,128]{2,1,0:T(8,128)(2,1)}, u32[]{:S(2)}, u32[]{:S(2)}) collective-permute-start(bf16[32,128,128]{2,1,0:T(8,128)(2,1)S(1)} %collective-permute-done.12.refs_14_), channel_id=1, source_target_pairs={{0,8},{8,0},{1,9},{9,1},{2,10},{10,2},{3,11},{11,3},{4,12},{12,4},... | collective-permute-start | bytes 3145736 | tf_op jit(solution)/shard_map/ppermute | solution.py:20
  211.3 18.0 %collective-permute-start.11 = (bf16[32,128,128]{2,1,0:T(8,128)(2,1)}, bf16[32,128,128]{2,1,0:T(8,128)(2,1)}, u32[]{:S(2)}, u32[]{:S(2)}) collective-permute-start(bf16[32,128,128]{2,1,0:T(8,128)(2,1)} %collective-permute-done.10.refs_12_), channel_id=1, source_target_pairs={{0,8},{8,0},{1,9},{9,1},{2,10},{10,2},{3,11},{11,3},{4,12},{12,4},... | collective-permute-start | bytes 3145736 | tf_op jit(solution)/shard_map/ppermute | solution.py:20
  215.5 45.2 %copy-start.5 = (bf16[32,128,128]{2,1,0:T(8,128)(2,1)}, bf16[32,128,128]{2,1,0:T(8,128)(2,1)S(1)}, u32[]{:S(2)}) copy-start(bf16[32,128,128]{2,1,0:T(8,128)(2,1)S(1)} %collective-permute-done.20.refs_22_) | copy-start | bytes 3145732
  215.5 23.5 %collective-permute-start.5 = (bf16[32,128,128]{2,1,0:T(8,128)(2,1)}, bf16[32,128,128]{2,1,0:T(8,128)(2,1)}, u32[]{:S(2)}, u32[]{:S(2)}) collective-permute-start(bf16[32,128,128]{2,1,0:T(8,128)(2,1)} %collective-permute-done.refs_1_), channel_id=1, source_target_pairs={{0,2},{2,4},{4,6},{6,0},{1,3},{3,5},{5,7},{7,1},{8,10},{10,12},{12... | collective-permute-start | bytes 3145736 | tf_op jit(solution)/shard_map/ppermute | solution.py:20
  216.3 9.4 %collective-permute-start.17 = (bf16[16,128,128]{2,1,0:T(8,128)(2,1)}, bf16[16,128,128]{2,1,0:T(8,128)(2,1)}, u32[]{:S(2)}, u32[]{:S(2)}) collective-permute-start(bf16[16,128,128]{2,1,0:T(8,128)(2,1)} %collective-permute-done.16.refs_18_), channel_id=1, source_target_pairs={{0,8},{8,0},{1,9},{9,1},{2,10},{10,2},{3,11},{11,3},{4,12},{12,4},... | collective-permute-start | bytes 1572872 | tf_op jit(solution)/shard_map/ppermute | solution.py:20
  224.3 21.3 %collective-permute-start.26 = (bf16[16,128,128]{2,1,0:T(8,128)(2,1)}, bf16[16,128,128]{2,1,0:T(8,128)(2,1)}, u32[]{:S(2)}, u32[]{:S(2)}) collective-permute-start(bf16[16,128,128]{2,1,0:T(8,128)(2,1)} %slice.49), channel_id=1, source_target_pairs={{0,96},{32,0},{64,32},{96,64},{1,97},{33,1},{65,33},{97,65},{2,98}... | collective-permute-start | bytes 1572872 | tf_op jit(solution)/shard_map/ppermute | solution.py:20
  225.7 19.9 %collective-permute-start.24 = (bf16[16,128,128]{2,1,0:T(8,128)(2,1)}, bf16[16,128,128]{2,1,0:T(8,128)(2,1)}, u32[]{:S(2)}, u32[]{:S(2)}) collective-permute-start(bf16[16,128,128]{2,1,0:T(8,128)(2,1)} %slice.48), channel_id=1, source_target_pairs={{0,32},{32,64},{64,96},{96,0},{1,33},{33,65},{65,97},{97,1},{2,34}... | collective-permute-start | bytes 1572872 | tf_op jit(solution)/shard_map/ppermute | solution.py:20
  225.7 20.0 %collective-permute-start.8 = (bf16[16,128,128]{2,1,0:T(8,128)(2,1)}, bf16[16,128,128]{2,1,0:T(8,128)(2,1)}, u32[]{:S(2)}, u32[]{:S(2)}) collective-permute-start(bf16[16,128,128]{2,1,0:T(8,128)(2,1)} %slice.45), channel_id=1, source_target_pairs={{0,6},{2,0},{4,2},{6,4},{1,7},{3,1},{5,3},{7,5},{8,14},{10,8},{12,... | collective-permute-start | bytes 1572872 | tf_op jit(solution)/shard_map/ppermute | solution.py:20
  229.3 31.3 %collective-permute-start.23 = (bf16[32,128,128]{2,1,0:T(8,128)(2,1)}, bf16[32,128,128]{2,1,0:T(8,128)(2,1)}, u32[]{:S(2)}, u32[]{:S(2)}) collective-permute-start(bf16[32,128,128]{2,1,0:T(8,128)(2,1)} %collective-permute-done.22.refs_24_), channel_id=1, source_target_pairs={{0,8},{8,0},{1,9},{9,1},{2,10},{10,2},{3,11},{11,3},{4,12},{12,4},... | collective-permute-start | bytes 3145736 | tf_op jit(solution)/shard_map/ppermute | solution.py:20
  239.0 21.7 %collective-permute-start.21 = (bf16[32,128,128]{2,1,0:T(8,128)(2,1)S(1)}, bf16[32,128,128]{2,1,0:T(8,128)(2,1)}, u32[]{:S(2)}, u32[]{:S(2)}) collective-permute-start(bf16[32,128,128]{2,1,0:T(8,128)(2,1)S(1)} %collective-permute-done.20.refs_22_), channel_id=1, source_target_pairs={{0,8},{8,0},{1,9},{9,1},{2,10},{10,2},{3,11},{11,3},{4,12},{12,4},... | collective-permute-start | bytes 3145736 | tf_op jit(solution)/shard_map/ppermute | solution.py:20
  245.6 15.1 %collective-permute-start.7 = (bf16[16,128,128]{2,1,0:T(8,128)(2,1)}, bf16[16,128,128]{2,1,0:T(8,128)(2,1)}, u32[]{:S(2)}, u32[]{:S(2)}) collective-permute-start(bf16[16,128,128]{2,1,0:T(8,128)(2,1)} %slice.44), channel_id=1, source_target_pairs={{0,2},{2,4},{4,6},{6,0},{1,3},{3,5},{5,7},{7,1},{8,10},{10,12},{12... | collective-permute-start | bytes 1572872 | tf_op jit(solution)/shard_map/ppermute | solution.py:20
  245.6 15.1 %collective-permute-start.27 = (bf16[16,128,128]{2,1,0:T(8,128)(2,1)}, bf16[16,128,128]{2,1,0:T(8,128)(2,1)}, u32[]{:S(2)}, u32[]{:S(2)}) collective-permute-start(bf16[16,128,128]{2,1,0:T(8,128)(2,1)} %collective-permute-done.26.refs_28_), channel_id=1, source_target_pairs={{0,8},{8,0},{1,9},{9,1},{2,10},{10,2},{3,11},{11,3},{4,12},{12,4},... | collective-permute-start | bytes 1572872 | tf_op jit(solution)/shard_map/ppermute | solution.py:20
  245.7 15.0 %collective-permute-start.25 = (bf16[16,128,128]{2,1,0:T(8,128)(2,1)}, bf16[16,128,128]{2,1,0:T(8,128)(2,1)}, u32[]{:S(2)}, u32[]{:S(2)}) collective-permute-start(bf16[16,128,128]{2,1,0:T(8,128)(2,1)} %collective-permute-done.24.refs_26_), channel_id=1, source_target_pairs={{0,8},{8,0},{1,9},{9,1},{2,10},{10,2},{3,11},{11,3},{4,12},{12,4},... | collective-permute-start | bytes 1572872 | tf_op jit(solution)/shard_map/ppermute | solution.py:20

commit v2 on v1

--- a/solution.py
+++ b/solution.py
@@ -170,19 +170,35 @@
     )(where, picks, *[piece for _, _, piece in pieces])
 
 
-def ring_and_pair(own, ring, pair, half):
-    got = {(0, 0): [(None, own)]}
-    across = shift(own, pair, 1)
-    got[(0, 1)] = [(None, across)]
-    for other, value in ((0, own), (1, across)):
-        behind, ahead = shift(value, ring, 1), shift(value, ring, -1)
-        got[(3, other)] = [(None, behind)]
-        got[(1, other)] = [(None, ahead)]
-        got[(2, other)] = [
-            (0, shift(behind[:half], ring, 1)),
-            (1, shift(ahead[half:], ring, -1)),
-        ]
-    return got
+def first_wave(own, ring, pair):
+    return [shift(own, ring, 1), shift(own, ring, -1), shift(own, pair, 1)]
+
+
+def second_wave(first, ring, half):
+    behind, ahead, across = first
+    return [
+        shift(across, ring, 1),
+        shift(across, ring, -1),
+        shift(behind[:half], ring, 1),
+        shift(ahead[half:], ring, -1),
+    ]
+
+
+def third_wave(second, ring, half):
+    return [shift(second[0][:half], ring, 1), shift(second[1][half:], ring, -1)]
+
+
+def all_pieces(own, first, second, third):
+    return {
+        (0, 0): [(None, own)],
+        (3, 0): [(None, first[0])],
+        (1, 0): [(None, first[1])],
+        (0, 1): [(None, first[2])],
+        (3, 1): [(None, second[0])],
+        (1, 1): [(None, second[1])],
+        (2, 0): [(0, second[2]), (1, second[3])],
+        (2, 1): [(0, third[0]), (1, third[1])],
+    }
 
 
 def body(basis_values, potential, task_pairs, task_owner, task_slot, matrix_blocks, matrix_columns):
@@ -193,8 +209,41 @@
     cells = 2 * lax.axis_size(COL)
     own = matrix_blocks.reshape(2 * cell_rows, width, width)
 
-    rows = ring_and_pair(own, "z", "yh", cell_rows)
-    columns = ring_and_pair(own, "x", "yl", cell_rows)
+    row_first = first_wave(own, "z", "yh")
+    column_first = first_wave(own, "x", "yl")
+
+    owners, slots = task_owner.reshape(-1), task_slot.reshape(-1)
+    task_count = owners.shape[0]
+    order = jnp.arange(task_count, dtype=jnp.int32)
+    earlier = (owners[:, None] == owners[None, :]) & (order[None, :] < order[:, None])
+    places = owners * 2 + jnp.sum(earlier.astype(jnp.int32), axis=1)
+    spots = jnp.arange(2 * device_count, dtype=jnp.int32)
+    named = places[None, :] == spots[:, None]
+    send_slots = jnp.max(jnp.where(named, slots[None, :], -1), axis=1)
+    send = pair_blocks(basis_values[0, 0], potential[0], task_pairs[0, 0], places, 2 * device_count)
+
+    own_columns = matrix_columns.reshape(1, -1)
+    numbers = jnp.concatenate(
+        [
+            send_slots.reshape(device_count, 2),
+            jnp.broadcast_to(own_columns, (device_count, own_columns.shape[1])),
+        ],
+        axis=1,
+    )
+    numbers = lax.all_to_all(numbers[:, None, :], ALL, 0, 0, tiled=True)[:, 0, :]
+    row_first, column_first, send, numbers = lax.optimization_barrier(
+        (row_first, column_first, send, numbers)
+    )
+    row_second = second_wave(row_first, "z", cell_rows)
+    column_second = second_wave(column_first, "x", cell_rows)
+    row_second, column_second, send = lax.optimization_barrier((row_second, column_second, send))
+    row_third = third_wave(row_second, "z", cell_rows)
+    column_third = third_wave(column_second, "x", cell_rows)
+    arrived = lax.all_to_all(send, ALL, 0, 0, tiled=True)
+    fock = fock_sum(numbers[:, :2].reshape(-1), arrived, 2 * cell_rows)
+
+    rows = all_pieces(own, row_first, row_second, row_third)
+    columns = all_pieces(own, column_first, column_second, column_third)
     pieces = []
     for (ring, pair), values in rows.items():
         first = 2 * (((z + ring) % 4) * 2 + (yh + pair) % 2)
@@ -206,28 +255,6 @@
         for half, value in values:
             pieces.append((1, first + (half or 0), value))
             pieces.append((1, other + (half or 0), shift(value, "c", 1)))
-
-    owners, slots = task_owner.reshape(-1), task_slot.reshape(-1)
-    task_count = owners.shape[0]
-    order = jnp.arange(task_count, dtype=jnp.int32)
-    earlier = (owners[:, None] == owners[None, :]) & (order[None, :] < order[:, None])
-    places = owners * 2 + jnp.sum(earlier.astype(jnp.int32), axis=1)
-    spots = jnp.arange(2 * device_count, dtype=jnp.int32)
-    named = places[None, :] == spots[:, None]
-    send_slots = jnp.max(jnp.where(named, slots[None, :], -1), axis=1)
-    send = pair_blocks(basis_values[0, 0], potential[0], task_pairs[0, 0], places, 2 * device_count)
-
-    own_columns = matrix_columns.reshape(1, -1)
-    numbers = jnp.concatenate(
-        [
-            send_slots.reshape(device_count, 2),
-            jnp.broadcast_to(own_columns, (device_count, own_columns.shape[1])),
-        ],
-        axis=1,
-    )
-    numbers = lax.all_to_all(numbers[:, None, :], ALL, 0, 0, tiled=True)[:, 0, :]
-    arrived = lax.all_to_all(send, ALL, 0, 0, tiled=True)
-    fock = fock_sum(numbers[:, :2].reshape(-1), arrived, 2 * cell_rows)
 
     every = numbers[:, 2:].reshape(row_count, cells, cell_rows)
     me_row = (x * 2 + yl) * 2 + c

time: 286 us -> 273 us (0.955)
  waiting for transfers between devices: 165 us -> 152 us
  starting transfers between devices: 63.9 us -> 58 us
  local copies, waits for them, and re-layouts: 11.2 us -> 14.5 us
    ppermute x28, waiting for transfers between devices: 165 us -> 152 us  [shift(): lax.ppermute(value, axis, [(i, (i + step) % size) for i in range(size)])]
    ppermute x28, starting transfers between devices: 42.1 us -> 37.7 us  [shift(): lax.ppermute(value, axis, [(i, (i + step) % size) for i in range(size)])]
  transfers between devices with their start and end apart: 30 -> 30, of which waited for: 8 -> 8; matrix products, arithmetic and copies ran while one was open for 4% -> 7% of each run, Pallas kernels for 11% -> 11%
where the time goes in v2:
time: 273 us; the launch traced here: 270 us
  waiting for transfers between devices  152 us (56%)
  starting transfers between devices  58 us (21%)
  Pallas kernels  39.4 us (14%)
  local copies, waits for them, and re-layouts  14.5 us (5%)
  other arithmetic  4.36 us (2%)
    ppermute x28, waiting for transfers between devices, shift(): lax.ppermute(value, axis, [(i, (i + step) % size) for i in range(size)])  152 us
    ppermute x28, starting transfers between devices, shift(): lax.ppermute(value, axis, [(i, (i + step) % size) for i in range(size)])  37.7 us
    pallas_call x1, Pallas kernels, pair_blocks(): pl.pallas_call(pair_kernel, out_shape=jax.ShapeDtypeStruct((slot_count, w...  15.1 us
    pallas_call x1, Pallas kernels, square_sum(): pl.pallas_call(functools.partial(square_kernel, places, cell_rows), out_s...  15.1 us
    all_to_all x1, starting transfers between devices, body(): arrived = lax.all_to_all(send, ALL, 0, 0, tiled=True)  11.3 us
    pallas_call x1, Pallas kernels, fock_sum(): pl.pallas_call(fock_kernel, grid=(count // chunk,), out_shape=jax.ShapeDt...  9.2 us
    all_to_all x1, starting transfers between devices, body(): lax.all_to_all(numbers[:, None, :], ALL, 0, 0, tiled=True)[:, 0, :]  8.91 us
    slice x4, local copies, waits for them, and re-layouts, third_wave(): return [shift(second[0][:half], ring, 1), shift(second[1][half:], ring, -1)]  7.57 us
  transfers between devices with their start and end apart: 30, of which 8 were waited for; matrix products, arithmetic and copies ran while one was open for 7% of the time, Pallas kernels for 11%

profile of v2, /device:TPU:1, one launch (start us, length us, event | category | flops | bytes accessed | tf_op | source)
XLA Modules:
  0.0 269.5 jit_solution(4174815667805610814)
XLA Ops:
  0.6 2.5 collective-permute-start
  3.2 2.2 collective-permute-start.1
  5.4 2.9 %collective-permute-start.2 = (bf16[32,128,128]{2,1,0:T(8,128)(2,1)}, bf16[32,128,128]{2,1,0:T(8,128)(2,1)}, u32[]{:S(2)}, u32[]{:S(2)}) collective-permute-start(bf16[32,128,128]{2,1,0:T(8,128)(2,1)} %bitcast.52), channel_id=1, source_target_pairs={{0,1},{1,0},{2,3},{3,2},{4,5},{5,4},{6,7},{7,6},{8,9},{9,8},{10,11... | collective-permute-start | bytes 3145736 | tf_op jit(solution)/shard_map/ppermute | solution.py:20
  8.3 1.2 collective-permute-start.3
  9.5 1.5 collective-permute-start.4
  11.0 0.9 convert_reduce_fusion
  11.9 0.7 multiply_add_fusion.places
  12.5 16.0 %collective-permute-done.refs_1_ = bf16[32,128,128]{2,1,0:T(8,128)(2,1)S(1)} collective-permute-done((bf16[32,128,128]{2,1,0:T(8,128)(2,1)}, bf16[32,128,128]{2,1,0:T(8,128)(2,1)S(1)}, u32[]{:S(2)}, u32[]{:S(2)}) %collective-permute-start) | collective-permute-done | bytes 1048608 | tf_op jit(solution)/shard_map/ppermute | solution.py:20
  28.5 1.2 collective-permute-start.5
  29.7 0.8 select_reduce_fusion.1
  30.5 0.1 reshape.94
  30.6 0.8 reshape.100
  31.4 0.6 pad_add_fusion
  32.1 8.9 %all-to-all-start = ((s32[128,1,34]{2,1,0:T(1,128)}), s32[128,1,34]{2,1,0:T(1,128)S(1)}, u32[]{:S(2)}, u32[]{:S(2)}) async-start(s32[128,1,34]{2,1,0:T(1,128)} %bitcast.5), calls=%async_computation | async-start | bytes 131072 | tf_op jit(solution)/shard_map/all_to_all | solution.py:233
  41.0 0.8 copy.20
  41.8 0.7 reshape_squeeze.3.pairs
  42.5 15.1 %pair_blocks.1 = bf16[256,128,128]{2,1,0:T(8,128)(2,1)} custom-call(s32[256]{0:T(256)} %reshape_squeeze.3.pairs, s32[128]{0:T(128)} %copy-done.11, bf16[16,128,1024]{2,1,0:T(8,128)(2,1)} %bitcast.65, f32[1,1024]{1,0:T(1,128)} %bitcast.66), custom_call_target="tpu_custom_call" | custom-call | flops 8589934592 | bytes 8388608 | tf_op jit(solution)/shard_map/pair_blocks/pallas_call | solution.py:55
  57.8 1.6 collective-permute-start.8
  59.4 1.9 collective-permute-start.9
  61.3 1.3 collective-permute-start.12
  62.6 2.7 collective-permute-start.7
  65.2 7.5 %collective-permute-done.8.refs_6_ = bf16[16,128,128]{2,1,0:T(8,128)(2,1)S(1)} collective-permute-done((bf16[16,128,128]{2,1,0:T(8,128)(2,1)S(1)}, bf16[16,128,128]{2,1,0:T(8,128)(2,1)S(1)}, u32[]{:S(2)}, u32[]{:S(2)}) %collective-permute-start.8) | collective-permute-done | bytes 524320 | tf_op jit(solution)/shard_map/ppermute | solution.py:20
  72.7 1.6 collective-permute-start.10
  74.3 1.3 collective-permute-start.11
  75.7 1.1 slice.34
  76.8 1.5 collective-permute-start.13
  78.2 30.7 %collective-permute-done.13.refs_24_ = bf16[16,128,128]{2,1,0:T(8,128)(2,1)} collective-permute-done((bf16[16,128,128]{2,1,0:T(8,128)(2,1)S(1)}, bf16[16,128,128]{2,1,0:T(8,128)(2,1)}, u32[]{:S(2)}, u32[]{:S(2)}) %collective-permute-start.13) | collective-permute-done | bytes 524320 | tf_op jit(solution)/shard_map/ppermute | solution.py:20
  109.0 11.3 %all-to-all-start.1 = ((bf16[256,128,128]{2,1,0:T(8,128)(2,1)}), bf16[256,128,128]{2,1,0:T(8,128)(2,1)}, u32[]{:S(2)}, u32[]{:S(2)}) async-start(bf16[256,128,128]{2,1,0:T(8,128)(2,1)} %pair_blocks.1), calls=%async_computation.1 | async-start | bytes 16777216 | tf_op jit(solution)/shard_map/all_to_all | solution.py:242
  120.3 1.2 collective-permute-start.16
  121.5 0.1 collective-permute-start.17
  121.6 0.4 collective-permute-start.18
  122.0 0.1 collective-permute-start.19
  122.1 1.9 slice.36
  124.0 0.8 collective-permute-start.14
  124.8 1.9 slice.37
  126.7 1.9 collective-permute-start.15
  128.6 0.1 stack.123
  128.7 0.5 broadcast_multiply_fusion.where
  129.2 1.9 slice.38
  131.1 1.9 slice.39
  133.0 1.0 collective-permute-start.20
  134.0 0.1 collective-permute-start.21
  134.1 0.4 collective-permute-start.22
  134.5 89.6 %collective-permute-done.14.refs_8_ = bf16[16,128,128]{2,1,0:T(8,128)(2,1)} collective-permute-done((bf16[16,128,128]{2,1,0:T(8,128)(2,1)}, bf16[16,128,128]{2,1,0:T(8,128)(2,1)}, u32[]{:S(2)}, u32[]{:S(2)}) %collective-permute-start.14) | collective-permute-done | bytes 524320 | tf_op jit(solution)/shard_map/ppermute | solution.py:20
  224.1 1.8 collective-permute-start.24
  225.8 1.3 collective-permute-done.15.refs_9_
  227.1 2.6 collective-permute-start.26
  229.7 0.1 copy.23
  229.9 0.7 reshape.95.slots
  230.8 0.8 collective-permute-start.23
  231.6 6.6 %collective-permute-done.24.refs_26_ = bf16[16,128,128]{2,1,0:T(8,128)(2,1)} collective-permute-done((bf16[16,128,128]{2,1,0:T(8,128)(2,1)}, bf16[16,128,128]{2,1,0:T(8,128)(2,1)}, u32[]{:S(2)}, u32[]{:S(2)}) %collective-permute-start.24) | collective-permute-done | bytes 524320 | tf_op jit(solution)/shard_map/ppermute | solution.py:20
  238.3 2.0 collective-permute-start.25
  240.3 0.5 collective-permute-done.26.refs_28_
  240.8 1.3 collective-permute-start.27
  242.2 0.1 iota_compare_fusion
  242.3 0.6 select_reduce_fusion
  242.9 0.1 compare_select_fusion
  243.0 0.2 copy.25
  243.2 0.7 select_n.163.picks
  244.0 0.1 collective-permute-done.27.refs_29_
  244.0 0.9 copy-done.6
  244.9 0.3 copy-done.7
  245.2 15.1 %square_sum.1 = bf16[32,128,128]{2,1,0:T(8,128)(2,1)} custom-call(s32[30]{0:T(128)} %broadcast_multiply_fusion.where, s32[512]{0:T(512)} %select_n.163.picks, bf16[32,128,128]{2,1,0:T(8,128)(2,1)} %bitcast.56, bf16[32,128,128]{2,1,0:T(8,128)(2,1)} %copy-done.1, bf16[32,128,128]{2,1,0:T(8,128)(2,1)} %copy-done.2, ...), custom_call_target="tpu_custom_call" | custom-call | flops 2147483648 | bytes 25165824 | tf_op jit(solution)/shard_map/square_sum/pallas_call | solution.py:154
  260.3 9.2 %fock_sum.1 = bf16[32,128,128]{2,1,0:T(8,128)(2,1)} custom-call(s32[256]{0:T(256)} %reshape.95.slots, bf16[256,128,128]{2,1,0:T(8,128)(2,1)} %all-to-all-done.1.arrived), custom_call_target="tpu_custom_call" | custom-call | flops 4194304 | bytes 8388608 | tf_op jit(solution)/shard_map/fock_sum/pallas_call | solution.py:101
  (57 shorter events, 0.6 us)
Async XLA Ops:
  0.6 27.9 %collective-permute-start = (bf16[32,128,128]{2,1,0:T(8,128)(2,1)}, bf16[32,128,128]{2,1,0:T(8,128)(2,1)S(1)}, u32[]{:S(2)}, u32[]{:S(2)}) collective-permute-start(bf16[32,128,128]{2,1,0:T(8,128)(2,1)} %bitcast.50), channel_id=1, source_target_pairs={{0,2},{2,4},{4,6},{6,0},{1,3},{3,5},{5,7},{7,1},{8,10},{10,12},{12... | collective-permute-start | bytes 3145736 | tf_op jit(solution)/shard_map/ppermute | solution.py:20
  3.2 54.5 %collective-permute-start.1 = (bf16[32,128,128]{2,1,0:T(8,128)(2,1)}, bf16[32,128,128]{2,1,0:T(8,128)(2,1)S(1)}, u32[]{:S(2)}, u32[]{:S(2)}) collective-permute-start(bf16[32,128,128]{2,1,0:T(8,128)(2,1)} %bitcast.51), channel_id=1, source_target_pairs={{0,6},{2,0},{4,2},{6,4},{1,7},{3,1},{5,3},{7,5},{8,14},{10,8},{12,... | collective-permute-start | bytes 3145736 | tf_op jit(solution)/shard_map/ppermute | solution.py:20
  5.4 52.3 %collective-permute-start.2 = (bf16[32,128,128]{2,1,0:T(8,128)(2,1)}, bf16[32,128,128]{2,1,0:T(8,128)(2,1)}, u32[]{:S(2)}, u32[]{:S(2)}) collective-permute-start(bf16[32,128,128]{2,1,0:T(8,128)(2,1)} %bitcast.52), channel_id=1, source_target_pairs={{0,1},{1,0},{2,3},{3,2},{4,5},{5,4},{6,7},{7,6},{8,9},{9,8},{10,11... | collective-permute-start | bytes 3145736 | tf_op jit(solution)/shard_map/ppermute | solution.py:20
  8.3 49.4 %collective-permute-start.3 = (bf16[32,128,128]{2,1,0:T(8,128)(2,1)}, bf16[32,128,128]{2,1,0:T(8,128)(2,1)S(1)}, u32[]{:S(2)}, u32[]{:S(2)}) collective-permute-start(bf16[32,128,128]{2,1,0:T(8,128)(2,1)} %bitcast.53), channel_id=1, source_target_pairs={{0,32},{32,64},{64,96},{96,0},{1,33},{33,65},{65,97},{97,1},{2,34}... | collective-permute-start | bytes 3145736 | tf_op jit(solution)/shard_map/ppermute | solution.py:20
  9.5 48.2 %collective-permute-start.4 = (bf16[32,128,128]{2,1,0:T(8,128)(2,1)}, bf16[32,128,128]{2,1,0:T(8,128)(2,1)}, u32[]{:S(2)}, u32[]{:S(2)}) collective-permute-start(bf16[32,128,128]{2,1,0:T(8,128)(2,1)} %bitcast.54), channel_id=1, source_target_pairs={{0,96},{32,0},{64,32},{96,64},{1,97},{33,1},{65,33},{97,65},{2,98}... | collective-permute-start | bytes 3145736 | tf_op jit(solution)/shard_map/ppermute | solution.py:20
  12.5 29.9 %copy-start.11 = (s32[128]{0:T(128)}, s32[128]{0:T(128)S(1)}, u32[]{:S(2)}) copy-start(s32[128]{0:T(128)S(1)} %multiply_add_fusion.places) | copy-start | bytes 1540
  28.5 29.2 %copy-start.1 = (bf16[32,128,128]{2,1,0:T(8,128)(2,1)}, bf16[32,128,128]{2,1,0:T(8,128)(2,1)S(1)}, u32[]{:S(2)}) copy-start(bf16[32,128,128]{2,1,0:T(8,128)(2,1)S(1)} %collective-permute-done.refs_1_) | copy-start | bytes 3145732
  28.5 29.2 %collective-permute-start.5 = (bf16[32,128,128]{2,1,0:T(8,128)(2,1)}, bf16[32,128,128]{2,1,0:T(8,128)(2,1)}, u32[]{:S(2)}, u32[]{:S(2)}) collective-permute-start(bf16[32,128,128]{2,1,0:T(8,128)(2,1)} %bitcast.55), channel_id=1, source_target_pairs={{0,16},{16,0},{1,17},{17,1},{2,18},{18,2},{3,19},{19,3},{4,20},{20... | collective-permute-start | bytes 3145736 | tf_op jit(solution)/shard_map/ppermute | solution.py:20
  32.1 25.5 %all-to-all-start = ((s32[128,1,34]{2,1,0:T(1,128)}), s32[128,1,34]{2,1,0:T(1,128)S(1)}, u32[]{:S(2)}, u32[]{:S(2)}) async-start(s32[128,1,34]{2,1,0:T(1,128)} %bitcast.5), calls=%async_computation | async-start | bytes 131072 | tf_op jit(solution)/shard_map/all_to_all | solution.py:233
  57.6 51.3 %copy-start.2 = (bf16[32,128,128]{2,1,0:T(8,128)(2,1)}, bf16[32,128,128]{2,1,0:T(8,128)(2,1)S(1)}, u32[]{:S(2)}) copy-start(bf16[32,128,128]{2,1,0:T(8,128)(2,1)S(1)} %collective-permute-done.1.refs_2_) | copy-start | bytes 3145732
  57.7 18.0 %copy-start.3 = (bf16[32,128,128]{2,1,0:T(8,128)(2,1)}, bf16[32,128,128]{2,1,0:T(8,128)(2,1)S(1)}, u32[]{:S(2)}) copy-start(bf16[32,128,128]{2,1,0:T(8,128)(2,1)S(1)} %collective-permute-done.3.refs_12_) | copy-start | bytes 3145732
  57.8 15.0 %collective-permute-start.8 = (bf16[16,128,128]{2,1,0:T(8,128)(2,1)S(1)}, bf16[16,128,128]{2,1,0:T(8,128)(2,1)S(1)}, u32[]{:S(2)}, u32[]{:S(2)}) collective-permute-start(bf16[16,128,128]{2,1,0:T(8,128)(2,1)S(1)} %slice.31), channel_id=1, source_target_pairs={{0,2},{2,4},{4,6},{6,0},{1,3},{3,5},{5,7},{7,1},{8,10},{10,12},{12... | collective-permute-start | bytes 1572872 | tf_op jit(solution)/shard_map/ppermute | solution.py:20
  59.4 15.0 %collective-permute-start.9 = (bf16[16,128,128]{2,1,0:T(8,128)(2,1)S(1)}, bf16[16,128,128]{2,1,0:T(8,128)(2,1)S(1)}, u32[]{:S(2)}, u32[]{:S(2)}) collective-permute-start(bf16[16,128,128]{2,1,0:T(8,128)(2,1)S(1)} %slice.32), channel_id=1, source_target_pairs={{0,6},{2,0},{4,2},{6,4},{1,7},{3,1},{5,3},{7,5},{8,14},{10,8},{12,... | collective-permute-start | bytes 1572872 | tf_op jit(solution)/shard_map/ppermute | solution.py:20
  61.2 47.7 %collective-permute-start.6 = (bf16[32,128,128]{2,1,0:T(8,128)(2,1)}, bf16[32,128,128]{2,1,0:T(8,128)(2,1)}, u32[]{:S(2)}, u32[]{:S(2)}) collective-permute-start(bf16[32,128,128]{2,1,0:T(8,128)(2,1)} %collective-permute-done.2.refs_3_), channel_id=1, source_target_pairs={{0,2},{2,4},{4,6},{6,0},{1,3},{3,5},{5,7},{7,1},{8,10},{10,12},{12... | collective-permute-start | bytes 3145736 | tf_op jit(solution)/shard_map/ppermute | solution.py:20
  61.3 15.5 %collective-permute-start.12 = (bf16[16,128,128]{2,1,0:T(8,128)(2,1)S(1)}, bf16[16,128,128]{2,1,0:T(8,128)(2,1)}, u32[]{:S(2)}, u32[]{:S(2)}) collective-permute-start(bf16[16,128,128]{2,1,0:T(8,128)(2,1)S(1)} %slice.33), channel_id=1, source_target_pairs={{0,32},{32,64},{64,96},{96,0},{1,33},{33,65},{65,97},{97,1},{2,34}... | collective-permute-start | bytes 1572872 | tf_op jit(solution)/shard_map/ppermute | solution.py:20
  62.6 46.4 %collective-permute-start.7 = (bf16[32,128,128]{2,1,0:T(8,128)(2,1)}, bf16[32,128,128]{2,1,0:T(8,128)(2,1)}, u32[]{:S(2)}, u32[]{:S(2)}) collective-permute-start(bf16[32,128,128]{2,1,0:T(8,128)(2,1)} %collective-permute-done.2.refs_3_), channel_id=1, source_target_pairs={{0,6},{2,0},{4,2},{6,4},{1,7},{3,1},{5,3},{7,5},{8,14},{10,8},{12,... | collective-permute-start | bytes 3145736 | tf_op jit(solution)/shard_map/ppermute | solution.py:20
  72.7 2.9 %copy-start.8 = (bf16[16,128,128]{2,1,0:T(8,128)(2,1)}, bf16[16,128,128]{2,1,0:T(8,128)(2,1)S(1)}, u32[]{:S(2)}) copy-start(bf16[16,128,128]{2,1,0:T(8,128)(2,1)S(1)} %collective-permute-done.8.refs_6_) | copy-start | bytes 1572868
  72.7 36.2 %collective-permute-start.10 = (bf16[32,128,128]{2,1,0:T(8,128)(2,1)}, bf16[32,128,128]{2,1,0:T(8,128)(2,1)}, u32[]{:S(2)}, u32[]{:S(2)}) collective-permute-start(bf16[32,128,128]{2,1,0:T(8,128)(2,1)} %collective-permute-done.5.refs_16_), channel_id=1, source_target_pairs={{0,32},{32,64},{64,96},{96,0},{1,33},{33,65},{65,97},{97,1},{2,34}... | collective-permute-start | bytes 3145736 | tf_op jit(solution)/shard_map/ppermute | solution.py:20
  74.3 1.3 copy-start.9
  74.3 34.6 %collective-permute-start.11 = (bf16[32,128,128]{2,1,0:T(8,128)(2,1)}, bf16[32,128,128]{2,1,0:T(8,128)(2,1)}, u32[]{:S(2)}, u32[]{:S(2)}) collective-permute-start(bf16[32,128,128]{2,1,0:T(8,128)(2,1)} %collective-permute-done.5.refs_16_), channel_id=1, source_target_pairs={{0,96},{32,0},{64,32},{96,64},{1,97},{33,1},{65,33},{97,65},{2,98}... | collective-permute-start | bytes 3145736 | tf_op jit(solution)/shard_map/ppermute | solution.py:20
  76.7 43.5 %copy-start = (bf16[1,2,16,128,128]{4,3,2,1,0:T(8,128)(2,1)S(1)}, bf16[1,2,16,128,128]{4,3,2,1,0:T(8,128)(2,1)}, u32[]{:S(2)}) copy-start(bf16[1,2,16,128,128]{4,3,2,1,0:T(8,128)(2,1)} %param.12) | copy-start | bytes 3145732
  76.8 44.8 %copy-start.4 = (bf16[32,128,128]{2,1,0:T(8,128)(2,1)S(1)}, bf16[32,128,128]{2,1,0:T(8,128)(2,1)}, u32[]{:S(2)}) copy-start(bf16[32,128,128]{2,1,0:T(8,128)(2,1)} %copy-done.3) | copy-start | bytes 3145732
  76.8 152.9 %copy-start.10 = (s32[1,2,16]{2,1,0:T(2,128)S(1)}, s32[1,2,16]{2,1,0:T(2,128)}, u32[]{:S(2)}) copy-start(s32[1,2,16]{2,1,0:T(2,128)} %param.13) | copy-start | bytes 388
  76.8 32.2 %collective-permute-start.13 = (bf16[16,128,128]{2,1,0:T(8,128)(2,1)S(1)}, bf16[16,128,128]{2,1,0:T(8,128)(2,1)}, u32[]{:S(2)}, u32[]{:S(2)}) collective-permute-start(bf16[16,128,128]{2,1,0:T(8,128)(2,1)S(1)} %slice.34), channel_id=1, source_target_pairs={{0,96},{32,0},{64,32},{96,64},{1,97},{33,1},{65,33},{97,65},{2,98}... | collective-permute-start | bytes 1572872 | tf_op jit(solution)/shard_map/ppermute | solution.py:20
  109.0 151.4 %all-to-all-start.1 = ((bf16[256,128,128]{2,1,0:T(8,128)(2,1)}), bf16[256,128,128]{2,1,0:T(8,128)(2,1)}, u32[]{:S(2)}, u32[]{:S(2)}) async-start(bf16[256,128,128]{2,1,0:T(8,128)(2,1)} %pair_blocks.1), calls=%async_computation.1 | async-start | bytes 16777216 | tf_op jit(solution)/shard_map/all_to_all | solution.py:242
  120.3 6.4 %collective-permute-start.16 = (bf16[32,128,128]{2,1,0:T(8,128)(2,1)S(1)}, bf16[32,128,128]{2,1,0:T(8,128)(2,1)S(1)}, u32[]{:S(2)}, u32[]{:S(2)}) collective-permute-start(bf16[32,128,128]{2,1,0:T(8,128)(2,1)S(1)} %bitcast.58), channel_id=1, source_target_pairs={{0,8},{8,0},{1,9},{9,1},{2,10},{10,2},{3,11},{11,3},{4,12},{12,4},... | collective-permute-start | bytes 3145736 | tf_op jit(solution)/shard_map/ppermute | solution.py:20
  121.5 11.5 %collective-permute-start.17 = (bf16[32,128,128]{2,1,0:T(8,128)(2,1)S(1)}, bf16[32,128,128]{2,1,0:T(8,128)(2,1)}, u32[]{:S(2)}, u32[]{:S(2)}) collective-permute-start(bf16[32,128,128]{2,1,0:T(8,128)(2,1)S(1)} %copy-done.4), channel_id=1, source_target_pairs={{0,8},{8,0},{1,9},{9,1},{2,10},{10,2},{3,11},{11,3},{4,12},{12,4},... | collective-permute-start | bytes 3145736 | tf_op jit(solution)/shard_map/ppermute | solution.py:20
  121.6 12.4 %collective-permute-start.18 = (bf16[32,128,128]{2,1,0:T(8,128)(2,1)}, bf16[32,128,128]{2,1,0:T(8,128)(2,1)}, u32[]{:S(2)}, u32[]{:S(2)}) collective-permute-start(bf16[32,128,128]{2,1,0:T(8,128)(2,1)} %collective-permute-done.4.refs_14_), channel_id=1, source_target_pairs={{0,8},{8,0},{1,9},{9,1},{2,10},{10,2},{3,11},{11,3},{4,12},{12,4},... | collective-permute-start | bytes 3145736 | tf_op jit(solution)/shard_map/ppermute | solution.py:20
  122.0 12.1 %collective-permute-start.19 = (bf16[32,128,128]{2,1,0:T(8,128)(2,1)}, bf16[32,128,128]{2,1,0:T(8,128)(2,1)}, u32[]{:S(2)}, u32[]{:S(2)}) collective-permute-start(bf16[32,128,128]{2,1,0:T(8,128)(2,1)} %collective-permute-done.5.refs_16_), channel_id=1, source_target_pairs={{0,8},{8,0},{1,9},{9,1},{2,10},{10,2},{3,11},{11,3},{4,12},{12,4},... | collective-permute-start | bytes 3145736 | tf_op jit(solution)/shard_map/ppermute | solution.py:20
  124.0 100.1 %collective-permute-start.14 = (bf16[16,128,128]{2,1,0:T(8,128)(2,1)}, bf16[16,128,128]{2,1,0:T(8,128)(2,1)}, u32[]{:S(2)}, u32[]{:S(2)}) collective-permute-start(bf16[16,128,128]{2,1,0:T(8,128)(2,1)} %slice.36), channel_id=1, source_target_pairs={{0,2},{2,4},{4,6},{6,0},{1,3},{3,5},{5,7},{7,1},{8,10},{10,12},{12... | collective-permute-start | bytes 1572872 | tf_op jit(solution)/shard_map/ppermute | solution.py:20
  126.7 117.4 %copy-start.5 = (bf16[32,128,128]{2,1,0:T(8,128)(2,1)}, bf16[32,128,128]{2,1,0:T(8,128)(2,1)S(1)}, u32[]{:S(2)}) copy-start(bf16[32,128,128]{2,1,0:T(8,128)(2,1)S(1)} %collective-permute-done.16.refs_11_) | copy-start | bytes 3145732
  126.7 100.5 %collective-permute-start.15 = (bf16[16,128,128]{2,1,0:T(8,128)(2,1)}, bf16[16,128,128]{2,1,0:T(8,128)(2,1)}, u32[]{:S(2)}, u32[]{:S(2)}) collective-permute-start(bf16[16,128,128]{2,1,0:T(8,128)(2,1)} %slice.37), channel_id=1, source_target_pairs={{0,6},{2,0},{4,2},{6,4},{1,7},{3,1},{5,3},{7,5},{8,14},{10,8},{12,... | collective-permute-start | bytes 1572872 | tf_op jit(solution)/shard_map/ppermute | solution.py:20
  133.0 110.9 %collective-permute-start.20 = (bf16[32,128,128]{2,1,0:T(8,128)(2,1)}, bf16[32,128,128]{2,1,0:T(8,128)(2,1)S(1)}, u32[]{:S(2)}, u32[]{:S(2)}) collective-permute-start(bf16[32,128,128]{2,1,0:T(8,128)(2,1)} %collective-permute-done.10.refs_18_), channel_id=1, source_target_pairs={{0,8},{8,0},{1,9},{9,1},{2,10},{10,2},{3,11},{11,3},{4,12},{12,4},... | collective-permute-start | bytes 3145736 | tf_op jit(solution)/shard_map/ppermute | solution.py:20
  134.0 109.9 %collective-permute-start.21 = (bf16[32,128,128]{2,1,0:T(8,128)(2,1)}, bf16[32,128,128]{2,1,0:T(8,128)(2,1)S(1)}, u32[]{:S(2)}, u32[]{:S(2)}) collective-permute-start(bf16[32,128,128]{2,1,0:T(8,128)(2,1)} %collective-permute-done.11.refs_20_), channel_id=1, source_target_pairs={{0,8},{8,0},{1,9},{9,1},{2,10},{10,2},{3,11},{11,3},{4,12},{12,4},... | collective-permute-start | bytes 3145736 | tf_op jit(solution)/shard_map/ppermute | solution.py:20
  134.1 96.7 %collective-permute-start.22 = (bf16[16,128,128]{2,1,0:T(8,128)(2,1)}, bf16[16,128,128]{2,1,0:T(8,128)(2,1)}, u32[]{:S(2)}, u32[]{:S(2)}) collective-permute-start(bf16[16,128,128]{2,1,0:T(8,128)(2,1)} %collective-permute-done.12.refs_22_), channel_id=1, source_target_pairs={{0,8},{8,0},{1,9},{9,1},{2,10},{10,2},{3,11},{11,3},{4,12},{12,4},... | collective-permute-start | bytes 1572872 | tf_op jit(solution)/shard_map/ppermute | solution.py:20
  224.1 14.2 %collective-permute-start.24 = (bf16[16,128,128]{2,1,0:T(8,128)(2,1)}, bf16[16,128,128]{2,1,0:T(8,128)(2,1)}, u32[]{:S(2)}, u32[]{:S(2)}) collective-permute-start(bf16[16,128,128]{2,1,0:T(8,128)(2,1)} %slice.38), channel_id=1, source_target_pairs={{0,32},{32,64},{64,96},{96,0},{1,33},{33,65},{65,97},{97,1},{2,34}... | collective-permute-start | bytes 1572872 | tf_op jit(solution)/shard_map/ppermute | solution.py:20
  227.1 13.7 %collective-permute-start.26 = (bf16[16,128,128]{2,1,0:T(8,128)(2,1)}, bf16[16,128,128]{2,1,0:T(8,128)(2,1)}, u32[]{:S(2)}, u32[]{:S(2)}) collective-permute-start(bf16[16,128,128]{2,1,0:T(8,128)(2,1)} %slice.39), channel_id=1, source_target_pairs={{0,96},{32,0},{64,32},{96,64},{1,97},{33,1},{65,33},{97,65},{2,98}... | collective-permute-start | bytes 1572872 | tf_op jit(solution)/shard_map/ppermute | solution.py:20
  230.8 13.1 %collective-permute-start.23 = (bf16[16,128,128]{2,1,0:T(8,128)(2,1)}, bf16[16,128,128]{2,1,0:T(8,128)(2,1)}, u32[]{:S(2)}, u32[]{:S(2)}) collective-permute-start(bf16[16,128,128]{2,1,0:T(8,128)(2,1)} %collective-permute-done.13.refs_24_), channel_id=1, source_target_pairs={{0,8},{8,0},{1,9},{9,1},{2,10},{10,2},{3,11},{11,3},{4,12},{12,4},... | collective-permute-start | bytes 1572872 | tf_op jit(solution)/shard_map/ppermute | solution.py:20
  238.3 5.7 %collective-permute-start.25 = (bf16[16,128,128]{2,1,0:T(8,128)(2,1)}, bf16[16,128,128]{2,1,0:T(8,128)(2,1)}, u32[]{:S(2)}, u32[]{:S(2)}) collective-permute-start(bf16[16,128,128]{2,1,0:T(8,128)(2,1)} %collective-permute-done.24.refs_26_), channel_id=1, source_target_pairs={{0,8},{8,0},{1,9},{9,1},{2,10},{10,2},{3,11},{11,3},{4,12},{12,4},... | collective-permute-start | bytes 1572872 | tf_op jit(solution)/shard_map/ppermute | solution.py:20
  240.8 3.2 %collective-permute-start.27 = (bf16[16,128,128]{2,1,0:T(8,128)(2,1)}, bf16[16,128,128]{2,1,0:T(8,128)(2,1)}, u32[]{:S(2)}, u32[]{:S(2)}) collective-permute-start(bf16[16,128,128]{2,1,0:T(8,128)(2,1)} %collective-permute-done.26.refs_28_), channel_id=1, source_target_pairs={{0,8},{8,0},{1,9},{9,1},{2,10},{10,2},{3,11},{11,3},{4,12},{12,4},... | collective-permute-start | bytes 1572872 | tf_op jit(solution)/shard_map/ppermute | solution.py:20
  243.9 1.0 copy-start.6
  243.9 1.3 copy-start.7

commit v3 on v1

v3 whole, which is shorter than its diff:
```python
import functools

import jax
import jax.numpy as jnp
from jax import lax
from jax.experimental import pallas as pl
from jax.experimental.pallas import tpu as pltpu
from jax.sharding import Mesh
from jax.sharding import PartitionSpec as P

ROW = ("x", "yl", "c")
COL = ("z", "yh")
ALL = ROW + COL
F32 = jnp.float32
BF16 = jnp.bfloat16


def shift(value, axis, step):
    size = lax.axis_size(axis)
    return lax.ppermute(value, axis, [(i, (i + step) % size) for i in range(size)])


def pair_kernel(pairs, owners, ranks, basis, potential, send0, send1, weighted, table, sem):
    local_count, width, points = basis.shape
    task_count = owners.shape[0]
    for a in range(local_count):
        weighted[a] = (basis[a].astype(F32) * potential[...]).astype(BF16)

    def columns(step, carry):
        left = weighted[...].reshape(local_count * width, points)
        right = basis[pl.ds(2 * step, 2)].reshape(2 * width, points)
        product = lax.dot_general(left, right, (((1,), (1,)), ((), ())), preferred_element_type=F32)
        product = product.astype(BF16).reshape(local_count, width, 2 * width)
        table[2 * step] = product[:, :, :width]
        table[2 * step + 1] = product[:, :, width:]
        return carry

    lax.fori_loop(0, local_count // 2, columns, 0)

    def start(t, carry):
        block = table.at[pairs[2 * t + 1], pairs[2 * t]]

        @pl.when(ranks[t] == 0)
        def _():
            pltpu.make_async_copy(block, send0.at[owners[t]], sem).start()

        @pl.when(ranks[t] != 0)
        def _():
            pltpu.make_async_copy(block, send1.at[owners[t]], sem).start()

        return carry

    lax.fori_loop(0, task_count, start, 0)
    whole = send0.at[pl.ds(0, task_count)]
    pltpu.make_async_copy(whole, whole, sem).wait()


def pair_blocks(basis, potential, pairs, owners, ranks, device_count):
    local_count, width, points = basis.shape
    task_count = owners.shape[0]
    smem = pl.BlockSpec(memory_space=pltpu.SMEM)
    vmem = pl.BlockSpec(memory_space=pltpu.VMEM)
    return pl.pallas_call(
        pair_kernel,
        out_shape=[jax.ShapeDtypeStruct((device_count, width, width), BF16)] * 2,
        in_specs=[smem, smem, smem, vmem, vmem],
        out_specs=[pl.BlockSpec(memory_space=pl.ANY)] * 2,
        scratch_shapes=[
            pltpu.VMEM((local_count, width, points), BF16),
            pltpu.VMEM((local_count, local_count, width, width), BF16),
            pltpu.SemaphoreType.DMA,
        ],
        cost_estimate=pl.CostEstimate(
            flops=2 * (local_count * width) ** 2 * points,
            transcendentals=0,
            bytes_accessed=2 * basis.size + 2 * task_count * width * width,
        ),
        name="pair_blocks",
    )(pairs.reshape(-1), owners, ranks, basis, potential)


def fock_kernel(order, starts, *refs):
    *before, arrived, out = refs

    def one_slot(slot, carry):
        if before:
            total = before[0][slot]
        else:
            total = jnp.zeros(out.shape[1:], F32)

        def add(p, total):
            return total + arrived[order[p]].astype(F32)

        total = lax.fori_loop(starts[slot], starts[slot + 1], add, total)
        out[slot] = total.astype(out.dtype)
        return carry

    lax.fori_loop(0, out.shape[0], one_slot, 0)


def fock_sum(slots, before, arrived, slot_count, kind):
    count, width, _ = arrived.shape
    number = jnp.arange(count, dtype=jnp.int32)
    valid = slots >= 0
    same = slots[None, :] == slots[:, None]
    ahead = (slots[None, :] < slots[:, None]) | (same & (number[None, :] < number[:, None]))
    spot = jnp.sum((ahead & valid[None, :]).astype(jnp.int32), axis=1)
    hit = (spot[None, :] == number[:, None]) & valid[None, :]
    order = jnp.sum(jnp.where(hit, number[None, :], 0), axis=1)
    bounds = jnp.arange(slot_count + 1, dtype=jnp.int32)
    starts = jnp.sum((valid & (slots < bounds[:, None])).astype(jnp.int32), axis=1)
    smem = pl.BlockSpec(memory_space=pltpu.SMEM)
    vmem = pl.BlockSpec(memory_space=pltpu.VMEM)
    return pl.pallas_call(
        fock_kernel,
        out_shape=jax.ShapeDtypeStruct((slot_count, width, width), kind),
        in_specs=[smem, smem] + [vmem] * (len(before) + 1),
        out_specs=vmem,
        cost_estimate=pl.CostEstimate(
            flops=arrived.size, transcendentals=0, bytes_accessed=2 * arrived.size
        ),
        name="fock_sum",
    )(order, starts, *before, arrived)


def square_kernel(places, cell_rows, where, picks, *refs):
    *pieces, out, left, right, sems = refs
    cells = left.shape[0] // cell_rows
    width = left.shape[-1]
    zero = right.shape[0] - 1
    copies = []
    for n, (piece, side, start, count) in enumerate(places):
        source = pieces[piece].at[pl.ds(start * cell_rows, count * cell_rows)]
        first = pl.multiple_of(where[n], cell_rows)
        target = (left if side == 0 else right).at[pl.ds(first, count * cell_rows)]
        copies.append(pltpu.make_async_copy(source, target, sems.at[n]))
    for copy in copies:
        copy.start()
    right[zero] = jnp.zeros((width, width), BF16)
    for copy in copies:
        copy.wait()

    def block_row(q, carry):
        total = jnp.zeros((width, 2 * width), F32)
        for k in range(0, cells, 2):
            a = jnp.concatenate([left[k * cell_rows + q], left[(k + 1) * cell_rows + q]], axis=1)
            b = [[right[picks[(q * cells + k + h) * 2 + j]] for j in range(2)] for h in range(2)]
            b = jnp.concatenate([jnp.concatenate(b[h], axis=1) for h in range(2)], axis=0)
            total += jnp.dot(a, b, preferred_element_type=F32)
        out[q] = total[:, :width].astype(BF16)
        out[cell_rows + q] = total[:, width:].astype(BF16)
        return carry

    lax.fori_loop(0, cell_rows, block_row, 0)


def square_sum(picks, parts, cells, cell_rows, width):
    pieces = []
    places = []
    for side, value, start, count, first in parts:
        if not any(value is piece for piece in pieces):
            pieces.append(value)
        index = [value is piece for piece in pieces].index(True)
        places.append((index, side, start, count))
    where = jnp.stack([part[4] for part in parts]).astype(jnp.int32) * cell_rows
    smem = pl.BlockSpec(memory_space=pltpu.SMEM)
    return pl.pallas_call(
        functools.partial(square_kernel, tuple(places), cell_rows),
        out_shape=jax.ShapeDtypeStruct((2 * cell_rows, width, width), BF16),
        in_specs=[smem, smem] + [pl.BlockSpec(memory_space=pl.ANY)] * len(pieces),
        out_specs=pl.BlockSpec(memory_space=pltpu.VMEM),
        scratch_shapes=[
            pltpu.VMEM((cells * cell_rows, width, width), BF16),
            pltpu.VMEM((cells * 2 * cell_rows + 1, width, width), BF16),
            pltpu.SemaphoreType.DMA((len(places),)),
        ],
        cost_estimate=pl.CostEstimate(
            flops=4 * cells * cell_rows * width**3,
            transcendentals=0,
            bytes_accessed=2 * 3 * cells * cell_rows * width * width,
        ),
        name="square_sum",
    )(where, picks, *pieces)


def body(basis_values, potential, task_pairs, task_owner, task_slot, matrix_blocks, matrix_columns):
    x, yl, c, z, yh = (lax.axis_index(axis) for axis in ALL)
    cell_rows, width = matrix_blocks.shape[2], matrix_blocks.shape[3]
    row_count = lax.axis_size(ROW)
    device_count = row_count * lax.axis_size(COL)
    cells = 2 * lax.axis_size(COL)
    half = cell_rows
    own = matrix_blocks.reshape(2 * cell_rows, width, width)

    x_behind, x_ahead = shift(own, "x", 1), shift(own, "x", -1)
    z_behind, z_ahead = shift(own, "z", 1), shift(own, "z", -1)
    y_low = shift(own, "yl", 1)
    y_both = lax.all_to_all(jnp.concatenate([own, own]), "yh", 0, 0, tiled=True)

    x_behind, x_ahead, z_behind, z_ahead, y_low, y_both, basis = lax.optimization_barrier(
        (x_behind, x_ahead, z_behind, z_ahead, y_low, y_both, basis_values)
    )
    y_high = lax.dynamic_slice_in_dim(y_both, (1 - yh) * 2 * cell_rows, 2 * cell_rows, 0)
    x_behind2, x_ahead2 = shift(y_low, "x", 1), shift(y_low, "x", -1)
    z_behind2, z_ahead2 = shift(y_high, "z", 1), shift(y_high, "z", -1)

    owners, slots = task_owner.reshape(-1), task_slot.reshape(-1)
    task_count = owners.shape[0]
    number = jnp.arange(task_count, dtype=jnp.int32)
    earlier = (owners[:, None] == owners[None, :]) & (number[None, :] < number[:, None])
    ranks = jnp.sum(earlier.astype(jnp.int32), axis=1)
    send0, send1 = pair_blocks(
        basis[0, 0], potential[0], task_pairs[0, 0], owners, ranks, device_count
    )
    spots = jnp.arange(device_count, dtype=jnp.int32)
    named = owners[None, :] == spots[:, None]
    send_slots = [
        jnp.max(jnp.where(named & (ranks == rank)[None, :], slots[None, :], -1), axis=1)
        for rank in range(2)
    ]
    own_columns = matrix_columns.reshape(1, -1)
    numbers = jnp.concatenate(
        [
            send_slots[0][:, None],
            send_slots[1][:, None],
            jnp.broadcast_to(own_columns, (device_count, own_columns.shape[1])),
        ],
        axis=1,
    )

    x_behind2, x_ahead2, z_behind2, z_ahead2, own2, x_behind, x_ahead, y_low, send0 = (
        lax.optimization_barrier(
            (x_behind2, x_ahead2, z_behind2, z_ahead2, own, x_behind, x_ahead, y_low, send0)
        )
    )
    arrived0 = lax.all_to_all(send0, ALL, 0, 0, tiled=True)
    x_far0 = shift(jnp.concatenate([x_behind[:half], x_behind2[:half]]), "x", 1)
    x_far1 = shift(jnp.concatenate([x_ahead[half:], x_ahead2[half:]]), "x", -1)
    z_far0 = shift(jnp.concatenate([z_behind[:half], z_behind2[:half]]), "z", 1)
    z_far1 = shift(jnp.concatenate([z_ahead[half:], z_ahead2[half:]]), "z", -1)

    arrived0, numbers = lax.optimization_barrier((arrived0, numbers))
    numbers = lax.all_to_all(numbers[:, None, :], ALL, 0, 0, tiled=True)[:, 0, :]
    x_far0, x_far1, z_far0, z_far1, numbers, send1 = lax.optimization_barrier(
        (x_far0, x_far1, z_far0, z_far1, numbers, send1)
    )
    arrived1 = lax.all_to_all(send1, ALL, 0, 0, tiled=True)

    parts = []

    def left(value, start, count, ring, pair, cell):
        first = 2 * (((z + ring) % 4) * 2 + (yh + pair) % 2) + cell
        parts.append((0, value, start, count, first))

    def right(value, *pieces):
        other = shift(value, "c", 1)
        for start, count, ring, pair, cell in pieces:
            base = 2 * (((x + ring) % 4) * 2 + (yl + pair) % 2)
            parts.append((1, value, start, count, 2 * (base // 2 * 2 + c) + cell))
            parts.append((1, other, start, count, 2 * (base // 2 * 2 + 1 - c) + cell))

    left(own, 0, 2, 0, 0, 0)
    left(z_behind, 0, 2, 3, 0, 0)
    left(z_ahead, 0, 2, 1, 0, 0)
    left(y_high, 0, 2, 0, 1, 0)
    left(z_behind2, 0, 2, 3, 1, 0)
    left(z_ahead2, 0, 2, 1, 1, 0)
    for pair in range(2):
        left(z_far0, pair, 1, 2, pair, 0)
        left(z_far1, pair, 1, 2, pair, 1)
    right(own2, (0, 2, 0, 0, 0))
    right(x_behind, (0, 2, 3, 0, 0))
    right(x_ahead, (0, 2, 1, 0, 0))
    right(y_low, (0, 2, 0, 1, 0))
    right(x_behind2, (0, 2, 3, 1, 0))
    right(x_ahead2, (0, 2, 1, 1, 0))
    right(x_far0, (0, 1, 2, 0, 0), (1, 1, 2, 1, 0))
    right(x_far1, (0, 1, 2, 0, 1), (1, 1, 2, 1, 1))

    every = numbers[:, 2:].reshape(row_count, cells, cell_rows)
    me_row = (x * 2 + yl) * 2 + c
    me_col = z * 2 + yh
    left_columns = lax.dynamic_index_in_dim(every, me_row, 0, keepdims=False)
    right_columns = lax.dynamic_slice_in_dim(every, 2 * me_col, 2, 1)
    target = matrix_columns.reshape(2, cell_rows)
    slot_range = jnp.arange(cell_rows, dtype=jnp.int32)
    cell_range = jnp.arange(cells, dtype=jnp.int32)
    chosen = left_columns.T[:, :, None, None] == slot_range
    found = jnp.sum(jnp.where(chosen, right_columns[None], 0), axis=-1)
    spot = (cell_range[None, :, None] * 2 + jnp.arange(2, dtype=jnp.int32)) * cell_rows
    spot = spot + left_columns.T[:, :, None]
    picks = jnp.where(found == target.T[:, None, :], spot, cells * 2 * cell_rows)
    square = square_sum(picks.reshape(-1), parts, cells, cell_rows, width)

    partial = fock_sum(numbers[:, 0], [], arrived0, 2 * cell_rows, F32)
    fock = fock_sum(numbers[:, 1], [partial], arrived1, 2 * cell_rows, BF16)
    shape = (1, 2, cell_rows, width, width)
    return fock.reshape(shape), square.reshape(shape)


def solution(mesh):
    finer = Mesh(mesh.devices.reshape(4, 2, 2, 4, 2), ALL)
    return jax.shard_map(
        body,
        mesh=finer,
        in_specs=(
            P(ROW, COL, None, None, None),
            P(ROW, COL, None),
            P(ROW, COL, None, None),
            P(ROW, COL, None, None),
            P(ROW, COL, None),
            P(ROW, COL, None, None, None),
            P(ROW, COL, None),
        ),
        out_specs=(P(ROW, COL, None, None, None), P(ROW, COL, None, None, None)),
        check_vma=False,
    )
```

time: 286 us -> 228 us (0.80)
  waiting for transfers between devices: 165 us -> 115 us
  starting transfers between devices: 63.9 us -> 46.3 us
  other arithmetic: 4.34 us -> 12.1 us
    ppermute x28 -> x21, waiting for transfers between devices: 165 us -> 40.7 us  [shift(): lax.ppermute(value, axis, [(i, (i + step) % size) for i in range(size)])]
    all_to_all x1 -> x3, waiting for transfers between devices: 0.01 us -> 70 us  [the longest x1 34.5 us: body(): arrived0 = lax.all_to_all(send0, ALL, 0, 0, tiled=True)]
    ppermute x28 -> x21, starting transfers between devices: 42.1 us -> 23.6 us  [shift(): lax.ppermute(value, axis, [(i, (i + step) % size) for i in range(size)])]
    concatenate x1 -> x6, other arithmetic: 0.64 us -> 7.52 us  [the longest x1 3.06 us: body(): y_both = lax.all_to_all(jnp.concatenate([own, own]), 'yh', 0, 0, tiled=True)]
    all_to_all x1 -> x3, starting transfers between devices: 10.2 us -> 16.8 us  [the longest x1 7.57 us: body(): arrived0 = lax.all_to_all(send0, ALL, 0, 0, tiled=True)]
    all_to_all x1, starting transfers between devices: 11.5 us -> 6.01 us  [body(): lax.all_to_all(numbers[:, None, :], ALL, 0, 0, tiled=True)[:, 0, :]]
    all_to_all x1, waiting for transfers between devices: 0.01 us -> 4.65 us  [body(): lax.all_to_all(numbers[:, None, :], ALL, 0, 0, tiled=True)[:, 0, :]]
    pallas_call x3 -> x4, Pallas kernels: 39.6 us -> 40.3 us  [the longest x1 15.8 us: pair_blocks(): pl.pallas_call(pair_kernel, out_shape=[jax.ShapeDtypeStruct((device_count...]
  transfers between devices with their start and end apart: 30 -> 25, of which waited for: 8 -> 16; matrix products, arithmetic and copies ran while one was open for 4% -> 10% of each run, Pallas kernels for 11% -> 16%
where the time goes in v3:
time: 228 us; the launch traced here: 226 us
  waiting for transfers between devices  115 us (50%)
  starting transfers between devices  46.3 us (20%)
  Pallas kernels  40.3 us (18%)
  other arithmetic  12.1 us (5%)
  local copies, waits for them, and re-layouts  10.9 us (5%)
    ppermute x21, waiting for transfers between devices, shift(): lax.ppermute(value, axis, [(i, (i + step) % size) for i in range(size)])  40.7 us
    all_to_all x1, waiting for transfers between devices, body(): arrived0 = lax.all_to_all(send0, ALL, 0, 0, tiled=True)  34.5 us
    ppermute x21, starting transfers between devices, shift(): lax.ppermute(value, axis, [(i, (i + step) % size) for i in range(size)])  23.6 us
    all_to_all x1, waiting for transfers between devices, body(): arrived1 = lax.all_to_all(send1, ALL, 0, 0, tiled=True)  18.5 us
    all_to_all x1, waiting for transfers between devices, body(): y_both = lax.all_to_all(jnp.concatenate([own, own]), 'yh', 0, 0, tiled=True)  17 us
    pallas_call x1, Pallas kernels, pair_blocks(): pl.pallas_call(pair_kernel, out_shape=[jax.ShapeDtypeStruct((device_count...  15.8 us
    pallas_call x1, Pallas kernels, square_sum(): pl.pallas_call(functools.partial(square_kernel, tuple(places), cell_rows)...  15.1 us
    pallas_call x2, Pallas kernels, fock_sum(): pl.pallas_call(fock_kernel, out_shape=jax.ShapeDtypeStruct((slot_count, w...  9.41 us
  transfers between devices with their start and end apart: 25, of which 16 were waited for; matrix products, arithmetic and copies ran while one was open for 10% of the time, Pallas kernels for 16%

profile of v3, /device:TPU:1, one launch (start us, length us, event | category | flops | bytes accessed | tf_op | source)
XLA Modules:
  0.0 226.3 jit_solution(13005833512070190385)
XLA Ops:
  0.6 2.2 collective-permute-start.4
  2.8 3.8 %collective-permute-start.3 = (bf16[32,128,128]{2,1,0:T(8,128)(2,1)}, bf16[32,128,128]{2,1,0:T(8,128)(2,1)S(1)}, u32[]{:S(2)}, u32[]{:S(2)}) collective-permute-start(bf16[32,128,128]{2,1,0:T(8,128)(2,1)} %bitcast.51), channel_id=1, source_target_pairs={{0,6},{2,0},{4,2},{6,4},{1,7},{3,1},{5,3},{7,5},{8,14},{10,8},{12,... | collective-permute-start | bytes 3145736 | tf_op jit(solution)/shard_map/ppermute | solution.py:20
  6.6 2.5 %collective-permute-start.1 = (bf16[32,128,128]{2,1,0:T(8,128)(2,1)}, bf16[32,128,128]{2,1,0:T(8,128)(2,1)}, u32[]{:S(2)}, u32[]{:S(2)}) collective-permute-start(bf16[32,128,128]{2,1,0:T(8,128)(2,1)} %bitcast.53), channel_id=1, source_target_pairs={{0,96},{32,0},{64,32},{96,64},{1,97},{33,1},{65,33},{97,65},{2,98}... | collective-permute-start | bytes 3145736 | tf_op jit(solution)/shard_map/ppermute | solution.py:20
  9.1 3.1 %pad_maximum_fusion = bf16[64,128,128]{2,1,0:T(8,128)(2,1)} fusion(bf16[32,128,128]{2,1,0:T(8,128)(2,1)} %bitcast.55), kind=kLoop, calls=%fused_computation | loop fusion | flops 1048576 | bytes 3145728 | tf_op jit(solution)/shard_map/concatenate | solution.py:198
  12.1 3.9 %all-to-all-start = ((bf16[64,128,128]{2,1,0:T(8,128)(2,1)}), bf16[64,128,128]{2,1,0:T(8,128)(2,1)S(1)}, u32[]{:S(2)}, u32[]{:S(2)}) async-start(bf16[64,128,128]{2,1,0:T(8,128)(2,1)} %pad_maximum_fusion), calls=%async_computation | async-start | bytes 4194304 | tf_op jit(solution)/shard_map/all_to_all | solution.py:198
  16.0 9.6 %collective-permute-done.4.refs_14_ = bf16[32,128,128]{2,1,0:T(8,128)(2,1)} collective-permute-done((bf16[32,128,128]{2,1,0:T(8,128)(2,1)}, bf16[32,128,128]{2,1,0:T(8,128)(2,1)}, u32[]{:S(2)}, u32[]{:S(2)}) %collective-permute-start.4) | collective-permute-done | bytes 1048608 | tf_op jit(solution)/shard_map/ppermute | solution.py:20
  25.6 2.8 %collective-permute-done.3.refs_2_ = bf16[32,128,128]{2,1,0:T(8,128)(2,1)S(1)} collective-permute-done((bf16[32,128,128]{2,1,0:T(8,128)(2,1)}, bf16[32,128,128]{2,1,0:T(8,128)(2,1)S(1)}, u32[]{:S(2)}, u32[]{:S(2)}) %collective-permute-start.3) | collective-permute-done | bytes 1048608 | tf_op jit(solution)/shard_map/ppermute | solution.py:20
  28.4 3.1 %collective-permute-done.2.refs_1_ = bf16[32,128,128]{2,1,0:T(8,128)(2,1)} collective-permute-done((bf16[32,128,128]{2,1,0:T(8,128)(2,1)}, bf16[32,128,128]{2,1,0:T(8,128)(2,1)}, u32[]{:S(2)}, u32[]{:S(2)}) %collective-permute-start.2) | collective-permute-done | bytes 1048608 | tf_op jit(solution)/shard_map/ppermute | solution.py:20
  31.5 2.2 collective-permute-done.refs_10_
  33.7 17.0 %all-to-all-done = bf16[64,128,128]{2,1,0:T(8,128)(2,1)S(1)} async-done(((bf16[64,128,128]{2,1,0:T(8,128)(2,1)}), bf16[64,128,128]{2,1,0:T(8,128)(2,1)S(1)}, u32[]{:S(2)}, u32[]{:S(2)}) %all-to-all-start) | async-done | bytes 2097184 | tf_op jit(solution)/shard_map/all_to_all | solution.py:198
  50.8 3.8 %collective-permute-start.8 = (bf16[32,128,128]{2,1,0:T(8,128)(2,1)S(1)}, bf16[32,128,128]{2,1,0:T(8,128)(2,1)S(1)}, u32[]{:S(2)}, u32[]{:S(2)}) collective-permute-start(bf16[32,128,128]{2,1,0:T(8,128)(2,1)S(1)} %constant_dynamic-slice_fusion.1.refs_3_), channel_id=1, source_target_pairs={{0,6},{2,0},{4,2},{6,4},{1,7},{3,1},{5,3},{7,5},{8,14},{10,8},{12,... | collective-permute-start | bytes 3145736 | tf_op jit(solution)/shard_map/ppermute | solution.py:20
  54.6 2.5 %collective-permute-start.6 = (bf16[32,128,128]{2,1,0:T(8,128)(2,1)}, bf16[32,128,128]{2,1,0:T(8,128)(2,1)}, u32[]{:S(2)}, u32[]{:S(2)}) collective-permute-start(bf16[32,128,128]{2,1,0:T(8,128)(2,1)} %collective-permute-done.4.refs_14_), channel_id=1, source_target_pairs={{0,96},{32,0},{64,32},{96,64},{1,97},{33,1},{65,33},{97,65},{2,98}... | collective-permute-start | bytes 3145736 | tf_op jit(solution)/shard_map/ppermute | solution.py:20
  57.1 0.1 copy.27
  57.2 0.7 reshape_squeeze.3.pairs
  57.9 0.7 convert_reduce_fusion.2.ranks
  58.6 15.8 %pair_blocks.1 = (bf16[128,128,128]{2,1,0:T(8,128)(2,1)}, bf16[128,128,128]{2,1,0:T(8,128)(2,1)}) custom-call(s32[256]{0:T(256)} %reshape_squeeze.3.pairs, s32[128]{0:T(128)} %bitcast.67, s32[128]{0:T(128)} %convert_reduce_fusion.2.ranks, bf16[16,128,1024]{2,1,0:T(8,128)(2,1)} %bitcast.70, f32[1,1024]{1,0:T(1,128)} %bitcast.71), custom_call_target="tpu_custom_call" | custom-call | flops 8589934592 | bytes 8388608 | tf_op jit(solution)/shard_map/pair_blocks/pallas_call | solution.py:63
  74.4 1.1 collective-permute-done.8.refs_5_
  75.5 3.2 %collective-permute-done.7.refs_4_ = bf16[32,128,128]{2,1,0:T(8,128)(2,1)} collective-permute-done((bf16[32,128,128]{2,1,0:T(8,128)(2,1)S(1)}, bf16[32,128,128]{2,1,0:T(8,128)(2,1)}, u32[]{:S(2)}, u32[]{:S(2)}) %collective-permute-start.7) | collective-permute-done | bytes 1048608 | tf_op jit(solution)/shard_map/ppermute | solution.py:20
  78.8 2.4 %collective-permute-done.5.refs_16_ = bf16[32,128,128]{2,1,0:T(8,128)(2,1)} collective-permute-done((bf16[32,128,128]{2,1,0:T(8,128)(2,1)}, bf16[32,128,128]{2,1,0:T(8,128)(2,1)}, u32[]{:S(2)}, u32[]{:S(2)}) %collective-permute-start.5) | collective-permute-done | bytes 1048608 | tf_op jit(solution)/shard_map/ppermute | solution.py:20
  81.2 7.6 %all-to-all-start.1 = ((bf16[128,128,128]{2,1,0:T(8,128)(2,1)}), bf16[128,128,128]{2,1,0:T(8,128)(2,1)}, u32[]{:S(2)}, u32[]{:S(2)}) async-start(bf16[128,128,128]{2,1,0:T(8,128)(2,1)} %get-tuple-element.42), calls=%async_computation.1 | async-start | bytes 8388608 | tf_op jit(solution)/shard_map/all_to_all | solution.py:236
  88.7 1.1 slice.37
  89.8 1.1 slice.38
  90.9 1.1 slice.33
  92.0 1.1 slice.34
  93.1 1.1 slice.35
  94.2 1.1 slice.36
  95.3 1.1 pad_maximum_fusion.2
  96.5 2.6 %collective-permute-start.10 = (bf16[32,128,128]{2,1,0:T(8,128)(2,1)}, bf16[32,128,128]{2,1,0:T(8,128)(2,1)S(1)}, u32[]{:S(2)}, u32[]{:S(2)}) collective-permute-start(bf16[32,128,128]{2,1,0:T(8,128)(2,1)} %pad_maximum_fusion.2), channel_id=1, source_target_pairs={{0,96},{32,0},{64,32},{96,64},{1,97},{33,1},{65,33},{97,65},{2,98}... | collective-permute-start | bytes 3145736 | tf_op jit(solution)/shard_map/ppermute | solution.py:20
  99.1 1.1 pad_maximum_fusion.1
  100.3 1.0 pad_maximum_fusion.4
  101.4 3.2 %collective-permute-start.12 = (bf16[32,128,128]{2,1,0:T(8,128)(2,1)}, bf16[32,128,128]{2,1,0:T(8,128)(2,1)S(1)}, u32[]{:S(2)}, u32[]{:S(2)}) collective-permute-start(bf16[32,128,128]{2,1,0:T(8,128)(2,1)} %pad_maximum_fusion.4), channel_id=1, source_target_pairs={{0,6},{2,0},{4,2},{6,4},{1,7},{3,1},{5,3},{7,5},{8,14},{10,8},{12,... | collective-permute-start | bytes 3145736 | tf_op jit(solution)/shard_map/ppermute | solution.py:20
  104.6 1.1 pad_maximum_fusion.3
  105.8 0.1 select_reduce_fusion.4
  106.0 34.5 %all-to-all-done.1.refs_0_ = bf16[128,128,128]{2,1,0:T(8,128)(2,1)} async-done(((bf16[128,128,128]{2,1,0:T(8,128)(2,1)}), bf16[128,128,128]{2,1,0:T(8,128)(2,1)}, u32[]{:S(2)}, u32[]{:S(2)}) %all-to-all-start.1) | async-done | bytes 4194336 | tf_op jit(solution)/shard_map/all_to_all | solution.py:236
  140.6 0.7 copy.28
  141.3 6.0 %all-to-all-start.2 = ((s32[128,1,34]{2,1,0:T(1,128)}), s32[128,1,34]{2,1,0:T(1,128)S(1)}, u32[]{:S(2)}, u32[]{:S(2)}) async-start(s32[128,1,34]{2,1,0:T(1,128)} %bitcast.7), calls=%async_computation.2 | async-start | bytes 131072 | tf_op jit(solution)/shard_map/all_to_all | solution.py:243
  147.3 10.0 %collective-permute-done.10.refs_22_ = bf16[32,128,128]{2,1,0:T(8,128)(2,1)S(1)} collective-permute-done((bf16[32,128,128]{2,1,0:T(8,128)(2,1)}, bf16[32,128,128]{2,1,0:T(8,128)(2,1)S(1)}, u32[]{:S(2)}, u32[]{:S(2)}) %collective-permute-start.10) | collective-permute-done | bytes 1048608 | tf_op jit(solution)/shard_map/ppermute | solution.py:20
  157.3 2.0 collective-permute-done.9.refs_20_
  159.4 1.0 collective-permute-done.11.refs_6_
  160.4 4.6 %all-to-all-done.2 = s32[128,1,34]{2,1,0:T(1,128)S(1)} async-done(((s32[128,1,34]{2,1,0:T(1,128)}), s32[128,1,34]{2,1,0:T(1,128)S(1)}, u32[]{:S(2)}, u32[]{:S(2)}) %all-to-all-start.2) | async-done | bytes 17440 | tf_op jit(solution)/shard_map/all_to_all | solution.py:243
  165.0 5.3 %all-to-all-start.3 = ((bf16[128,128,128]{2,1,0:T(8,128)(2,1)}), bf16[128,128,128]{2,1,0:T(8,128)(2,1)}, u32[]{:S(2)}, u32[]{:S(2)}) async-start(bf16[128,128,128]{2,1,0:T(8,128)(2,1)} %get-tuple-element.47), calls=%async_computation.3 | async-start | bytes 8388608 | tf_op jit(solution)/shard_map/all_to_all | solution.py:247
  170.8 0.6 broadcast_multiply_fusion.where
  171.4 1.1 collective-permute-start.14
  172.5 0.5 collective-permute-start.16
  173.2 0.5 collective-permute-start.15
  174.1 0.6 select_reduce_fusion
  174.8 3.0 %collective-permute-done.13.refs_9_ = bf16[32,128,128]{2,1,0:T(8,128)(2,1)} collective-permute-done((bf16[32,128,128]{2,1,0:T(8,128)(2,1)S(1)}, bf16[32,128,128]{2,1,0:T(8,128)(2,1)}, u32[]{:S(2)}, u32[]{:S(2)}) %collective-permute-start.13) | collective-permute-done | bytes 1048608 | tf_op jit(solution)/shard_map/ppermute | solution.py:20
  177.8 0.1 collective-permute-start.18
  178.0 0.2 collective-permute-done.16.refs_15_
  178.2 0.4 collective-permute-start.19
  178.6 0.2 collective-permute-start.20
  178.8 0.2 slice_reduce_fusion
  178.9 0.2 copy.33
  179.1 0.7 select_n.208.picks
  179.9 0.7 convert_reduce_fusion.3
  180.5 0.2 convert_reduce_fusion
  180.7 0.7 select_reduce_fusion.1.order
  181.4 5.2 %fock_sum.2.refs_0_ = f32[32,128,128]{2,1,0:T(8,128)} custom-call(s32[128]{0:T(128)} %select_reduce_fusion.1.order, s32[33]{0:T(128)} %get-tuple-element.60.starts, bf16[128,128,128]{2,1,0:T(8,128)(2,1)} %all-to-all-done.1.refs_0_), custom_call_target="tpu_custom_call" | custom-call | flops 2097152 | bytes 4194304 | tf_op jit(solution)/shard_map/fock_sum/pallas_call | solution.py:114
  186.6 0.2 convert_reduce_fusion.1
  186.7 0.6 select_reduce_fusion.2.order
  187.4 1.0 copy-done.8
  188.4 15.1 %square_sum.1 = bf16[32,128,128]{2,1,0:T(8,128)(2,1)} custom-call(s32[30]{0:T(128)} %broadcast_multiply_fusion.where, s32[512]{0:T(512)} %select_n.208.picks, bf16[32,128,128]{2,1,0:T(8,128)(2,1)} %bitcast.56, bf16[32,128,128]{2,1,0:T(8,128)(2,1)} %collective-permute-done.2.refs_1_, bf16[32,128,128]{2,1,0:T(8,128)(2,1)} %copy-done.2, ...), custom_call_target="tpu_custom_call" | custom-call | flops 2147483648 | bytes 25165824 | tf_op jit(solution)/shard_map/square_sum/pallas_call | solution.py:167
  203.5 18.5 %all-to-all-done.3.refs_1_ = bf16[128,128,128]{2,1,0:T(8,128)(2,1)} async-done(((bf16[128,128,128]{2,1,0:T(8,128)(2,1)}), bf16[128,128,128]{2,1,0:T(8,128)(2,1)}, u32[]{:S(2)}, u32[]{:S(2)}) %all-to-all-start.3) | async-done | bytes 4194336 | tf_op jit(solution)/shard_map/all_to_all | solution.py:247
  222.0 4.2 %fock_sum.3 = bf16[32,128,128]{2,1,0:T(8,128)(2,1)} custom-call(s32[128]{0:T(128)} %select_reduce_fusion.2.order, s32[33]{0:T(128)} %get-tuple-element.61.starts, f32[32,128,128]{2,1,0:T(8,128)} %fock_sum.2.refs_0_, bf16[128,128,128]{2,1,0:T(8,128)(2,1)} %all-to-all-done.3.refs_1_), custom_call_target="tpu_custom_call" | custom-call | flops 2097152 | bytes 4194304 | tf_op jit(solution)/shard_map/fock_sum/pallas_call | solution.py:114
  (69 shorter events, 1.2 us)
Async XLA Ops:
  0.6 25.0 %collective-permute-start.4 = (bf16[32,128,128]{2,1,0:T(8,128)(2,1)}, bf16[32,128,128]{2,1,0:T(8,128)(2,1)}, u32[]{:S(2)}, u32[]{:S(2)}) collective-permute-start(bf16[32,128,128]{2,1,0:T(8,128)(2,1)} %bitcast.50), channel_id=1, source_target_pairs={{0,16},{16,0},{1,17},{17,1},{2,18},{18,2},{3,19},{19,3},{4,20},{20... | collective-permute-start | bytes 3145736 | tf_op jit(solution)/shard_map/ppermute | solution.py:20
  2.8 25.6 %collective-permute-start.3 = (bf16[32,128,128]{2,1,0:T(8,128)(2,1)}, bf16[32,128,128]{2,1,0:T(8,128)(2,1)S(1)}, u32[]{:S(2)}, u32[]{:S(2)}) collective-permute-start(bf16[32,128,128]{2,1,0:T(8,128)(2,1)} %bitcast.51), channel_id=1, source_target_pairs={{0,6},{2,0},{4,2},{6,4},{1,7},{3,1},{5,3},{7,5},{8,14},{10,8},{12,... | collective-permute-start | bytes 3145736 | tf_op jit(solution)/shard_map/ppermute | solution.py:20
  6.6 24.9 %collective-permute-start.2 = (bf16[32,128,128]{2,1,0:T(8,128)(2,1)}, bf16[32,128,128]{2,1,0:T(8,128)(2,1)}, u32[]{:S(2)}, u32[]{:S(2)}) collective-permute-start(bf16[32,128,128]{2,1,0:T(8,128)(2,1)} %bitcast.52), channel_id=1, source_target_pairs={{0,2},{2,4},{4,6},{6,0},{1,3},{3,5},{5,7},{7,1},{8,10},{10,12},{12... | collective-permute-start | bytes 3145736 | tf_op jit(solution)/shard_map/ppermute | solution.py:20
  6.6 24.9 %collective-permute-start.1 = (bf16[32,128,128]{2,1,0:T(8,128)(2,1)}, bf16[32,128,128]{2,1,0:T(8,128)(2,1)}, u32[]{:S(2)}, u32[]{:S(2)}) collective-permute-start(bf16[32,128,128]{2,1,0:T(8,128)(2,1)} %bitcast.53), channel_id=1, source_target_pairs={{0,96},{32,0},{64,32},{96,64},{1,97},{33,1},{65,33},{97,65},{2,98}... | collective-permute-start | bytes 3145736 | tf_op jit(solution)/shard_map/ppermute | solution.py:20
  9.1 24.7 %collective-permute-start = (bf16[32,128,128]{2,1,0:T(8,128)(2,1)}, bf16[32,128,128]{2,1,0:T(8,128)(2,1)}, u32[]{:S(2)}, u32[]{:S(2)}) collective-permute-start(bf16[32,128,128]{2,1,0:T(8,128)(2,1)} %bitcast.54), channel_id=1, source_target_pairs={{0,32},{32,64},{64,96},{96,0},{1,33},{33,65},{65,97},{97,1},{2,34}... | collective-permute-start | bytes 3145736 | tf_op jit(solution)/shard_map/ppermute | solution.py:20
  12.1 38.6 %all-to-all-start = ((bf16[64,128,128]{2,1,0:T(8,128)(2,1)}), bf16[64,128,128]{2,1,0:T(8,128)(2,1)S(1)}, u32[]{:S(2)}, u32[]{:S(2)}) async-start(bf16[64,128,128]{2,1,0:T(8,128)(2,1)} %pad_maximum_fusion), calls=%async_computation | async-start | bytes 4194304 | tf_op jit(solution)/shard_map/all_to_all | solution.py:198
  16.0 41.1 %copy-start.9 = (s32[1,1,128,2]{2,3,1,0:T(2,128)S(1)}, s32[1,1,128,2]{2,3,1,0:T(2,128)}, u32[]{:S(2)}) copy-start(s32[1,1,128,2]{2,3,1,0:T(2,128)} %param.9) | copy-start | bytes 3076
  16.0 41.9 %copy-start.12 = (s32[1,1,128,1]{2,3,1,0:T(1,128)S(1)}, s32[1,1,128,1]{2,3,1,0:T(1,128)}, u32[]{:S(2)}) copy-start(s32[1,1,128,1]{2,3,1,0:T(1,128)} %param.10) | copy-start | bytes 1540
  28.4 5.3 %copy-start.2 = (bf16[32,128,128]{2,1,0:T(8,128)(2,1)}, bf16[32,128,128]{2,1,0:T(8,128)(2,1)S(1)}, u32[]{:S(2)}) copy-start(bf16[32,128,128]{2,1,0:T(8,128)(2,1)S(1)} %collective-permute-done.3.refs_2_) | copy-start | bytes 3145732
  50.8 23.7 %copy-start.1 = (bf16[32,128,128]{2,1,0:T(8,128)(2,1)}, bf16[32,128,128]{2,1,0:T(8,128)(2,1)S(1)}, u32[]{:S(2)}) copy-start(bf16[32,128,128]{2,1,0:T(8,128)(2,1)S(1)} %constant_dynamic-slice_fusion.1.refs_3_) | copy-start | bytes 3145732
  50.8 24.7 %collective-permute-start.8 = (bf16[32,128,128]{2,1,0:T(8,128)(2,1)S(1)}, bf16[32,128,128]{2,1,0:T(8,128)(2,1)S(1)}, u32[]{:S(2)}, u32[]{:S(2)}) collective-permute-start(bf16[32,128,128]{2,1,0:T(8,128)(2,1)S(1)} %constant_dynamic-slice_fusion.1.refs_3_), channel_id=1, source_target_pairs={{0,6},{2,0},{4,2},{6,4},{1,7},{3,1},{5,3},{7,5},{8,14},{10,8},{12,... | collective-permute-start | bytes 3145736 | tf_op jit(solution)/shard_map/ppermute | solution.py:20
  54.6 24.1 %collective-permute-start.7 = (bf16[32,128,128]{2,1,0:T(8,128)(2,1)S(1)}, bf16[32,128,128]{2,1,0:T(8,128)(2,1)}, u32[]{:S(2)}, u32[]{:S(2)}) collective-permute-start(bf16[32,128,128]{2,1,0:T(8,128)(2,1)S(1)} %constant_dynamic-slice_fusion.1.refs_3_), channel_id=1, source_target_pairs={{0,2},{2,4},{4,6},{6,0},{1,3},{3,5},{5,7},{7,1},{8,10},{10,12},{12... | collective-permute-start | bytes 3145736 | tf_op jit(solution)/shard_map/ppermute | solution.py:20
  54.6 24.1 %collective-permute-start.6 = (bf16[32,128,128]{2,1,0:T(8,128)(2,1)}, bf16[32,128,128]{2,1,0:T(8,128)(2,1)}, u32[]{:S(2)}, u32[]{:S(2)}) collective-permute-start(bf16[32,128,128]{2,1,0:T(8,128)(2,1)} %collective-permute-done.4.refs_14_), channel_id=1, source_target_pairs={{0,96},{32,0},{64,32},{96,64},{1,97},{33,1},{65,33},{97,65},{2,98}... | collective-permute-start | bytes 3145736 | tf_op jit(solution)/shard_map/ppermute | solution.py:20
  57.1 24.1 %collective-permute-start.5 = (bf16[32,128,128]{2,1,0:T(8,128)(2,1)}, bf16[32,128,128]{2,1,0:T(8,128)(2,1)}, u32[]{:S(2)}, u32[]{:S(2)}) collective-permute-start(bf16[32,128,128]{2,1,0:T(8,128)(2,1)} %collective-permute-done.4.refs_14_), channel_id=1, source_target_pairs={{0,32},{32,64},{64,96},{96,0},{1,33},{33,65},{65,97},{97,1},{2,34}... | collective-permute-start | bytes 3145736 | tf_op jit(solution)/shard_map/ppermute | solution.py:20
  75.5 15.4 %copy-start.3 = (bf16[32,128,128]{2,1,0:T(8,128)(2,1)}, bf16[32,128,128]{2,1,0:T(8,128)(2,1)S(1)}, u32[]{:S(2)}) copy-start(bf16[32,128,128]{2,1,0:T(8,128)(2,1)S(1)} %collective-permute-done.8.refs_5_) | copy-start | bytes 3145732
  81.2 59.4 %all-to-all-start.1 = ((bf16[128,128,128]{2,1,0:T(8,128)(2,1)}), bf16[128,128,128]{2,1,0:T(8,128)(2,1)}, u32[]{:S(2)}, u32[]{:S(2)}) async-start(bf16[128,128,128]{2,1,0:T(8,128)(2,1)} %get-tuple-element.42), calls=%async_computation.1 | async-start | bytes 8388608 | tf_op jit(solution)/shard_map/all_to_all | solution.py:236
  95.3 5.0 %slice-start = ((bf16[32,128,128]{2,1,0:T(8,128)(2,1)}), bf16[16,128,128]{2,1,0:T(8,128)(2,1)S(1)}, s32[]{:S(2)}) async-start(bf16[32,128,128]{2,1,0:T(8,128)(2,1)} %copy-done.2), calls=%async_computation.4 | async-start | bytes 1048576 | tf_op jit(solution)/shard_map/slice | solution.py:240
  95.3 5.0 %slice-start.1 = ((bf16[32,128,128]{2,1,0:T(8,128)(2,1)}), bf16[16,128,128]{2,1,0:T(8,128)(2,1)S(1)}, s32[]{:S(2)}) async-start(bf16[32,128,128]{2,1,0:T(8,128)(2,1)} %copy-done.3), calls=%async_computation.5 | async-start | bytes 1048576 | tf_op jit(solution)/shard_map/slice | solution.py:240
  96.5 60.9 %collective-permute-start.10 = (bf16[32,128,128]{2,1,0:T(8,128)(2,1)}, bf16[32,128,128]{2,1,0:T(8,128)(2,1)S(1)}, u32[]{:S(2)}, u32[]{:S(2)}) collective-permute-start(bf16[32,128,128]{2,1,0:T(8,128)(2,1)} %pad_maximum_fusion.2), channel_id=1, source_target_pairs={{0,96},{32,0},{64,32},{96,64},{1,97},{33,1},{65,33},{97,65},{2,98}... | collective-permute-start | bytes 3145736 | tf_op jit(solution)/shard_map/ppermute | solution.py:20
  100.2 5.4 %copy-start.10 = (s32[1,2,16]{2,1,0:T(2,128)S(1)}, s32[1,2,16]{2,1,0:T(2,128)}, u32[]{:S(2)}) copy-start(s32[1,2,16]{2,1,0:T(2,128)} %param.13) | copy-start | bytes 388
  100.2 5.6 %copy-start.14 = (s32[128]{0:T(128)S(1)}, s32[128]{0:T(128)}, u32[]{:S(2)}) copy-start(s32[128]{0:T(128)} %convert_reduce_fusion.2.ranks) | copy-start | bytes 1540
  100.2 5.6 %copy-start.11 = (s32[1,1,128]{2,1,0:T(1,128)S(1)}, s32[1,1,128]{2,1,0:T(1,128)}, u32[]{:S(2)}) copy-start(s32[1,1,128]{2,1,0:T(1,128)} %param.11) | copy-start | bytes 1540
  100.2 5.6 %copy-start.13 = (s32[1,1,128,1]{2,3,1,0:T(1,128)S(1)}, s32[1,1,128,1]{2,3,1,0:T(1,128)}, u32[]{:S(2)}) copy-start(s32[1,1,128,1]{2,3,1,0:T(1,128)} %param.10) | copy-start | bytes 1540
  100.2 59.2 %collective-permute-start.9 = (bf16[32,128,128]{2,1,0:T(8,128)(2,1)}, bf16[32,128,128]{2,1,0:T(8,128)(2,1)}, u32[]{:S(2)}, u32[]{:S(2)}) collective-permute-start(bf16[32,128,128]{2,1,0:T(8,128)(2,1)} %pad_maximum_fusion.1), channel_id=1, source_target_pairs={{0,32},{32,64},{64,96},{96,0},{1,33},{33,65},{65,97},{97,1},{2,34}... | collective-permute-start | bytes 3145736 | tf_op jit(solution)/shard_map/ppermute | solution.py:20
  101.4 58.0 %collective-permute-start.12 = (bf16[32,128,128]{2,1,0:T(8,128)(2,1)}, bf16[32,128,128]{2,1,0:T(8,128)(2,1)S(1)}, u32[]{:S(2)}, u32[]{:S(2)}) collective-permute-start(bf16[32,128,128]{2,1,0:T(8,128)(2,1)} %pad_maximum_fusion.4), channel_id=1, source_target_pairs={{0,6},{2,0},{4,2},{6,4},{1,7},{3,1},{5,3},{7,5},{8,14},{10,8},{12,... | collective-permute-start | bytes 3145736 | tf_op jit(solution)/shard_map/ppermute | solution.py:20
  105.6 54.7 %collective-permute-start.11 = (bf16[32,128,128]{2,1,0:T(8,128)(2,1)}, bf16[32,128,128]{2,1,0:T(8,128)(2,1)S(1)}, u32[]{:S(2)}, u32[]{:S(2)}) collective-permute-start(bf16[32,128,128]{2,1,0:T(8,128)(2,1)} %pad_maximum_fusion.3), channel_id=1, source_target_pairs={{0,2},{2,4},{4,6},{6,0},{1,3},{3,5},{5,7},{7,1},{8,10},{10,12},{12... | collective-permute-start | bytes 3145736 | tf_op jit(solution)/shard_map/ppermute | solution.py:20
  141.3 23.7 %all-to-all-start.2 = ((s32[128,1,34]{2,1,0:T(1,128)}), s32[128,1,34]{2,1,0:T(1,128)S(1)}, u32[]{:S(2)}, u32[]{:S(2)}) async-start(s32[128,1,34]{2,1,0:T(1,128)} %bitcast.7), calls=%async_computation.2 | async-start | bytes 131072 | tf_op jit(solution)/shard_map/all_to_all | solution.py:243
  157.3 21.2 %copy-start.4 = (bf16[32,128,128]{2,1,0:T(8,128)(2,1)}, bf16[32,128,128]{2,1,0:T(8,128)(2,1)S(1)}, u32[]{:S(2)}) copy-start(bf16[32,128,128]{2,1,0:T(8,128)(2,1)S(1)} %collective-permute-done.10.refs_22_) | copy-start | bytes 3145732
  159.4 5.6 %copy-start.5 = (bf16[32,128,128]{2,1,0:T(8,128)(2,1)}, bf16[32,128,128]{2,1,0:T(8,128)(2,1)S(1)}, u32[]{:S(2)}) copy-start(bf16[32,128,128]{2,1,0:T(8,128)(2,1)S(1)} %collective-permute-done.12.refs_7_) | copy-start | bytes 3145732
  160.4 4.7 %copy-start.6 = (bf16[32,128,128]{2,1,0:T(8,128)(2,1)}, bf16[32,128,128]{2,1,0:T(8,128)(2,1)S(1)}, u32[]{:S(2)}) copy-start(bf16[32,128,128]{2,1,0:T(8,128)(2,1)S(1)} %collective-permute-done.11.refs_6_) | copy-start | bytes 3145732
  165.0 7.5 %copy-start = (bf16[1,2,16,128,128]{4,3,2,1,0:T(8,128)(2,1)S(1)}, bf16[1,2,16,128,128]{4,3,2,1,0:T(8,128)(2,1)}, u32[]{:S(2)}) copy-start(bf16[1,2,16,128,128]{4,3,2,1,0:T(8,128)(2,1)} %param.12) | copy-start | bytes 3145732
  165.0 57.0 %all-to-all-start.3 = ((bf16[128,128,128]{2,1,0:T(8,128)(2,1)}), bf16[128,128,128]{2,1,0:T(8,128)(2,1)}, u32[]{:S(2)}, u32[]{:S(2)}) async-start(bf16[128,128,128]{2,1,0:T(8,128)(2,1)} %get-tuple-element.47), calls=%async_computation.3 | async-start | bytes 8388608 | tf_op jit(solution)/shard_map/all_to_all | solution.py:247
  171.4 7.2 %collective-permute-start.14 = (bf16[32,128,128]{2,1,0:T(8,128)(2,1)}, bf16[32,128,128]{2,1,0:T(8,128)(2,1)S(1)}, u32[]{:S(2)}, u32[]{:S(2)}) collective-permute-start(bf16[32,128,128]{2,1,0:T(8,128)(2,1)} %collective-permute-done.refs_10_), channel_id=1, source_target_pairs={{0,8},{8,0},{1,9},{9,1},{2,10},{10,2},{3,11},{11,3},{4,12},{12,4},... | collective-permute-start | bytes 3145736 | tf_op jit(solution)/shard_map/ppermute | solution.py:20
  172.5 5.3 %collective-permute-start.13 = (bf16[32,128,128]{2,1,0:T(8,128)(2,1)S(1)}, bf16[32,128,128]{2,1,0:T(8,128)(2,1)}, u32[]{:S(2)}, u32[]{:S(2)}) collective-permute-start(bf16[32,128,128]{2,1,0:T(8,128)(2,1)S(1)} %bitcast.58), channel_id=1, source_target_pairs={{0,8},{8,0},{1,9},{9,1},{2,10},{10,2},{3,11},{11,3},{4,12},{12,4},... | collective-permute-start | bytes 3145736 | tf_op jit(solution)/shard_map/ppermute | solution.py:20
  172.5 5.6 %collective-permute-start.16 = (bf16[32,128,128]{2,1,0:T(8,128)(2,1)}, bf16[32,128,128]{2,1,0:T(8,128)(2,1)}, u32[]{:S(2)}, u32[]{:S(2)}) collective-permute-start(bf16[32,128,128]{2,1,0:T(8,128)(2,1)} %collective-permute-done.4.refs_14_), channel_id=1, source_target_pairs={{0,8},{8,0},{1,9},{9,1},{2,10},{10,2},{3,11},{11,3},{4,12},{12,4},... | collective-permute-start | bytes 3145736 | tf_op jit(solution)/shard_map/ppermute | solution.py:20
  173.1 14.2 %collective-permute-start.17 = (bf16[32,128,128]{2,1,0:T(8,128)(2,1)}, bf16[32,128,128]{2,1,0:T(8,128)(2,1)}, u32[]{:S(2)}, u32[]{:S(2)}) collective-permute-start(bf16[32,128,128]{2,1,0:T(8,128)(2,1)} %collective-permute-done.5.refs_16_), channel_id=1, source_target_pairs={{0,8},{8,0},{1,9},{9,1},{2,10},{10,2},{3,11},{11,3},{4,12},{12,4},... | collective-permute-start | bytes 3145736 | tf_op jit(solution)/shard_map/ppermute | solution.py:20
  173.2 14.2 %collective-permute-start.15 = (bf16[32,128,128]{2,1,0:T(8,128)(2,1)}, bf16[32,128,128]{2,1,0:T(8,128)(2,1)}, u32[]{:S(2)}, u32[]{:S(2)}) collective-permute-start(bf16[32,128,128]{2,1,0:T(8,128)(2,1)} %collective-permute-done.1.refs_12_), channel_id=1, source_target_pairs={{0,8},{8,0},{1,9},{9,1},{2,10},{10,2},{3,11},{11,3},{4,12},{12,4},... | collective-permute-start | bytes 3145736 | tf_op jit(solution)/shard_map/ppermute | solution.py:20
  177.8 9.5 %collective-permute-start.18 = (bf16[32,128,128]{2,1,0:T(8,128)(2,1)}, bf16[32,128,128]{2,1,0:T(8,128)(2,1)S(1)}, u32[]{:S(2)}, u32[]{:S(2)}) collective-permute-start(bf16[32,128,128]{2,1,0:T(8,128)(2,1)} %collective-permute-done.6.refs_18_), channel_id=1, source_target_pairs={{0,8},{8,0},{1,9},{9,1},{2,10},{10,2},{3,11},{11,3},{4,12},{12,4},... | collective-permute-start | bytes 3145736 | tf_op jit(solution)/shard_map/ppermute | solution.py:20
  178.2 9.2 %collective-permute-start.19 = (bf16[32,128,128]{2,1,0:T(8,128)(2,1)}, bf16[32,128,128]{2,1,0:T(8,128)(2,1)}, u32[]{:S(2)}, u32[]{:S(2)}) collective-permute-start(bf16[32,128,128]{2,1,0:T(8,128)(2,1)} %collective-permute-done.9.refs_20_), channel_id=1, source_target_pairs={{0,8},{8,0},{1,9},{9,1},{2,10},{10,2},{3,11},{11,3},{4,12},{12,4},... | collective-permute-start | bytes 3145736 | tf_op jit(solution)/shard_map/ppermute | solution.py:20
  178.6 8.0 %copy-start.7 = (bf16[32,128,128]{2,1,0:T(8,128)(2,1)}, bf16[32,128,128]{2,1,0:T(8,128)(2,1)S(1)}, u32[]{:S(2)}) copy-start(bf16[32,128,128]{2,1,0:T(8,128)(2,1)S(1)} %collective-permute-done.14.refs_11_) | copy-start | bytes 3145732
  178.6 8.8 %collective-permute-start.20 = (bf16[32,128,128]{2,1,0:T(8,128)(2,1)S(1)}, bf16[32,128,128]{2,1,0:T(8,128)(2,1)}, u32[]{:S(2)}, u32[]{:S(2)}) collective-permute-start(bf16[32,128,128]{2,1,0:T(8,128)(2,1)S(1)} %collective-permute-done.10.refs_22_), channel_id=1, source_target_pairs={{0,8},{8,0},{1,9},{9,1},{2,10},{10,2},{3,11},{11,3},{4,12},{12,4},... | collective-permute-start | bytes 3145736 | tf_op jit(solution)/shard_map/ppermute | solution.py:20
  187.4 1.1 copy-start.8

commit v4 on v3

--- a/solution.py
+++ b/solution.py
@@ -192,26 +192,11 @@
     half = cell_rows
     own = matrix_blocks.reshape(2 * cell_rows, width, width)
 
-    x_behind, x_ahead = shift(own, "x", 1), shift(own, "x", -1)
-    z_behind, z_ahead = shift(own, "z", 1), shift(own, "z", -1)
-    y_low = shift(own, "yl", 1)
-    y_both = lax.all_to_all(jnp.concatenate([own, own]), "yh", 0, 0, tiled=True)
-
-    x_behind, x_ahead, z_behind, z_ahead, y_low, y_both, basis = lax.optimization_barrier(
-        (x_behind, x_ahead, z_behind, z_ahead, y_low, y_both, basis_values)
-    )
-    y_high = lax.dynamic_slice_in_dim(y_both, (1 - yh) * 2 * cell_rows, 2 * cell_rows, 0)
-    x_behind2, x_ahead2 = shift(y_low, "x", 1), shift(y_low, "x", -1)
-    z_behind2, z_ahead2 = shift(y_high, "z", 1), shift(y_high, "z", -1)
-
     owners, slots = task_owner.reshape(-1), task_slot.reshape(-1)
     task_count = owners.shape[0]
     number = jnp.arange(task_count, dtype=jnp.int32)
     earlier = (owners[:, None] == owners[None, :]) & (number[None, :] < number[:, None])
     ranks = jnp.sum(earlier.astype(jnp.int32), axis=1)
-    send0, send1 = pair_blocks(
-        basis[0, 0], potential[0], task_pairs[0, 0], owners, ranks, device_count
-    )
     spots = jnp.arange(device_count, dtype=jnp.int32)
     named = owners[None, :] == spots[:, None]
     send_slots = [
@@ -228,21 +213,39 @@
         axis=1,
     )
 
-    x_behind2, x_ahead2, z_behind2, z_ahead2, own2, x_behind, x_ahead, y_low, send0 = (
+    y_both = lax.all_to_all(jnp.concatenate([own, own]), "yh", 0, 0, tiled=True)
+    y_low = shift(own, "yl", 1)
+    x_behind, x_ahead = shift(own, "x", 1), shift(own, "x", -1)
+    z_behind, z_ahead = shift(own, "z", 1), shift(own, "z", -1)
+    send0, send1 = pair_blocks(
+        basis_values[0, 0], potential[0], task_pairs[0, 0], owners, ranks, device_count
+    )
+
+    x_behind, x_ahead, z_behind, z_ahead, y_low, send0, send1 = lax.optimization_barrier(
+        (x_behind, x_ahead, z_behind, z_ahead, y_low, send0, send1)
+    )
+    z_far0, z_far1 = shift(z_behind[:half], "z", 1), shift(z_ahead[half:], "z", -1)
+    x_behind2, x_ahead2 = shift(y_low, "x", 1), shift(y_low, "x", -1)
+
+    z_far0, z_far1, y_both, numbers, x_behind3, x_ahead3 = lax.optimization_barrier(
+        (z_far0, z_far1, y_both, numbers, x_behind, x_ahead)
+    )
+    y_high = lax.dynamic_slice_in_dim(y_both, (1 - yh) * 2 * cell_rows, 2 * cell_rows, 0)
+    z_behind2, z_ahead2 = shift(y_high, "z", 1), shift(y_high, "z", -1)
+    x_far0, x_far1 = shift(x_behind3[:half], "x", 1), shift(x_ahead3[half:], "x", -1)
+    numbers = lax.all_to_all(numbers[:, None, :], ALL, 0, 0, tiled=True)[:, 0, :]
+
+    x_behind2, x_ahead2, z_behind2, z_ahead2, x_far0, x_far1, numbers, own2, send0 = (
         lax.optimization_barrier(
-            (x_behind2, x_ahead2, z_behind2, z_ahead2, own, x_behind, x_ahead, y_low, send0)
+            (x_behind2, x_ahead2, z_behind2, z_ahead2, x_far0, x_far1, numbers, own, send0)
         )
     )
     arrived0 = lax.all_to_all(send0, ALL, 0, 0, tiled=True)
-    x_far0 = shift(jnp.concatenate([x_behind[:half], x_behind2[:half]]), "x", 1)
-    x_far1 = shift(jnp.concatenate([x_ahead[half:], x_ahead2[half:]]), "x", -1)
-    z_far0 = shift(jnp.concatenate([z_behind[:half], z_behind2[:half]]), "z", 1)
-    z_far1 = shift(jnp.concatenate([z_ahead[half:], z_ahead2[half:]]), "z", -1)
-
-    arrived0, numbers = lax.optimization_barrier((arrived0, numbers))
-    numbers = lax.all_to_all(numbers[:, None, :], ALL, 0, 0, tiled=True)[:, 0, :]
-    x_far0, x_far1, z_far0, z_far1, numbers, send1 = lax.optimization_barrier(
-        (x_far0, x_far1, z_far0, z_far1, numbers, send1)
+    x_far2, x_far3 = shift(x_behind2[:half], "x", 1), shift(x_ahead2[half:], "x", -1)
+    z_far2, z_far3 = shift(z_behind2[:half], "z", 1), shift(z_ahead2[half:], "z", -1)
+
+    arrived0, x_far2, x_far3, z_far2, z_far3, send1 = lax.optimization_barrier(
+        (arrived0, x_far2, x_far3, z_far2, z_far3, send1)
     )
     arrived1 = lax.all_to_all(send1, ALL, 0, 0, tiled=True)
 
@@ -265,17 +268,20 @@
     left(y_high, 0, 2, 0, 1, 0)
     left(z_behind2, 0, 2, 3, 1, 0)
     left(z_ahead2, 0, 2, 1, 1, 0)
-    for pair in range(2):
-        left(z_far0, pair, 1, 2, pair, 0)
-        left(z_far1, pair, 1, 2, pair, 1)
+    left(z_far0, 0, 1, 2, 0, 0)
+    left(z_far1, 0, 1, 2, 0, 1)
+    left(z_far2, 0, 1, 2, 1, 0)
+    left(z_far3, 0, 1, 2, 1, 1)
     right(own2, (0, 2, 0, 0, 0))
     right(x_behind, (0, 2, 3, 0, 0))
     right(x_ahead, (0, 2, 1, 0, 0))
     right(y_low, (0, 2, 0, 1, 0))
     right(x_behind2, (0, 2, 3, 1, 0))
     right(x_ahead2, (0, 2, 1, 1, 0))
-    right(x_far0, (0, 1, 2, 0, 0), (1, 1, 2, 1, 0))
-    right(x_far1, (0, 1, 2, 0, 1), (1, 1, 2, 1, 1))
+    right(x_far0, (0, 1, 2, 0, 0))
+    right(x_far1, (0, 1, 2, 0, 1))
+    right(x_far2, (0, 1, 2, 1, 0))
+    right(x_far3, (0, 1, 2, 1, 1))
 
     every = numbers[:, 2:].reshape(row_count, cells, cell_rows)
     me_row = (x * 2 + yl) * 2 + c

time: 228 us -> 216 us (0.947)
  waiting for transfers between devices: 115 us -> 84.6 us
  blocking collectives: 0 us -> 18.8 us
  other arithmetic: 12.1 us -> 7.69 us
  local copies, waits for them, and re-layouts: 10.9 us -> 13.8 us
    all_to_all x1, waiting for transfers between devices: 34.5 us -> 0.01 us  [body(): arrived0 = lax.all_to_all(send0, ALL, 0, 0, tiled=True)]
    all_to_all x0 -> x1, blocking collectives: none -> 18.8 us  [body(): lax.all_to_all(numbers[:, None, :], ALL, 0, 0, tiled=True)[:, 0, :]]
    ppermute x21 -> x27, waiting for transfers between devices: 40.7 us -> 58 us  [shift(): lax.ppermute(value, axis, [(i, (i + step) % size) for i in range(size)])]
    all_to_all x1 -> x0, starting transfers between devices: 6.01 us -> none  [body(): lax.all_to_all(numbers[:, None, :], ALL, 0, 0, tiled=True)[:, 0, :]]
    ppermute x21 -> x27, starting transfers between devices: 23.6 us -> 29.5 us  [shift(): lax.ppermute(value, axis, [(i, (i + step) % size) for i in range(size)])]
    all_to_all x1, waiting for transfers between devices: 18.5 us -> 13.7 us  [body(): arrived1 = lax.all_to_all(send1, ALL, 0, 0, tiled=True)]
    all_to_all x1 -> x0, waiting for transfers between devices: 4.65 us -> none  [body(): lax.all_to_all(numbers[:, None, :], ALL, 0, 0, tiled=True)[:, 0, :]]
    concatenate x4 -> x0, other arithmetic: 4.38 us -> none  [the longest x1 1.15 us: body(): x_far1 = shift(jnp.concatenate([x_ahead[half:], x_ahead2[half:]]), 'x', -1)]
  transfers between devices with their start and end apart: 25 -> 30, of which waited for: 16 -> 8; matrix products, arithmetic and copies ran while one was open for 10% -> 9% of each run, Pallas kernels for 16% -> 17%
where the time goes in v4:
time: 216 us
  waiting for transfers between devices  84.6 us (39%)
  starting transfers between devices  47.7 us (22%)
  Pallas kernels  41.9 us (19%)
  blocking collectives  18.8 us (9%)
  local copies, waits for them, and re-layouts  13.8 us (6%)
  other arithmetic  7.69 us (4%)
    ppermute x27, waiting for transfers between devices, shift(): lax.ppermute(value, axis, [(i, (i + step) % size) for i in range(size)])  58 us
    ppermute x27, starting transfers between devices, shift(): lax.ppermute(value, axis, [(i, (i + step) % size) for i in range(size)])  29.5 us
    all_to_all x1, blocking collectives, body(): lax.all_to_all(numbers[:, None, :], ALL, 0, 0, tiled=True)[:, 0, :]  18.8 us
    pallas_call x1, Pallas kernels, pair_blocks(): pl.pallas_call(pair_kernel, out_shape=[jax.ShapeDtypeStruct((device_count...  15.8 us
    pallas_call x1, Pallas kernels, square_sum(): pl.pallas_call(functools.partial(square_kernel, tuple(places), cell_rows)...  15.1 us
    all_to_all x1, waiting for transfers between devices, body(): arrived1 = lax.all_to_all(send1, ALL, 0, 0, tiled=True)  13.7 us
    all_to_all x1, waiting for transfers between devices, body(): y_both = lax.all_to_all(jnp.concatenate([own, own]), 'yh', 0, 0, tiled=True)  12.9 us
    pallas_call x2, Pallas kernels, fock_sum(): pl.pallas_call(fock_kernel, out_shape=jax.ShapeDtypeStruct((slot_count, w...  11 us
  transfers between devices with their start and end apart: 30, of which 8 were waited for; matrix products, arithmetic and copies ran while one was open for 9% of the time, Pallas kernels for 17%

profile of v4, /device:TPU:1, one launch (start us, length us, event | category | flops | bytes accessed | tf_op | source)
XLA Modules:
  0.0 215.8 jit_solution(2524022115898852704)
XLA Ops:
  0.6 2.1 collective-permute-start
  2.7 1.4 collective-permute-start.1
  4.1 1.8 collective-permute-start.2
  5.8 2.1 collective-permute-start.3
  8.0 1.3 collective-permute-start.4
  9.3 3.1 %pad_maximum_fusion = bf16[64,128,128]{2,1,0:T(8,128)(2,1)} fusion(bf16[32,128,128]{2,1,0:T(8,128)(2,1)} %bitcast.55), kind=kLoop, calls=%fused_computation | loop fusion | flops 1048576 | bytes 3145728 | tf_op jit(solution)/shard_map/concatenate | solution.py:216
  12.4 4.0 %all-to-all-start = ((bf16[64,128,128]{2,1,0:T(8,128)(2,1)}), bf16[64,128,128]{2,1,0:T(8,128)(2,1)S(1)}, u32[]{:S(2)}, u32[]{:S(2)}) async-start(bf16[64,128,128]{2,1,0:T(8,128)(2,1)} %pad_maximum_fusion), calls=%async_computation | async-start | bytes 4194304 | tf_op jit(solution)/shard_map/all_to_all | solution.py:216
  16.4 0.1 copy.27
  16.5 0.7 reshape_squeeze.3.pairs
  17.2 0.7 convert_reduce_fusion.2.ranks
  17.9 15.8 %pair_blocks.1 = (bf16[128,128,128]{2,1,0:T(8,128)(2,1)}, bf16[128,128,128]{2,1,0:T(8,128)(2,1)}) custom-call(s32[256]{0:T(256)} %reshape_squeeze.3.pairs, s32[128]{0:T(128)} %bitcast.68, s32[128]{0:T(128)} %convert_reduce_fusion.2.ranks, bf16[16,128,1024]{2,1,0:T(8,128)(2,1)} %bitcast.71, f32[1,1024]{1,0:T(1,128)} %bitcast.72), custom_call_target="tpu_custom_call" | custom-call | flops 8589934592 | bytes 8388608 | tf_op jit(solution)/shard_map/pair_blocks/pallas_call | solution.py:63
  33.9 2.1 slice.33
  36.0 1.9 slice.34
  37.9 2.7 %collective-permute-start.8 = (bf16[16,128,128]{2,1,0:T(8,128)(2,1)}, bf16[16,128,128]{2,1,0:T(8,128)(2,1)}, u32[]{:S(2)}, u32[]{:S(2)}) collective-permute-start(bf16[16,128,128]{2,1,0:T(8,128)(2,1)} %slice.34), channel_id=1, source_target_pairs={{0,6},{2,0},{4,2},{6,4},{1,7},{3,1},{5,3},{7,5},{8,14},{10,8},{12,... | collective-permute-start | bytes 1572872 | tf_op jit(solution)/shard_map/ppermute | solution.py:20
  40.8 0.1 select_reduce_fusion.4
  40.9 2.4 %collective-permute-start.6 = (bf16[32,128,128]{2,1,0:T(8,128)(2,1)}, bf16[32,128,128]{2,1,0:T(8,128)(2,1)}, u32[]{:S(2)}, u32[]{:S(2)}) collective-permute-start(bf16[32,128,128]{2,1,0:T(8,128)(2,1)} %collective-permute-done.4.refs_16_), channel_id=1, source_target_pairs={{0,96},{32,0},{64,32},{96,64},{1,97},{33,1},{65,33},{97,65},{2,98}... | collective-permute-start | bytes 3145736 | tf_op jit(solution)/shard_map/ppermute | solution.py:20
  43.4 12.9 %all-to-all-done = bf16[64,128,128]{2,1,0:T(8,128)(2,1)S(1)} async-done(((bf16[64,128,128]{2,1,0:T(8,128)(2,1)}), bf16[64,128,128]{2,1,0:T(8,128)(2,1)S(1)}, u32[]{:S(2)}, u32[]{:S(2)}) %all-to-all-start) | async-done | bytes 2097184 | tf_op jit(solution)/shard_map/all_to_all | solution.py:216
  56.4 2.7 %collective-permute-start.10 = (bf16[32,128,128]{2,1,0:T(8,128)(2,1)S(1)}, bf16[32,128,128]{2,1,0:T(8,128)(2,1)S(1)}, u32[]{:S(2)}, u32[]{:S(2)}) collective-permute-start(bf16[32,128,128]{2,1,0:T(8,128)(2,1)S(1)} %constant_dynamic-slice_fusion.1.refs_3_), channel_id=1, source_target_pairs={{0,6},{2,0},{4,2},{6,4},{1,7},{3,1},{5,3},{7,5},{8,14},{10,8},{12,... | collective-permute-start | bytes 3145736 | tf_op jit(solution)/shard_map/ppermute | solution.py:20
  59.1 0.8 slice.35
  59.9 1.9 slice.36
  61.9 2.7 %collective-permute-start.12 = (bf16[16,128,128]{2,1,0:T(8,128)(2,1)}, bf16[16,128,128]{2,1,0:T(8,128)(2,1)}, u32[]{:S(2)}, u32[]{:S(2)}) collective-permute-start(bf16[16,128,128]{2,1,0:T(8,128)(2,1)} %slice.36), channel_id=1, source_target_pairs={{0,96},{32,0},{64,32},{96,64},{1,97},{33,1},{65,33},{97,65},{2,98}... | collective-permute-start | bytes 1572872 | tf_op jit(solution)/shard_map/ppermute | solution.py:20
  64.5 0.1 copy.28
  64.6 18.8 %all_to_all.20 = s32[128,1,34]{2,1,0:T(1,128)S(1)} all-to-all(s32[128,1,34]{2,1,0:T(1,128)S(1)} %bitcast.63), channel_id=1, replica_groups=mesh['x'=4,'yl'=2,'c'=2,'z'=4,'yh'=2] {'x','yl','c','z','yh'}, dimensions={0} | all-to-all | bytes 34816 | tf_op jit(solution)/shard_map/all_to_all | solution.py:236
  83.5 6.1 %all-to-all-start.2 = ((bf16[128,128,128]{2,1,0:T(8,128)(2,1)}), bf16[128,128,128]{2,1,0:T(8,128)(2,1)}, u32[]{:S(2)}, u32[]{:S(2)}) async-start(bf16[128,128,128]{2,1,0:T(8,128)(2,1)} %get-tuple-element.45), calls=%async_computation.2 | async-start | bytes 8388608 | tf_op jit(solution)/shard_map/all_to_all | solution.py:243
  89.6 1.1 slice.39
  90.7 1.5 collective-permute-start.13
  92.2 1.1 slice.40
  93.2 1.4 collective-permute-start.14
  94.7 1.6 collective-permute-start.15
  96.3 1.8 collective-permute-start.16
  98.1 50.7 %collective-permute-done.13.refs_26_ = bf16[16,128,128]{2,1,0:T(8,128)(2,1)} collective-permute-done((bf16[16,128,128]{2,1,0:T(8,128)(2,1)S(1)}, bf16[16,128,128]{2,1,0:T(8,128)(2,1)}, u32[]{:S(2)}, u32[]{:S(2)}) %collective-permute-start.13) | collective-permute-done | bytes 524320 | tf_op jit(solution)/shard_map/ppermute | solution.py:20
  148.8 0.6 collective-permute-done.15.refs_8_
  149.4 0.8 copy-done.9
  150.2 0.2 copy-done.10
  150.4 8.1 %all-to-all-start.3 = ((bf16[128,128,128]{2,1,0:T(8,128)(2,1)}), bf16[128,128,128]{2,1,0:T(8,128)(2,1)}, u32[]{:S(2)}, u32[]{:S(2)}) async-start(bf16[128,128,128]{2,1,0:T(8,128)(2,1)} %get-tuple-element.52), calls=%async_computation.3 | async-start | bytes 8388608 | tf_op jit(solution)/shard_map/all_to_all | solution.py:250
  158.9 0.1 stack.123
  159.0 0.5 broadcast_multiply_fusion.where
  159.5 1.1 collective-permute-start.18
  160.7 0.5 collective-permute-start.20
  161.3 0.5 collective-permute-start.22
  162.1 0.1 iota_compare_fusion
  162.2 0.6 select_reduce_fusion
  162.9 1.5 collective-permute-done.18.refs_13_
  164.4 0.4 collective-permute-start.17
  164.8 0.4 collective-permute-start.23
  165.2 1.1 collective-permute-done.20.refs_17_
  166.3 0.4 collective-permute-start.24
  166.7 0.2 slice_reduce_fusion
  166.8 0.2 copy.33
  167.0 0.7 select_n.208.picks
  167.8 3.8 %collective-permute-done.23.refs_23_ = bf16[16,128,128]{2,1,0:T(8,128)(2,1)} collective-permute-done((bf16[16,128,128]{2,1,0:T(8,128)(2,1)}, bf16[16,128,128]{2,1,0:T(8,128)(2,1)}, u32[]{:S(2)}, u32[]{:S(2)}) %collective-permute-start.23) | collective-permute-done | bytes 524320 | tf_op jit(solution)/shard_map/ppermute | solution.py:20
  171.5 0.4 collective-permute-start.25
  171.9 0.4 collective-permute-done.24.refs_25_
  172.3 0.4 collective-permute-start.26
  172.7 0.6 convert_reduce_fusion.3
  173.3 0.2 convert_reduce_fusion.1
  173.5 0.7 select_reduce_fusion.2.order
  174.2 0.2 convert_reduce_fusion
  174.3 0.6 select_reduce_fusion.1.order
  175.0 5.4 %fock_sum.2.refs_0_ = f32[32,128,128]{2,1,0:T(8,128)} custom-call(s32[128]{0:T(128)} %select_reduce_fusion.1.order, s32[33]{0:T(128)} %get-tuple-element.68.starts, bf16[128,128,128]{2,1,0:T(8,128)(2,1)} %all-to-all-done.2.refs_0_), custom_call_target="tpu_custom_call" | custom-call | flops 2097152 | bytes 4194304 | tf_op jit(solution)/shard_map/fock_sum/pallas_call | solution.py:114
  180.4 1.0 copy-done.8
  181.4 15.1 %square_sum.1 = bf16[32,128,128]{2,1,0:T(8,128)(2,1)} custom-call(s32[30]{0:T(128)} %broadcast_multiply_fusion.where, s32[512]{0:T(512)} %select_n.208.picks, bf16[32,128,128]{2,1,0:T(8,128)(2,1)} %bitcast.56, bf16[32,128,128]{2,1,0:T(8,128)(2,1)} %collective-permute-done.2.refs_1_, bf16[32,128,128]{2,1,0:T(8,128)(2,1)} %collective-permute-done.3.refs_2_, ...), custom_call_target="tpu_custom_call" | custom-call | flops 2147483648 | bytes 25165824 | tf_op jit(solution)/shard_map/square_sum/pallas_call | solution.py:167
  196.5 13.7 %all-to-all-done.3.refs_1_ = bf16[128,128,128]{2,1,0:T(8,128)(2,1)} async-done(((bf16[128,128,128]{2,1,0:T(8,128)(2,1)}), bf16[128,128,128]{2,1,0:T(8,128)(2,1)}, u32[]{:S(2)}, u32[]{:S(2)}) %all-to-all-start.3) | async-done | bytes 4194336 | tf_op jit(solution)/shard_map/all_to_all | solution.py:250
  210.2 5.6 %fock_sum.3 = bf16[32,128,128]{2,1,0:T(8,128)(2,1)} custom-call(s32[128]{0:T(128)} %select_reduce_fusion.2.order, s32[33]{0:T(128)} %get-tuple-element.69.starts, f32[32,128,128]{2,1,0:T(8,128)} %fock_sum.2.refs_0_, bf16[128,128,128]{2,1,0:T(8,128)(2,1)} %all-to-all-done.3.refs_1_), custom_call_target="tpu_custom_call" | custom-call | flops 2097152 | bytes 4194304 | tf_op jit(solution)/shard_map/fock_sum/pallas_call | solution.py:114
  (78 shorter events, 1.2 us)
Async XLA Ops:
  0.6 33.1 %collective-permute-start = (bf16[32,128,128]{2,1,0:T(8,128)(2,1)}, bf16[32,128,128]{2,1,0:T(8,128)(2,1)S(1)}, u32[]{:S(2)}, u32[]{:S(2)}) collective-permute-start(bf16[32,128,128]{2,1,0:T(8,128)(2,1)} %bitcast.50), channel_id=1, source_target_pairs={{0,32},{32,64},{64,96},{96,0},{1,33},{33,65},{65,97},{97,1},{2,34}... | collective-permute-start | bytes 3145736 | tf_op jit(solution)/shard_map/ppermute | solution.py:20
  2.7 31.0 %collective-permute-start.1 = (bf16[32,128,128]{2,1,0:T(8,128)(2,1)}, bf16[32,128,128]{2,1,0:T(8,128)(2,1)}, u32[]{:S(2)}, u32[]{:S(2)}) collective-permute-start(bf16[32,128,128]{2,1,0:T(8,128)(2,1)} %bitcast.51), channel_id=1, source_target_pairs={{0,96},{32,0},{64,32},{96,64},{1,97},{33,1},{65,33},{97,65},{2,98}... | collective-permute-start | bytes 3145736 | tf_op jit(solution)/shard_map/ppermute | solution.py:20
  4.1 29.7 %collective-permute-start.2 = (bf16[32,128,128]{2,1,0:T(8,128)(2,1)}, bf16[32,128,128]{2,1,0:T(8,128)(2,1)}, u32[]{:S(2)}, u32[]{:S(2)}) collective-permute-start(bf16[32,128,128]{2,1,0:T(8,128)(2,1)} %bitcast.52), channel_id=1, source_target_pairs={{0,2},{2,4},{4,6},{6,0},{1,3},{3,5},{5,7},{7,1},{8,10},{10,12},{12... | collective-permute-start | bytes 3145736 | tf_op jit(solution)/shard_map/ppermute | solution.py:20
  5.8 27.9 %collective-permute-start.3 = (bf16[32,128,128]{2,1,0:T(8,128)(2,1)}, bf16[32,128,128]{2,1,0:T(8,128)(2,1)}, u32[]{:S(2)}, u32[]{:S(2)}) collective-permute-start(bf16[32,128,128]{2,1,0:T(8,128)(2,1)} %bitcast.53), channel_id=1, source_target_pairs={{0,6},{2,0},{4,2},{6,4},{1,7},{3,1},{5,3},{7,5},{8,14},{10,8},{12,... | collective-permute-start | bytes 3145736 | tf_op jit(solution)/shard_map/ppermute | solution.py:20
  8.0 25.8 %collective-permute-start.4 = (bf16[32,128,128]{2,1,0:T(8,128)(2,1)}, bf16[32,128,128]{2,1,0:T(8,128)(2,1)}, u32[]{:S(2)}, u32[]{:S(2)}) collective-permute-start(bf16[32,128,128]{2,1,0:T(8,128)(2,1)} %bitcast.54), channel_id=1, source_target_pairs={{0,16},{16,0},{1,17},{17,1},{2,18},{18,2},{3,19},{19,3},{4,20},{20... | collective-permute-start | bytes 3145736 | tf_op jit(solution)/shard_map/ppermute | solution.py:20
  12.4 4.0 %copy-start.11 = (s32[1,1,128,2]{2,3,1,0:T(2,128)S(1)}, s32[1,1,128,2]{2,3,1,0:T(2,128)}, u32[]{:S(2)}) copy-start(s32[1,1,128,2]{2,3,1,0:T(2,128)} %param.9) | copy-start | bytes 3076
  12.4 4.8 %copy-start.14 = (s32[1,1,128,1]{2,3,1,0:T(1,128)S(1)}, s32[1,1,128,1]{2,3,1,0:T(1,128)}, u32[]{:S(2)}) copy-start(s32[1,1,128,1]{2,3,1,0:T(1,128)} %param.10) | copy-start | bytes 1540
  12.4 43.9 %all-to-all-start = ((bf16[64,128,128]{2,1,0:T(8,128)(2,1)}), bf16[64,128,128]{2,1,0:T(8,128)(2,1)S(1)}, u32[]{:S(2)}, u32[]{:S(2)}) async-start(bf16[64,128,128]{2,1,0:T(8,128)(2,1)} %pad_maximum_fusion), calls=%async_computation | async-start | bytes 4194304 | tf_op jit(solution)/shard_map/all_to_all | solution.py:216
  33.7 6.9 %copy-start.16 = (s32[128]{0:T(128)S(1)}, s32[128]{0:T(128)}, u32[]{:S(2)}) copy-start(s32[128]{0:T(128)} %convert_reduce_fusion.2.ranks) | copy-start | bytes 1540
  33.7 6.9 %copy-start.12 = (s32[1,2,16]{2,1,0:T(2,128)S(1)}, s32[1,2,16]{2,1,0:T(2,128)}, u32[]{:S(2)}) copy-start(s32[1,2,16]{2,1,0:T(2,128)} %param.13) | copy-start | bytes 388
  33.7 7.0 %copy-start.13 = (s32[1,1,128]{2,1,0:T(1,128)S(1)}, s32[1,1,128]{2,1,0:T(1,128)}, u32[]{:S(2)}) copy-start(s32[1,1,128]{2,1,0:T(1,128)} %param.11) | copy-start | bytes 1540
  33.7 7.0 %copy-start.15 = (s32[1,1,128,1]{2,3,1,0:T(1,128)S(1)}, s32[1,1,128,1]{2,3,1,0:T(1,128)}, u32[]{:S(2)}) copy-start(s32[1,1,128,1]{2,3,1,0:T(1,128)} %param.10) | copy-start | bytes 1540
  33.7 22.5 %copy-start.2 = (bf16[32,128,128]{2,1,0:T(8,128)(2,1)}, bf16[32,128,128]{2,1,0:T(8,128)(2,1)S(1)}, u32[]{:S(2)}) copy-start(bf16[32,128,128]{2,1,0:T(8,128)(2,1)S(1)} %collective-permute-done.refs_12_) | copy-start | bytes 3145732
  33.8 28.1 %collective-permute-start.5 = (bf16[32,128,128]{2,1,0:T(8,128)(2,1)}, bf16[32,128,128]{2,1,0:T(8,128)(2,1)}, u32[]{:S(2)}, u32[]{:S(2)}) collective-permute-start(bf16[32,128,128]{2,1,0:T(8,128)(2,1)} %collective-permute-done.4.refs_16_), channel_id=1, source_target_pairs={{0,32},{32,64},{64,96},{96,0},{1,33},{33,65},{65,97},{97,1},{2,34}... | collective-permute-start | bytes 3145736 | tf_op jit(solution)/shard_map/ppermute | solution.py:20
  36.0 20.2 %collective-permute-start.7 = (bf16[16,128,128]{2,1,0:T(8,128)(2,1)}, bf16[16,128,128]{2,1,0:T(8,128)(2,1)}, u32[]{:S(2)}, u32[]{:S(2)}) collective-permute-start(bf16[16,128,128]{2,1,0:T(8,128)(2,1)} %slice.33), channel_id=1, source_target_pairs={{0,2},{2,4},{4,6},{6,0},{1,3},{3,5},{5,7},{7,1},{8,10},{10,12},{12... | collective-permute-start | bytes 1572872 | tf_op jit(solution)/shard_map/ppermute | solution.py:20
  37.9 18.3 %collective-permute-start.8 = (bf16[16,128,128]{2,1,0:T(8,128)(2,1)}, bf16[16,128,128]{2,1,0:T(8,128)(2,1)}, u32[]{:S(2)}, u32[]{:S(2)}) collective-permute-start(bf16[16,128,128]{2,1,0:T(8,128)(2,1)} %slice.34), channel_id=1, source_target_pairs={{0,6},{2,0},{4,2},{6,4},{1,7},{3,1},{5,3},{7,5},{8,14},{10,8},{12,... | collective-permute-start | bytes 1572872 | tf_op jit(solution)/shard_map/ppermute | solution.py:20
  40.9 42.5 %collective-permute-start.6 = (bf16[32,128,128]{2,1,0:T(8,128)(2,1)}, bf16[32,128,128]{2,1,0:T(8,128)(2,1)}, u32[]{:S(2)}, u32[]{:S(2)}) collective-permute-start(bf16[32,128,128]{2,1,0:T(8,128)(2,1)} %collective-permute-done.4.refs_16_), channel_id=1, source_target_pairs={{0,96},{32,0},{64,32},{96,64},{1,97},{33,1},{65,33},{97,65},{2,98}... | collective-permute-start | bytes 3145736 | tf_op jit(solution)/shard_map/ppermute | solution.py:20
  56.2 2.9 %copy-start.3 = (bf16[32,128,128]{2,1,0:T(8,128)(2,1)S(1)}, bf16[32,128,128]{2,1,0:T(8,128)(2,1)}, u32[]{:S(2)}) copy-start(bf16[32,128,128]{2,1,0:T(8,128)(2,1)} %copy-done.2) | copy-start | bytes 3145732
  56.3 27.2 %copy-start.1 = (bf16[32,128,128]{2,1,0:T(8,128)(2,1)}, bf16[32,128,128]{2,1,0:T(8,128)(2,1)S(1)}, u32[]{:S(2)}) copy-start(bf16[32,128,128]{2,1,0:T(8,128)(2,1)S(1)} %constant_dynamic-slice_fusion.1.refs_3_) | copy-start | bytes 3145732
  56.4 27.1 %collective-permute-start.9 = (bf16[32,128,128]{2,1,0:T(8,128)(2,1)S(1)}, bf16[32,128,128]{2,1,0:T(8,128)(2,1)S(1)}, u32[]{:S(2)}, u32[]{:S(2)}) collective-permute-start(bf16[32,128,128]{2,1,0:T(8,128)(2,1)S(1)} %constant_dynamic-slice_fusion.1.refs_3_), channel_id=1, source_target_pairs={{0,2},{2,4},{4,6},{6,0},{1,3},{3,5},{5,7},{7,1},{8,10},{10,12},{12... | collective-permute-start | bytes 3145736 | tf_op jit(solution)/shard_map/ppermute | solution.py:20
  56.4 27.1 %collective-permute-start.10 = (bf16[32,128,128]{2,1,0:T(8,128)(2,1)S(1)}, bf16[32,128,128]{2,1,0:T(8,128)(2,1)S(1)}, u32[]{:S(2)}, u32[]{:S(2)}) collective-permute-start(bf16[32,128,128]{2,1,0:T(8,128)(2,1)S(1)} %constant_dynamic-slice_fusion.1.refs_3_), channel_id=1, source_target_pairs={{0,6},{2,0},{4,2},{6,4},{1,7},{3,1},{5,3},{7,5},{8,14},{10,8},{12,... | collective-permute-start | bytes 3145736 | tf_op jit(solution)/shard_map/ppermute | solution.py:20
  59.9 23.6 %collective-permute-start.11 = (bf16[16,128,128]{2,1,0:T(8,128)(2,1)}, bf16[16,128,128]{2,1,0:T(8,128)(2,1)}, u32[]{:S(2)}, u32[]{:S(2)}) collective-permute-start(bf16[16,128,128]{2,1,0:T(8,128)(2,1)} %slice.35), channel_id=1, source_target_pairs={{0,32},{32,64},{64,96},{96,0},{1,33},{33,65},{65,97},{97,1},{2,34}... | collective-permute-start | bytes 1572872 | tf_op jit(solution)/shard_map/ppermute | solution.py:20
  61.9 21.6 %collective-permute-start.12 = (bf16[16,128,128]{2,1,0:T(8,128)(2,1)}, bf16[16,128,128]{2,1,0:T(8,128)(2,1)}, u32[]{:S(2)}, u32[]{:S(2)}) collective-permute-start(bf16[16,128,128]{2,1,0:T(8,128)(2,1)} %slice.36), channel_id=1, source_target_pairs={{0,96},{32,0},{64,32},{96,64},{1,97},{33,1},{65,33},{97,65},{2,98}... | collective-permute-start | bytes 1572872 | tf_op jit(solution)/shard_map/ppermute | solution.py:20
  83.5 11.1 %copy-start.5 = (bf16[32,128,128]{2,1,0:T(8,128)(2,1)}, bf16[32,128,128]{2,1,0:T(8,128)(2,1)S(1)}, u32[]{:S(2)}) copy-start(bf16[32,128,128]{2,1,0:T(8,128)(2,1)S(1)} %collective-permute-done.9.refs_4_) | copy-start | bytes 3145732
  83.5 12.7 %copy-start.6 = (bf16[32,128,128]{2,1,0:T(8,128)(2,1)}, bf16[32,128,128]{2,1,0:T(8,128)(2,1)S(1)}, u32[]{:S(2)}) copy-start(bf16[32,128,128]{2,1,0:T(8,128)(2,1)S(1)} %collective-permute-done.10.refs_5_) | copy-start | bytes 3145732
  83.5 65.9 %all-to-all-start.2 = ((bf16[128,128,128]{2,1,0:T(8,128)(2,1)}), bf16[128,128,128]{2,1,0:T(8,128)(2,1)}, u32[]{:S(2)}, u32[]{:S(2)}) async-start(bf16[128,128,128]{2,1,0:T(8,128)(2,1)} %get-tuple-element.45), calls=%async_computation.2 | async-start | bytes 8388608 | tf_op jit(solution)/shard_map/all_to_all | solution.py:243
  90.7 58.1 %collective-permute-start.13 = (bf16[16,128,128]{2,1,0:T(8,128)(2,1)S(1)}, bf16[16,128,128]{2,1,0:T(8,128)(2,1)}, u32[]{:S(2)}, u32[]{:S(2)}) collective-permute-start(bf16[16,128,128]{2,1,0:T(8,128)(2,1)S(1)} %slice.39), channel_id=1, source_target_pairs={{0,32},{32,64},{64,96},{96,0},{1,33},{33,65},{65,97},{97,1},{2,34}... | collective-permute-start | bytes 1572872 | tf_op jit(solution)/shard_map/ppermute | solution.py:20
  93.2 55.6 %collective-permute-start.14 = (bf16[16,128,128]{2,1,0:T(8,128)(2,1)S(1)}, bf16[16,128,128]{2,1,0:T(8,128)(2,1)}, u32[]{:S(2)}, u32[]{:S(2)}) collective-permute-start(bf16[16,128,128]{2,1,0:T(8,128)(2,1)S(1)} %slice.40), channel_id=1, source_target_pairs={{0,96},{32,0},{64,32},{96,64},{1,97},{33,1},{65,33},{97,65},{2,98}... | collective-permute-start | bytes 1572872 | tf_op jit(solution)/shard_map/ppermute | solution.py:20
  94.7 54.7 %collective-permute-start.15 = (bf16[16,128,128]{2,1,0:T(8,128)(2,1)S(1)}, bf16[16,128,128]{2,1,0:T(8,128)(2,1)S(1)}, u32[]{:S(2)}, u32[]{:S(2)}) collective-permute-start(bf16[16,128,128]{2,1,0:T(8,128)(2,1)S(1)} %slice.41), channel_id=1, source_target_pairs={{0,2},{2,4},{4,6},{6,0},{1,3},{3,5},{5,7},{7,1},{8,10},{10,12},{12... | collective-permute-start | bytes 1572872 | tf_op jit(solution)/shard_map/ppermute | solution.py:20
  96.3 63.2 %copy-start.4 = (bf16[32,128,128]{2,1,0:T(8,128)(2,1)S(1)}, bf16[32,128,128]{2,1,0:T(8,128)(2,1)}, u32[]{:S(2)}) copy-start(bf16[32,128,128]{2,1,0:T(8,128)(2,1)} %copy-done.2) | copy-start | bytes 3145732
  96.3 68.1 %copy-start = (bf16[1,2,16,128,128]{4,3,2,1,0:T(8,128)(2,1)S(1)}, bf16[1,2,16,128,128]{4,3,2,1,0:T(8,128)(2,1)}, u32[]{:S(2)}) copy-start(bf16[1,2,16,128,128]{4,3,2,1,0:T(8,128)(2,1)} %param.12) | copy-start | bytes 3145732
  96.3 53.1 %collective-permute-start.16 = (bf16[16,128,128]{2,1,0:T(8,128)(2,1)S(1)}, bf16[16,128,128]{2,1,0:T(8,128)(2,1)S(1)}, u32[]{:S(2)}, u32[]{:S(2)}) collective-permute-start(bf16[16,128,128]{2,1,0:T(8,128)(2,1)S(1)} %slice.42), channel_id=1, source_target_pairs={{0,6},{2,0},{4,2},{6,4},{1,7},{3,1},{5,3},{7,5},{8,14},{10,8},{12,... | collective-permute-start | bytes 1572872 | tf_op jit(solution)/shard_map/ppermute | solution.py:20
  149.4 0.8 copy-start.9
  149.4 1.0 copy-start.10
  150.4 59.8 %all-to-all-start.3 = ((bf16[128,128,128]{2,1,0:T(8,128)(2,1)}), bf16[128,128,128]{2,1,0:T(8,128)(2,1)}, u32[]{:S(2)}, u32[]{:S(2)}) async-start(bf16[128,128,128]{2,1,0:T(8,128)(2,1)} %get-tuple-element.52), calls=%async_computation.3 | async-start | bytes 8388608 | tf_op jit(solution)/shard_map/all_to_all | solution.py:250
  159.5 4.9 %collective-permute-start.18 = (bf16[32,128,128]{2,1,0:T(8,128)(2,1)S(1)}, bf16[32,128,128]{2,1,0:T(8,128)(2,1)S(1)}, u32[]{:S(2)}, u32[]{:S(2)}) collective-permute-start(bf16[32,128,128]{2,1,0:T(8,128)(2,1)S(1)} %copy-done.4), channel_id=1, source_target_pairs={{0,8},{8,0},{1,9},{9,1},{2,10},{10,2},{3,11},{11,3},{4,12},{12,4},... | collective-permute-start | bytes 3145736 | tf_op jit(solution)/shard_map/ppermute | solution.py:20
  160.7 4.1 %collective-permute-start.19 = (bf16[32,128,128]{2,1,0:T(8,128)(2,1)}, bf16[32,128,128]{2,1,0:T(8,128)(2,1)}, u32[]{:S(2)}, u32[]{:S(2)}) collective-permute-start(bf16[32,128,128]{2,1,0:T(8,128)(2,1)} %collective-permute-done.1.refs_14_), channel_id=1, source_target_pairs={{0,8},{8,0},{1,9},{9,1},{2,10},{10,2},{3,11},{11,3},{4,12},{12,4},... | collective-permute-start | bytes 3145736 | tf_op jit(solution)/shard_map/ppermute | solution.py:20
  160.7 5.6 %collective-permute-start.20 = (bf16[32,128,128]{2,1,0:T(8,128)(2,1)}, bf16[32,128,128]{2,1,0:T(8,128)(2,1)}, u32[]{:S(2)}, u32[]{:S(2)}) collective-permute-start(bf16[32,128,128]{2,1,0:T(8,128)(2,1)} %collective-permute-done.4.refs_16_), channel_id=1, source_target_pairs={{0,8},{8,0},{1,9},{9,1},{2,10},{10,2},{3,11},{11,3},{4,12},{12,4},... | collective-permute-start | bytes 3145736 | tf_op jit(solution)/shard_map/ppermute | solution.py:20
  161.3 19.1 %collective-permute-start.21 = (bf16[32,128,128]{2,1,0:T(8,128)(2,1)}, bf16[32,128,128]{2,1,0:T(8,128)(2,1)}, u32[]{:S(2)}, u32[]{:S(2)}) collective-permute-start(bf16[32,128,128]{2,1,0:T(8,128)(2,1)} %collective-permute-done.5.refs_18_), channel_id=1, source_target_pairs={{0,8},{8,0},{1,9},{9,1},{2,10},{10,2},{3,11},{11,3},{4,12},{12,4},... | collective-permute-start | bytes 3145736 | tf_op jit(solution)/shard_map/ppermute | solution.py:20
  161.3 19.1 %collective-permute-start.22 = (bf16[32,128,128]{2,1,0:T(8,128)(2,1)}, bf16[32,128,128]{2,1,0:T(8,128)(2,1)}, u32[]{:S(2)}, u32[]{:S(2)}) collective-permute-start(bf16[32,128,128]{2,1,0:T(8,128)(2,1)} %collective-permute-done.6.refs_20_), channel_id=1, source_target_pairs={{0,8},{8,0},{1,9},{9,1},{2,10},{10,2},{3,11},{11,3},{4,12},{12,4},... | collective-permute-start | bytes 3145736 | tf_op jit(solution)/shard_map/ppermute | solution.py:20
  164.4 16.0 %copy-start.7 = (bf16[32,128,128]{2,1,0:T(8,128)(2,1)}, bf16[32,128,128]{2,1,0:T(8,128)(2,1)S(1)}, u32[]{:S(2)}) copy-start(bf16[32,128,128]{2,1,0:T(8,128)(2,1)S(1)} %collective-permute-done.18.refs_13_) | copy-start | bytes 3145732
  164.4 16.0 %collective-permute-start.17 = (bf16[32,128,128]{2,1,0:T(8,128)(2,1)S(1)}, bf16[32,128,128]{2,1,0:T(8,128)(2,1)S(1)}, u32[]{:S(2)}, u32[]{:S(2)}) collective-permute-start(bf16[32,128,128]{2,1,0:T(8,128)(2,1)S(1)} %bitcast.58), channel_id=1, source_target_pairs={{0,8},{8,0},{1,9},{9,1},{2,10},{10,2},{3,11},{11,3},{4,12},{12,4},... | collective-permute-start | bytes 3145736 | tf_op jit(solution)/shard_map/ppermute | solution.py:20
  164.8 6.7 %collective-permute-start.23 = (bf16[16,128,128]{2,1,0:T(8,128)(2,1)}, bf16[16,128,128]{2,1,0:T(8,128)(2,1)}, u32[]{:S(2)}, u32[]{:S(2)}) collective-permute-start(bf16[16,128,128]{2,1,0:T(8,128)(2,1)} %collective-permute-done.11.refs_22_), channel_id=1, source_target_pairs={{0,8},{8,0},{1,9},{9,1},{2,10},{10,2},{3,11},{11,3},{4,12},{12,4},... | collective-permute-start | bytes 1572872 | tf_op jit(solution)/shard_map/ppermute | solution.py:20
  166.3 6.0 %collective-permute-start.24 = (bf16[16,128,128]{2,1,0:T(8,128)(2,1)}, bf16[16,128,128]{2,1,0:T(8,128)(2,1)}, u32[]{:S(2)}, u32[]{:S(2)}) collective-permute-start(bf16[16,128,128]{2,1,0:T(8,128)(2,1)} %collective-permute-done.12.refs_24_), channel_id=1, source_target_pairs={{0,8},{8,0},{1,9},{9,1},{2,10},{10,2},{3,11},{11,3},{4,12},{12,4},... | collective-permute-start | bytes 1572872 | tf_op jit(solution)/shard_map/ppermute | solution.py:20
  171.5 8.9 %collective-permute-start.25 = (bf16[16,128,128]{2,1,0:T(8,128)(2,1)}, bf16[16,128,128]{2,1,0:T(8,128)(2,1)}, u32[]{:S(2)}, u32[]{:S(2)}) collective-permute-start(bf16[16,128,128]{2,1,0:T(8,128)(2,1)} %collective-permute-done.13.refs_26_), channel_id=1, source_target_pairs={{0,8},{8,0},{1,9},{9,1},{2,10},{10,2},{3,11},{11,3},{4,12},{12,4},... | collective-permute-start | bytes 1572872 | tf_op jit(solution)/shard_map/ppermute | solution.py:20
  172.3 8.1 %collective-permute-start.26 = (bf16[16,128,128]{2,1,0:T(8,128)(2,1)}, bf16[16,128,128]{2,1,0:T(8,128)(2,1)}, u32[]{:S(2)}, u32[]{:S(2)}) collective-permute-start(bf16[16,128,128]{2,1,0:T(8,128)(2,1)} %collective-permute-done.14.refs_28_), channel_id=1, source_target_pairs={{0,8},{8,0},{1,9},{9,1},{2,10},{10,2},{3,11},{11,3},{4,12},{12,4},... | collective-permute-start | bytes 1572872 | tf_op jit(solution)/shard_map/ppermute | solution.py:20
  180.4 1.1 copy-start.8

commit v5 on v4

--- a/solution.py
+++ b/solution.py
@@ -217,18 +217,19 @@
     y_low = shift(own, "yl", 1)
     x_behind, x_ahead = shift(own, "x", 1), shift(own, "x", -1)
     z_behind, z_ahead = shift(own, "z", 1), shift(own, "z", -1)
-    send0, send1 = pair_blocks(
-        basis_values[0, 0], potential[0], task_pairs[0, 0], owners, ranks, device_count
-    )
-
-    x_behind, x_ahead, z_behind, z_ahead, y_low, send0, send1 = lax.optimization_barrier(
-        (x_behind, x_ahead, z_behind, z_ahead, y_low, send0, send1)
+
+    x_behind, x_ahead, z_behind, z_ahead, y_low, basis = lax.optimization_barrier(
+        (x_behind, x_ahead, z_behind, z_ahead, y_low, basis_values)
     )
     z_far0, z_far1 = shift(z_behind[:half], "z", 1), shift(z_ahead[half:], "z", -1)
     x_behind2, x_ahead2 = shift(y_low, "x", 1), shift(y_low, "x", -1)
 
-    z_far0, z_far1, y_both, numbers, x_behind3, x_ahead3 = lax.optimization_barrier(
-        (z_far0, z_far1, y_both, numbers, x_behind, x_ahead)
+    send0, send1 = pair_blocks(
+        basis[0, 0], potential[0], task_pairs[0, 0], owners, ranks, device_count
+    )
+
+    z_far0, z_far1, y_both, numbers, x_behind3, x_ahead3, send0, send1 = lax.optimization_barrier(
+        (z_far0, z_far1, y_both, numbers, x_behind, x_ahead, send0, send1)
     )
     y_high = lax.dynamic_slice_in_dim(y_both, (1 - yh) * 2 * cell_rows, 2 * cell_rows, 0)
     z_behind2, z_ahead2 = shift(y_high, "z", 1), shift(y_high, "z", -1)

time: 216 us -> 217 us (level)
    ppermute x27, waiting for transfers between devices: 58 us -> 71.6 us  [shift(): lax.ppermute(value, axis, [(i, (i + step) % size) for i in range(size)])]
    all_to_all x1, waiting for transfers between devices: 12.9 us -> 0.01 us  [body(): y_both = lax.all_to_all(jnp.concatenate([own, own]), 'yh', 0, 0, tiled=True)]
  transfers between devices with their start and end apart: 30 -> 30, of which waited for: 8 -> 10; matrix products, arithmetic and copies ran while one was open for 9% -> 9% of each run, Pallas kernels for 17% -> 17%
where the time goes in v5:
time: 217 us; the launch traced here: 216 us
  waiting for transfers between devices  85.3 us (39%)
  starting transfers between devices  47.7 us (22%)
  Pallas kernels  40.5 us (19%)
  blocking collectives  20.4 us (9%)
  local copies, waits for them, and re-layouts  13.5 us (6%)
  other arithmetic  7.26 us (3%)
    ppermute x27, waiting for transfers between devices, shift(): lax.ppermute(value, axis, [(i, (i + step) % size) for i in range(size)])  71.6 us
    ppermute x27, starting transfers between devices, shift(): lax.ppermute(value, axis, [(i, (i + step) % size) for i in range(size)])  29.7 us
    all_to_all x1, blocking collectives, body(): lax.all_to_all(numbers[:, None, :], ALL, 0, 0, tiled=True)[:, 0, :]  20.4 us
    pallas_call x1, Pallas kernels, pair_blocks(): pl.pallas_call(pair_kernel, out_shape=[jax.ShapeDtypeStruct((device_count...  15.8 us
    pallas_call x1, Pallas kernels, square_sum(): pl.pallas_call(functools.partial(square_kernel, tuple(places), cell_rows)...  15.1 us
    all_to_all x1, waiting for transfers between devices, body(): arrived1 = lax.all_to_all(send1, ALL, 0, 0, tiled=True)  13.6 us
    pallas_call x2, Pallas kernels, fock_sum(): pl.pallas_call(fock_kernel, out_shape=jax.ShapeDtypeStruct((slot_count, w...  9.61 us
    all_to_all x1, starting transfers between devices, body(): arrived1 = lax.all_to_all(send1, ALL, 0, 0, tiled=True)  8.14 us
  transfers between devices with their start and end apart: 30, of which 10 were waited for; matrix products, arithmetic and copies ran while one was open for 9% of the time, Pallas kernels for 17%

profile of v5, /device:TPU:1, one launch (start us, length us, event | category | flops | bytes accessed | tf_op | source)
XLA Modules:
  0.0 216.0 jit_solution(13232216296024764114)
XLA Ops:
  0.6 2.1 collective-permute-start
  2.7 1.4 collective-permute-start.1
  4.1 1.8 collective-permute-start.2
  5.8 2.1 collective-permute-start.3
  8.0 1.3 collective-permute-start.4
  9.3 3.1 %pad_maximum_fusion = bf16[64,128,128]{2,1,0:T(8,128)(2,1)} fusion(bf16[32,128,128]{2,1,0:T(8,128)(2,1)} %bitcast.55), kind=kLoop, calls=%fused_computation | loop fusion | flops 1048576 | bytes 3145728 | tf_op jit(solution)/shard_map/concatenate | solution.py:216
  12.4 4.0 %all-to-all-start = ((bf16[64,128,128]{2,1,0:T(8,128)(2,1)}), bf16[64,128,128]{2,1,0:T(8,128)(2,1)S(1)}, u32[]{:S(2)}, u32[]{:S(2)}) async-start(bf16[64,128,128]{2,1,0:T(8,128)(2,1)} %pad_maximum_fusion), calls=%async_computation | async-start | bytes 4194304 | tf_op jit(solution)/shard_map/all_to_all | solution.py:216
  16.4 0.2 convert_reduce_fusion.2.ranks
  16.6 0.1 select_reduce_fusion.4
  16.8 0.1 copy.27
  17.0 0.7 reshape_squeeze.3.pairs
  17.8 8.9 %collective-permute-done.refs_12_ = bf16[32,128,128]{2,1,0:T(8,128)(2,1)S(1)} collective-permute-done((bf16[32,128,128]{2,1,0:T(8,128)(2,1)}, bf16[32,128,128]{2,1,0:T(8,128)(2,1)S(1)}, u32[]{:S(2)}, u32[]{:S(2)}) %collective-permute-start) | collective-permute-done | bytes 1048608 | tf_op jit(solution)/shard_map/ppermute | solution.py:20
  26.8 3.8 %collective-permute-done.2.refs_1_ = bf16[32,128,128]{2,1,0:T(8,128)(2,1)} collective-permute-done((bf16[32,128,128]{2,1,0:T(8,128)(2,1)}, bf16[32,128,128]{2,1,0:T(8,128)(2,1)}, u32[]{:S(2)}, u32[]{:S(2)}) %collective-permute-start.2) | collective-permute-done | bytes 1048608 | tf_op jit(solution)/shard_map/ppermute | solution.py:20
  30.6 0.9 collective-permute-done.4.refs_16_
  31.4 2.7 %collective-permute-start.6 = (bf16[32,128,128]{2,1,0:T(8,128)(2,1)}, bf16[32,128,128]{2,1,0:T(8,128)(2,1)}, u32[]{:S(2)}, u32[]{:S(2)}) collective-permute-start(bf16[32,128,128]{2,1,0:T(8,128)(2,1)} %collective-permute-done.4.refs_16_), channel_id=1, source_target_pairs={{0,96},{32,0},{64,32},{96,64},{1,97},{33,1},{65,33},{97,65},{2,98}... | collective-permute-start | bytes 3145736 | tf_op jit(solution)/shard_map/ppermute | solution.py:20
  34.1 1.9 slice.33
  36.0 1.9 slice.34
  37.9 2.7 %collective-permute-start.8 = (bf16[16,128,128]{2,1,0:T(8,128)(2,1)}, bf16[16,128,128]{2,1,0:T(8,128)(2,1)}, u32[]{:S(2)}, u32[]{:S(2)}) collective-permute-start(bf16[16,128,128]{2,1,0:T(8,128)(2,1)} %slice.34), channel_id=1, source_target_pairs={{0,6},{2,0},{4,2},{6,4},{1,7},{3,1},{5,3},{7,5},{8,14},{10,8},{12,... | collective-permute-start | bytes 1572872 | tf_op jit(solution)/shard_map/ppermute | solution.py:20
  40.5 15.8 %pair_blocks.1 = (bf16[128,128,128]{2,1,0:T(8,128)(2,1)}, bf16[128,128,128]{2,1,0:T(8,128)(2,1)}) custom-call(s32[256]{0:T(256)} %reshape_squeeze.3.pairs, s32[128]{0:T(128)} %bitcast.68, s32[128]{0:T(128)} %copy-done.15, bf16[16,128,1024]{2,1,0:T(8,128)(2,1)} %bitcast.71, f32[1,1024]{1,0:T(1,128)} %bitcast.72), custom_call_target="tpu_custom_call" | custom-call | flops 8589934592 | bytes 8388608 | tf_op jit(solution)/shard_map/pair_blocks/pallas_call | solution.py:63
  56.6 2.7 %collective-permute-start.10 = (bf16[32,128,128]{2,1,0:T(8,128)(2,1)S(1)}, bf16[32,128,128]{2,1,0:T(8,128)(2,1)S(1)}, u32[]{:S(2)}, u32[]{:S(2)}) collective-permute-start(bf16[32,128,128]{2,1,0:T(8,128)(2,1)S(1)} %constant_dynamic-slice_fusion.1.refs_3_), channel_id=1, source_target_pairs={{0,6},{2,0},{4,2},{6,4},{1,7},{3,1},{5,3},{7,5},{8,14},{10,8},{12,... | collective-permute-start | bytes 3145736 | tf_op jit(solution)/shard_map/ppermute | solution.py:20
  59.3 0.8 slice.35
  60.1 1.9 slice.36
  62.0 2.7 %collective-permute-start.12 = (bf16[16,128,128]{2,1,0:T(8,128)(2,1)}, bf16[16,128,128]{2,1,0:T(8,128)(2,1)}, u32[]{:S(2)}, u32[]{:S(2)}) collective-permute-start(bf16[16,128,128]{2,1,0:T(8,128)(2,1)} %slice.36), channel_id=1, source_target_pairs={{0,96},{32,0},{64,32},{96,64},{1,97},{33,1},{65,33},{97,65},{2,98}... | collective-permute-start | bytes 1572872 | tf_op jit(solution)/shard_map/ppermute | solution.py:20
  64.8 20.4 %all_to_all.20 = s32[128,1,34]{2,1,0:T(1,128)S(1)} all-to-all(s32[128,1,34]{2,1,0:T(1,128)S(1)} %bitcast.63), channel_id=1, replica_groups=mesh['x'=4,'yl'=2,'c'=2,'z'=4,'yh'=2] {'x','yl','c','z','yh'}, dimensions={0} | all-to-all | bytes 34816 | tf_op jit(solution)/shard_map/all_to_all | solution.py:237
  85.3 5.8 %all-to-all-start.2 = ((bf16[128,128,128]{2,1,0:T(8,128)(2,1)}), bf16[128,128,128]{2,1,0:T(8,128)(2,1)}, u32[]{:S(2)}, u32[]{:S(2)}) async-start(bf16[128,128,128]{2,1,0:T(8,128)(2,1)} %get-tuple-element.47), calls=%async_computation.2 | async-start | bytes 8388608 | tf_op jit(solution)/shard_map/all_to_all | solution.py:244
  91.1 1.1 slice.39
  92.2 1.5 collective-permute-start.13
  93.7 1.1 slice.40
  94.8 1.4 collective-permute-start.14
  96.2 1.6 collective-permute-start.15
  97.8 1.8 collective-permute-start.16
  99.7 50.7 %collective-permute-done.13.refs_26_ = bf16[16,128,128]{2,1,0:T(8,128)(2,1)} collective-permute-done((bf16[16,128,128]{2,1,0:T(8,128)(2,1)S(1)}, bf16[16,128,128]{2,1,0:T(8,128)(2,1)}, u32[]{:S(2)}, u32[]{:S(2)}) %collective-permute-start.13) | collective-permute-done | bytes 524320 | tf_op jit(solution)/shard_map/ppermute | solution.py:20
  150.3 0.6 collective-permute-done.15.refs_8_
  150.9 0.8 copy-done.9
  151.7 0.2 copy-done.10
  151.9 8.1 %all-to-all-start.3 = ((bf16[128,128,128]{2,1,0:T(8,128)(2,1)}), bf16[128,128,128]{2,1,0:T(8,128)(2,1)}, u32[]{:S(2)}, u32[]{:S(2)}) async-start(bf16[128,128,128]{2,1,0:T(8,128)(2,1)} %get-tuple-element.54), calls=%async_computation.3 | async-start | bytes 8388608 | tf_op jit(solution)/shard_map/all_to_all | solution.py:251
  160.4 0.1 stack.123
  160.5 0.5 broadcast_multiply_fusion.where
  161.0 1.1 collective-permute-start.18
  162.2 0.5 collective-permute-start.20
  162.8 0.5 collective-permute-start.22
  163.7 0.6 select_reduce_fusion
  164.4 1.5 collective-permute-done.18.refs_13_
  165.9 0.4 collective-permute-start.17
  166.3 0.4 collective-permute-start.23
  166.7 1.1 collective-permute-done.20.refs_17_
  167.8 0.4 collective-permute-start.24
  168.2 0.2 slice_reduce_fusion
  168.3 0.2 copy.33
  168.5 0.7 select_n.208.picks
  169.3 3.8 %collective-permute-done.23.refs_23_ = bf16[16,128,128]{2,1,0:T(8,128)(2,1)} collective-permute-done((bf16[16,128,128]{2,1,0:T(8,128)(2,1)}, bf16[16,128,128]{2,1,0:T(8,128)(2,1)}, u32[]{:S(2)}, u32[]{:S(2)}) %collective-permute-start.23) | collective-permute-done | bytes 524320 | tf_op jit(solution)/shard_map/ppermute | solution.py:20
  173.0 0.4 collective-permute-start.25
  173.4 0.4 collective-permute-done.24.refs_25_
  173.8 0.4 collective-permute-start.26
  174.2 0.7 convert_reduce_fusion.3
  174.8 0.2 convert_reduce_fusion.1
  175.0 0.7 select_reduce_fusion.2.order
  175.7 0.2 convert_reduce_fusion
  175.9 0.7 select_reduce_fusion.1.order
  176.6 5.4 %fock_sum.2.refs_0_ = f32[32,128,128]{2,1,0:T(8,128)} custom-call(s32[128]{0:T(128)} %select_reduce_fusion.1.order, s32[33]{0:T(128)} %get-tuple-element.70.starts, bf16[128,128,128]{2,1,0:T(8,128)(2,1)} %all-to-all-done.2.refs_0_), custom_call_target="tpu_custom_call" | custom-call | flops 2097152 | bytes 4194304 | tf_op jit(solution)/shard_map/fock_sum/pallas_call | solution.py:114
  182.0 1.0 copy-done.8
  183.0 15.1 %square_sum.1 = bf16[32,128,128]{2,1,0:T(8,128)(2,1)} custom-call(s32[30]{0:T(128)} %broadcast_multiply_fusion.where, s32[512]{0:T(512)} %select_n.208.picks, bf16[32,128,128]{2,1,0:T(8,128)(2,1)} %bitcast.56, bf16[32,128,128]{2,1,0:T(8,128)(2,1)} %collective-permute-done.2.refs_1_, bf16[32,128,128]{2,1,0:T(8,128)(2,1)} %collective-permute-done.3.refs_2_, ...), custom_call_target="tpu_custom_call" | custom-call | flops 2147483648 | bytes 25165824 | tf_op jit(solution)/shard_map/square_sum/pallas_call | solution.py:167
  198.1 13.6 %all-to-all-done.3.refs_1_ = bf16[128,128,128]{2,1,0:T(8,128)(2,1)} async-done(((bf16[128,128,128]{2,1,0:T(8,128)(2,1)}), bf16[128,128,128]{2,1,0:T(8,128)(2,1)}, u32[]{:S(2)}, u32[]{:S(2)}) %all-to-all-start.3) | async-done | bytes 4194336 | tf_op jit(solution)/shard_map/all_to_all | solution.py:251
  211.7 4.2 %fock_sum.3 = bf16[32,128,128]{2,1,0:T(8,128)(2,1)} custom-call(s32[128]{0:T(128)} %select_reduce_fusion.2.order, s32[33]{0:T(128)} %get-tuple-element.71.starts, f32[32,128,128]{2,1,0:T(8,128)} %fock_sum.2.refs_0_, bf16[128,128,128]{2,1,0:T(8,128)(2,1)} %all-to-all-done.3.refs_1_), custom_call_target="tpu_custom_call" | custom-call | flops 2097152 | bytes 4194304 | tf_op jit(solution)/shard_map/fock_sum/pallas_call | solution.py:114
  (76 shorter events, 1.3 us)
Async XLA Ops:
  0.6 26.1 %collective-permute-start = (bf16[32,128,128]{2,1,0:T(8,128)(2,1)}, bf16[32,128,128]{2,1,0:T(8,128)(2,1)S(1)}, u32[]{:S(2)}, u32[]{:S(2)}) collective-permute-start(bf16[32,128,128]{2,1,0:T(8,128)(2,1)} %bitcast.50), channel_id=1, source_target_pairs={{0,32},{32,64},{64,96},{96,0},{1,33},{33,65},{65,97},{97,1},{2,34}... | collective-permute-start | bytes 3145736 | tf_op jit(solution)/shard_map/ppermute | solution.py:20
  2.7 24.0 %collective-permute-start.1 = (bf16[32,128,128]{2,1,0:T(8,128)(2,1)}, bf16[32,128,128]{2,1,0:T(8,128)(2,1)}, u32[]{:S(2)}, u32[]{:S(2)}) collective-permute-start(bf16[32,128,128]{2,1,0:T(8,128)(2,1)} %bitcast.51), channel_id=1, source_target_pairs={{0,96},{32,0},{64,32},{96,64},{1,97},{33,1},{65,33},{97,65},{2,98}... | collective-permute-start | bytes 3145736 | tf_op jit(solution)/shard_map/ppermute | solution.py:20
  4.1 26.5 %collective-permute-start.2 = (bf16[32,128,128]{2,1,0:T(8,128)(2,1)}, bf16[32,128,128]{2,1,0:T(8,128)(2,1)}, u32[]{:S(2)}, u32[]{:S(2)}) collective-permute-start(bf16[32,128,128]{2,1,0:T(8,128)(2,1)} %bitcast.52), channel_id=1, source_target_pairs={{0,2},{2,4},{4,6},{6,0},{1,3},{3,5},{5,7},{7,1},{8,10},{10,12},{12... | collective-permute-start | bytes 3145736 | tf_op jit(solution)/shard_map/ppermute | solution.py:20
  5.8 24.7 %collective-permute-start.3 = (bf16[32,128,128]{2,1,0:T(8,128)(2,1)}, bf16[32,128,128]{2,1,0:T(8,128)(2,1)}, u32[]{:S(2)}, u32[]{:S(2)}) collective-permute-start(bf16[32,128,128]{2,1,0:T(8,128)(2,1)} %bitcast.53), channel_id=1, source_target_pairs={{0,6},{2,0},{4,2},{6,4},{1,7},{3,1},{5,3},{7,5},{8,14},{10,8},{12,... | collective-permute-start | bytes 3145736 | tf_op jit(solution)/shard_map/ppermute | solution.py:20
  8.0 23.4 %collective-permute-start.4 = (bf16[32,128,128]{2,1,0:T(8,128)(2,1)}, bf16[32,128,128]{2,1,0:T(8,128)(2,1)}, u32[]{:S(2)}, u32[]{:S(2)}) collective-permute-start(bf16[32,128,128]{2,1,0:T(8,128)(2,1)} %bitcast.54), channel_id=1, source_target_pairs={{0,16},{16,0},{1,17},{17,1},{2,18},{18,2},{3,19},{19,3},{4,20},{20... | collective-permute-start | bytes 3145736 | tf_op jit(solution)/shard_map/ppermute | solution.py:20
  12.4 4.0 %copy-start.14 = (s32[1,1,128,1]{2,3,1,0:T(1,128)S(1)}, s32[1,1,128,1]{2,3,1,0:T(1,128)}, u32[]{:S(2)}) copy-start(s32[1,1,128,1]{2,3,1,0:T(1,128)} %param.10) | copy-start | bytes 1540
  12.4 4.2 %copy-start.13 = (s32[1,1,128]{2,1,0:T(1,128)S(1)}, s32[1,1,128]{2,1,0:T(1,128)}, u32[]{:S(2)}) copy-start(s32[1,1,128]{2,1,0:T(1,128)} %param.11) | copy-start | bytes 1540
  12.4 4.4 %copy-start.12 = (s32[1,2,16]{2,1,0:T(2,128)S(1)}, s32[1,2,16]{2,1,0:T(2,128)}, u32[]{:S(2)}) copy-start(s32[1,2,16]{2,1,0:T(2,128)} %param.13) | copy-start | bytes 388
  12.4 4.5 %copy-start.11 = (s32[1,1,128,2]{2,3,1,0:T(2,128)S(1)}, s32[1,1,128,2]{2,3,1,0:T(2,128)}, u32[]{:S(2)}) copy-start(s32[1,1,128,2]{2,3,1,0:T(2,128)} %param.9) | copy-start | bytes 3076
  12.4 44.0 %all-to-all-start = ((bf16[64,128,128]{2,1,0:T(8,128)(2,1)}), bf16[64,128,128]{2,1,0:T(8,128)(2,1)S(1)}, u32[]{:S(2)}, u32[]{:S(2)}) async-start(bf16[64,128,128]{2,1,0:T(8,128)(2,1)} %pad_maximum_fusion), calls=%async_computation | async-start | bytes 4194304 | tf_op jit(solution)/shard_map/all_to_all | solution.py:216
  16.6 23.9 %copy-start.15 = (s32[128]{0:T(128)}, s32[128]{0:T(128)S(1)}, u32[]{:S(2)}) copy-start(s32[128]{0:T(128)S(1)} %convert_reduce_fusion.2.ranks) | copy-start | bytes 1540
  26.8 29.6 %copy-start.2 = (bf16[32,128,128]{2,1,0:T(8,128)(2,1)}, bf16[32,128,128]{2,1,0:T(8,128)(2,1)S(1)}, u32[]{:S(2)}) copy-start(bf16[32,128,128]{2,1,0:T(8,128)(2,1)S(1)} %collective-permute-done.refs_12_) | copy-start | bytes 3145732
  31.4 30.6 %collective-permute-start.5 = (bf16[32,128,128]{2,1,0:T(8,128)(2,1)}, bf16[32,128,128]{2,1,0:T(8,128)(2,1)}, u32[]{:S(2)}, u32[]{:S(2)}) collective-permute-start(bf16[32,128,128]{2,1,0:T(8,128)(2,1)} %collective-permute-done.4.refs_16_), channel_id=1, source_target_pairs={{0,32},{32,64},{64,96},{96,0},{1,33},{33,65},{65,97},{97,1},{2,34}... | collective-permute-start | bytes 3145736 | tf_op jit(solution)/shard_map/ppermute | solution.py:20
  31.4 53.8 %collective-permute-start.6 = (bf16[32,128,128]{2,1,0:T(8,128)(2,1)}, bf16[32,128,128]{2,1,0:T(8,128)(2,1)}, u32[]{:S(2)}, u32[]{:S(2)}) collective-permute-start(bf16[32,128,128]{2,1,0:T(8,128)(2,1)} %collective-permute-done.4.refs_16_), channel_id=1, source_target_pairs={{0,96},{32,0},{64,32},{96,64},{1,97},{33,1},{65,33},{97,65},{2,98}... | collective-permute-start | bytes 3145736 | tf_op jit(solution)/shard_map/ppermute | solution.py:20
  36.0 20.4 %collective-permute-start.7 = (bf16[16,128,128]{2,1,0:T(8,128)(2,1)}, bf16[16,128,128]{2,1,0:T(8,128)(2,1)}, u32[]{:S(2)}, u32[]{:S(2)}) collective-permute-start(bf16[16,128,128]{2,1,0:T(8,128)(2,1)} %slice.33), channel_id=1, source_target_pairs={{0,2},{2,4},{4,6},{6,0},{1,3},{3,5},{5,7},{7,1},{8,10},{10,12},{12... | collective-permute-start | bytes 1572872 | tf_op jit(solution)/shard_map/ppermute | solution.py:20
  37.9 18.6 %collective-permute-start.8 = (bf16[16,128,128]{2,1,0:T(8,128)(2,1)}, bf16[16,128,128]{2,1,0:T(8,128)(2,1)}, u32[]{:S(2)}, u32[]{:S(2)}) collective-permute-start(bf16[16,128,128]{2,1,0:T(8,128)(2,1)} %slice.34), channel_id=1, source_target_pairs={{0,6},{2,0},{4,2},{6,4},{1,7},{3,1},{5,3},{7,5},{8,14},{10,8},{12,... | collective-permute-start | bytes 1572872 | tf_op jit(solution)/shard_map/ppermute | solution.py:20
  56.4 2.9 %copy-start.3 = (bf16[32,128,128]{2,1,0:T(8,128)(2,1)S(1)}, bf16[32,128,128]{2,1,0:T(8,128)(2,1)}, u32[]{:S(2)}) copy-start(bf16[32,128,128]{2,1,0:T(8,128)(2,1)} %copy-done.2) | copy-start | bytes 3145732
  56.5 28.8 %copy-start.1 = (bf16[32,128,128]{2,1,0:T(8,128)(2,1)}, bf16[32,128,128]{2,1,0:T(8,128)(2,1)S(1)}, u32[]{:S(2)}) copy-start(bf16[32,128,128]{2,1,0:T(8,128)(2,1)S(1)} %constant_dynamic-slice_fusion.1.refs_3_) | copy-start | bytes 3145732
  56.5 28.7 %collective-permute-start.9 = (bf16[32,128,128]{2,1,0:T(8,128)(2,1)S(1)}, bf16[32,128,128]{2,1,0:T(8,128)(2,1)S(1)}, u32[]{:S(2)}, u32[]{:S(2)}) collective-permute-start(bf16[32,128,128]{2,1,0:T(8,128)(2,1)S(1)} %constant_dynamic-slice_fusion.1.refs_3_), channel_id=1, source_target_pairs={{0,2},{2,4},{4,6},{6,0},{1,3},{3,5},{5,7},{7,1},{8,10},{10,12},{12... | collective-permute-start | bytes 3145736 | tf_op jit(solution)/shard_map/ppermute | solution.py:20
  56.6 28.7 %collective-permute-start.10 = (bf16[32,128,128]{2,1,0:T(8,128)(2,1)S(1)}, bf16[32,128,128]{2,1,0:T(8,128)(2,1)S(1)}, u32[]{:S(2)}, u32[]{:S(2)}) collective-permute-start(bf16[32,128,128]{2,1,0:T(8,128)(2,1)S(1)} %constant_dynamic-slice_fusion.1.refs_3_), channel_id=1, source_target_pairs={{0,6},{2,0},{4,2},{6,4},{1,7},{3,1},{5,3},{7,5},{8,14},{10,8},{12,... | collective-permute-start | bytes 3145736 | tf_op jit(solution)/shard_map/ppermute | solution.py:20
  60.1 25.2 %collective-permute-start.11 = (bf16[16,128,128]{2,1,0:T(8,128)(2,1)}, bf16[16,128,128]{2,1,0:T(8,128)(2,1)}, u32[]{:S(2)}, u32[]{:S(2)}) collective-permute-start(bf16[16,128,128]{2,1,0:T(8,128)(2,1)} %slice.35), channel_id=1, source_target_pairs={{0,32},{32,64},{64,96},{96,0},{1,33},{33,65},{65,97},{97,1},{2,34}... | collective-permute-start | bytes 1572872 | tf_op jit(solution)/shard_map/ppermute | solution.py:20
  62.0 23.2 %collective-permute-start.12 = (bf16[16,128,128]{2,1,0:T(8,128)(2,1)}, bf16[16,128,128]{2,1,0:T(8,128)(2,1)}, u32[]{:S(2)}, u32[]{:S(2)}) collective-permute-start(bf16[16,128,128]{2,1,0:T(8,128)(2,1)} %slice.36), channel_id=1, source_target_pairs={{0,96},{32,0},{64,32},{96,64},{1,97},{33,1},{65,33},{97,65},{2,98}... | collective-permute-start | bytes 1572872 | tf_op jit(solution)/shard_map/ppermute | solution.py:20
  85.3 10.9 %copy-start.5 = (bf16[32,128,128]{2,1,0:T(8,128)(2,1)}, bf16[32,128,128]{2,1,0:T(8,128)(2,1)S(1)}, u32[]{:S(2)}) copy-start(bf16[32,128,128]{2,1,0:T(8,128)(2,1)S(1)} %collective-permute-done.9.refs_4_) | copy-start | bytes 3145732
  85.3 12.5 %copy-start.6 = (bf16[32,128,128]{2,1,0:T(8,128)(2,1)}, bf16[32,128,128]{2,1,0:T(8,128)(2,1)S(1)}, u32[]{:S(2)}) copy-start(bf16[32,128,128]{2,1,0:T(8,128)(2,1)S(1)} %collective-permute-done.10.refs_5_) | copy-start | bytes 3145732
  85.3 65.6 %all-to-all-start.2 = ((bf16[128,128,128]{2,1,0:T(8,128)(2,1)}), bf16[128,128,128]{2,1,0:T(8,128)(2,1)}, u32[]{:S(2)}, u32[]{:S(2)}) async-start(bf16[128,128,128]{2,1,0:T(8,128)(2,1)} %get-tuple-element.47), calls=%async_computation.2 | async-start | bytes 8388608 | tf_op jit(solution)/shard_map/all_to_all | solution.py:244
  92.2 58.1 %collective-permute-start.13 = (bf16[16,128,128]{2,1,0:T(8,128)(2,1)S(1)}, bf16[16,128,128]{2,1,0:T(8,128)(2,1)}, u32[]{:S(2)}, u32[]{:S(2)}) collective-permute-start(bf16[16,128,128]{2,1,0:T(8,128)(2,1)S(1)} %slice.39), channel_id=1, source_target_pairs={{0,32},{32,64},{64,96},{96,0},{1,33},{33,65},{65,97},{97,1},{2,34}... | collective-permute-start | bytes 1572872 | tf_op jit(solution)/shard_map/ppermute | solution.py:20
  94.8 55.6 %collective-permute-start.14 = (bf16[16,128,128]{2,1,0:T(8,128)(2,1)S(1)}, bf16[16,128,128]{2,1,0:T(8,128)(2,1)}, u32[]{:S(2)}, u32[]{:S(2)}) collective-permute-start(bf16[16,128,128]{2,1,0:T(8,128)(2,1)S(1)} %slice.40), channel_id=1, source_target_pairs={{0,96},{32,0},{64,32},{96,64},{1,97},{33,1},{65,33},{97,65},{2,98}... | collective-permute-start | bytes 1572872 | tf_op jit(solution)/shard_map/ppermute | solution.py:20
  96.2 54.7 %collective-permute-start.15 = (bf16[16,128,128]{2,1,0:T(8,128)(2,1)S(1)}, bf16[16,128,128]{2,1,0:T(8,128)(2,1)S(1)}, u32[]{:S(2)}, u32[]{:S(2)}) collective-permute-start(bf16[16,128,128]{2,1,0:T(8,128)(2,1)S(1)} %slice.41), channel_id=1, source_target_pairs={{0,2},{2,4},{4,6},{6,0},{1,3},{3,5},{5,7},{7,1},{8,10},{10,12},{12... | collective-permute-start | bytes 1572872 | tf_op jit(solution)/shard_map/ppermute | solution.py:20
  97.8 63.2 %copy-start.4 = (bf16[32,128,128]{2,1,0:T(8,128)(2,1)S(1)}, bf16[32,128,128]{2,1,0:T(8,128)(2,1)}, u32[]{:S(2)}) copy-start(bf16[32,128,128]{2,1,0:T(8,128)(2,1)} %copy-done.2) | copy-start | bytes 3145732
  97.8 68.1 %copy-start = (bf16[1,2,16,128,128]{4,3,2,1,0:T(8,128)(2,1)S(1)}, bf16[1,2,16,128,128]{4,3,2,1,0:T(8,128)(2,1)}, u32[]{:S(2)}) copy-start(bf16[1,2,16,128,128]{4,3,2,1,0:T(8,128)(2,1)} %param.12) | copy-start | bytes 3145732
  97.8 53.1 %collective-permute-start.16 = (bf16[16,128,128]{2,1,0:T(8,128)(2,1)S(1)}, bf16[16,128,128]{2,1,0:T(8,128)(2,1)S(1)}, u32[]{:S(2)}, u32[]{:S(2)}) collective-permute-start(bf16[16,128,128]{2,1,0:T(8,128)(2,1)S(1)} %slice.42), channel_id=1, source_target_pairs={{0,6},{2,0},{4,2},{6,4},{1,7},{3,1},{5,3},{7,5},{8,14},{10,8},{12,... | collective-permute-start | bytes 1572872 | tf_op jit(solution)/shard_map/ppermute | solution.py:20
  150.9 0.8 copy-start.9
  150.9 1.0 copy-start.10
  151.9 59.8 %all-to-all-start.3 = ((bf16[128,128,128]{2,1,0:T(8,128)(2,1)}), bf16[128,128,128]{2,1,0:T(8,128)(2,1)}, u32[]{:S(2)}, u32[]{:S(2)}) async-start(bf16[128,128,128]{2,1,0:T(8,128)(2,1)} %get-tuple-element.54), calls=%async_computation.3 | async-start | bytes 8388608 | tf_op jit(solution)/shard_map/all_to_all | solution.py:251
  161.0 4.9 %collective-permute-start.18 = (bf16[32,128,128]{2,1,0:T(8,128)(2,1)S(1)}, bf16[32,128,128]{2,1,0:T(8,128)(2,1)S(1)}, u32[]{:S(2)}, u32[]{:S(2)}) collective-permute-start(bf16[32,128,128]{2,1,0:T(8,128)(2,1)S(1)} %copy-done.4), channel_id=1, source_target_pairs={{0,8},{8,0},{1,9},{9,1},{2,10},{10,2},{3,11},{11,3},{4,12},{12,4},... | collective-permute-start | bytes 3145736 | tf_op jit(solution)/shard_map/ppermute | solution.py:20
  162.2 4.1 %collective-permute-start.19 = (bf16[32,128,128]{2,1,0:T(8,128)(2,1)}, bf16[32,128,128]{2,1,0:T(8,128)(2,1)}, u32[]{:S(2)}, u32[]{:S(2)}) collective-permute-start(bf16[32,128,128]{2,1,0:T(8,128)(2,1)} %collective-permute-done.1.refs_14_), channel_id=1, source_target_pairs={{0,8},{8,0},{1,9},{9,1},{2,10},{10,2},{3,11},{11,3},{4,12},{12,4},... | collective-permute-start | bytes 3145736 | tf_op jit(solution)/shard_map/ppermute | solution.py:20
  162.2 5.6 %collective-permute-start.20 = (bf16[32,128,128]{2,1,0:T(8,128)(2,1)}, bf16[32,128,128]{2,1,0:T(8,128)(2,1)}, u32[]{:S(2)}, u32[]{:S(2)}) collective-permute-start(bf16[32,128,128]{2,1,0:T(8,128)(2,1)} %collective-permute-done.4.refs_16_), channel_id=1, source_target_pairs={{0,8},{8,0},{1,9},{9,1},{2,10},{10,2},{3,11},{11,3},{4,12},{12,4},... | collective-permute-start | bytes 3145736 | tf_op jit(solution)/shard_map/ppermute | solution.py:20
  162.8 19.2 %collective-permute-start.21 = (bf16[32,128,128]{2,1,0:T(8,128)(2,1)}, bf16[32,128,128]{2,1,0:T(8,128)(2,1)}, u32[]{:S(2)}, u32[]{:S(2)}) collective-permute-start(bf16[32,128,128]{2,1,0:T(8,128)(2,1)} %collective-permute-done.5.refs_18_), channel_id=1, source_target_pairs={{0,8},{8,0},{1,9},{9,1},{2,10},{10,2},{3,11},{11,3},{4,12},{12,4},... | collective-permute-start | bytes 3145736 | tf_op jit(solution)/shard_map/ppermute | solution.py:20
  162.8 19.2 %collective-permute-start.22 = (bf16[32,128,128]{2,1,0:T(8,128)(2,1)}, bf16[32,128,128]{2,1,0:T(8,128)(2,1)}, u32[]{:S(2)}, u32[]{:S(2)}) collective-permute-start(bf16[32,128,128]{2,1,0:T(8,128)(2,1)} %collective-permute-done.6.refs_20_), channel_id=1, source_target_pairs={{0,8},{8,0},{1,9},{9,1},{2,10},{10,2},{3,11},{11,3},{4,12},{12,4},... | collective-permute-start | bytes 3145736 | tf_op jit(solution)/shard_map/ppermute | solution.py:20
  165.9 16.0 %copy-start.7 = (bf16[32,128,128]{2,1,0:T(8,128)(2,1)}, bf16[32,128,128]{2,1,0:T(8,128)(2,1)S(1)}, u32[]{:S(2)}) copy-start(bf16[32,128,128]{2,1,0:T(8,128)(2,1)S(1)} %collective-permute-done.18.refs_13_) | copy-start | bytes 3145732
  165.9 16.0 %collective-permute-start.17 = (bf16[32,128,128]{2,1,0:T(8,128)(2,1)S(1)}, bf16[32,128,128]{2,1,0:T(8,128)(2,1)S(1)}, u32[]{:S(2)}, u32[]{:S(2)}) collective-permute-start(bf16[32,128,128]{2,1,0:T(8,128)(2,1)S(1)} %bitcast.58), channel_id=1, source_target_pairs={{0,8},{8,0},{1,9},{9,1},{2,10},{10,2},{3,11},{11,3},{4,12},{12,4},... | collective-permute-start | bytes 3145736 | tf_op jit(solution)/shard_map/ppermute | solution.py:20
  166.3 6.7 %collective-permute-start.23 = (bf16[16,128,128]{2,1,0:T(8,128)(2,1)}, bf16[16,128,128]{2,1,0:T(8,128)(2,1)}, u32[]{:S(2)}, u32[]{:S(2)}) collective-permute-start(bf16[16,128,128]{2,1,0:T(8,128)(2,1)} %collective-permute-done.11.refs_22_), channel_id=1, source_target_pairs={{0,8},{8,0},{1,9},{9,1},{2,10},{10,2},{3,11},{11,3},{4,12},{12,4},... | collective-permute-start | bytes 1572872 | tf_op jit(solution)/shard_map/ppermute | solution.py:20
  167.8 6.0 %collective-permute-start.24 = (bf16[16,128,128]{2,1,0:T(8,128)(2,1)}, bf16[16,128,128]{2,1,0:T(8,128)(2,1)}, u32[]{:S(2)}, u32[]{:S(2)}) collective-permute-start(bf16[16,128,128]{2,1,0:T(8,128)(2,1)} %collective-permute-done.12.refs_24_), channel_id=1, source_target_pairs={{0,8},{8,0},{1,9},{9,1},{2,10},{10,2},{3,11},{11,3},{4,12},{12,4},... | collective-permute-start | bytes 1572872 | tf_op jit(solution)/shard_map/ppermute | solution.py:20
  173.0 8.9 %collective-permute-start.25 = (bf16[16,128,128]{2,1,0:T(8,128)(2,1)}, bf16[16,128,128]{2,1,0:T(8,128)(2,1)}, u32[]{:S(2)}, u32[]{:S(2)}) collective-permute-start(bf16[16,128,128]{2,1,0:T(8,128)(2,1)} %collective-permute-done.13.refs_26_), channel_id=1, source_target_pairs={{0,8},{8,0},{1,9},{9,1},{2,10},{10,2},{3,11},{11,3},{4,12},{12,4},... | collective-permute-start | bytes 1572872 | tf_op jit(solution)/shard_map/ppermute | solution.py:20
  173.8 8.2 %collective-permute-start.26 = (bf16[16,128,128]{2,1,0:T(8,128)(2,1)}, bf16[16,128,128]{2,1,0:T(8,128)(2,1)}, u32[]{:S(2)}, u32[]{:S(2)}) collective-permute-start(bf16[16,128,128]{2,1,0:T(8,128)(2,1)} %collective-permute-done.14.refs_28_), channel_id=1, source_target_pairs={{0,8},{8,0},{1,9},{9,1},{2,10},{10,2},{3,11},{11,3},{4,12},{12,4},... | collective-permute-start | bytes 1572872 | tf_op jit(solution)/shard_map/ppermute | solution.py:20
  181.9 1.0 copy-start.8
